TPU v7x, 512 devices: a whole 4x4x16 slice. The times are simulated.
512 devices in a mesh: sec: 4 (over z_hi, core), tile: 128 (over z_lo, x, y).
Axes of the slice: x: 4, y: 4, z: 16 (z_hi: 2, z_lo: 8; z = z_hi * 8 + z_lo), core: 2. Of those that a mesh axis runs over, the one named last changes fastest.
Arguments:
- state: float32 [4, 128, 65536], P('sec', None, 'tile'), may hold values from -6 to 6
- tendency: bfloat16 [4, 128, 65536], P('sec', None, 'tile'), may hold values from -4 to 4
- diffusion: bfloat16 [4, 128, 65536], P('sec', None, 'tile'), may hold values from 0.019897461 to 0.23925781
- mixing: float32 [4, 128, 128], P('sec')
- coupling: float32 [4, 128], P('sec'), may hold values from 0.05 to 0.4
- remap_index: int32 [4, 4, 65536], P('sec', None, 'tile'), may hold values from 0 to 1535, as said below
- remap_weight: float32 [4, 4, 65536], P('sec', None, 'tile'), may hold values from 0.1 to 0.4
- active_cols: int32 [4], replicated, may hold values from 256 to 512
- send_cols: int32 [2, 4, 128, 128, 4], P(None, 'sec', 'tile'), may hold values from 0 to 511
- occ_slot: int32 [2, 4, 8, 8192], P(None, 'sec', None, 'tile'), may hold values from 0 to 511
- occ_weight: float32 [2, 4, 8, 8192], P(None, 'sec', None, 'tile'), may hold values from 0.2 to 0.6
- occ_count: int32 [2, 4, 8192], P(None, 'sec', 'tile'), may hold values from 1 to 8
- refraction: float32 [4, 128, 128], P('sec'), may hold values from -0.5 to 0.5
- abel_matrix: float32 [128, 256], replicated
- observed: float32 [2, 8192, 256], P(None, ('sec', 'tile')), may hold values from -6 to 6
Outputs:
- final_state: float32 [4, 128, 65536], P('sec', None, 'tile')
- departures: float32 [2, 8192, 256], P(None, ('sec', 'tile'))
Inputs may be any that keep to these rules, and one draw needn't show every extreme that they name: `remap_index`: for an atmosphere section the value is a column within the tile of the ocean section; for the last section, value // 512 is the atmosphere section and value % 512 the column within the tile.
All inputs are finite; a program needn't handle non-finite values.
Results may differ from a plain program's by a relative error of at most 0.00035.
Values sent between devices are 32-bit elements; how exact they have to be, the bound alone decides.
No kernel may reach another device: no remote copies, remote signals or barrier semaphores. Data moves between devices by JAX's collectives and lax.ppermute only.
A program may use at most 64 MiB of HBM per device.

v0:
```python
import jax
import jax.numpy as jnp
from jax import lax
from jax.sharding import PartitionSpec as P

SUBS = 4
STEPS = 2


def extended(block, sides, width):
    for axis, dim in sides:
        count = lax.axis_size(axis)
        forward = [(i, i + 1) for i in range(count - 1)]
        forward.append((count - 1, 0))
        backward = [(target, source) for source, target in forward]
        low = lax.ppermute(
            lax.slice_in_dim(block, block.shape[dim] - width, None, axis=dim), axis, forward
        )
        high = lax.ppermute(lax.slice_in_dim(block, 0, width, axis=dim), axis, backward)
        block = jnp.concatenate([low, block, high], axis=dim)
    return block


def observe(arrived_rows, slots, weights, counts, refraction, abel_matrix, observed_step):
    highest = lax.Precision.HIGHEST
    gathered = jnp.take(arrived_rows, slots, axis=0)
    tangent_rank = jnp.arange(slots.shape[0], dtype=jnp.int32)[:, None]
    live_weight = jnp.where(tangent_rank < counts[None, :], weights, 0.0)
    profile = jnp.sum(live_weight[:, :, None] * gathered, axis=0)
    projected = jnp.dot(profile, refraction, precision=highest, preferred_element_type=jnp.float32)
    bending = jnp.dot(projected, abel_matrix, precision=highest, preferred_element_type=jnp.float32)
    owned = lax.psum_scatter(bending, "sec", scatter_dimension=0, tiled=True)
    return observed_step - owned


def shards(
    state,
    tendency,
    diffusion,
    mixing,
    coupling,
    remap_index,
    remap_weight,
    active_cols,
    send_cols,
    occ_slot,
    occ_weight,
    occ_count,
    refraction,
    abel_matrix,
    observed,
):
    highest = lax.Precision.HIGHEST
    section = lax.axis_index("sec")
    sections = lax.axis_size("sec")
    tile_count = lax.axis_size("tile")
    levels = state.shape[1]
    columns = state.shape[2]
    field = state[0]
    live_limit = lax.dynamic_index_in_dim(active_cols, section, 0, keepdims=False)
    live_mask = jnp.arange(columns, dtype=jnp.int32) < live_limit
    is_ocean = section == sections - 1
    position = jnp.where(is_ocean, remap_index[0], (sections - 1) * columns + remap_index[0])
    rates = diffusion[0]
    forcing = tendency[0].astype(jnp.float32)
    matrix = mixing[0]
    response = coupling[0][:, None]
    outgoing = []
    finished = []
    for period in range(STEPS):
        surface = field[levels - 1]
        surfaces = lax.all_gather(surface[None], "sec", axis=0, tiled=True)
        picked = jnp.take(surfaces.reshape(-1), position)
        boundary = jnp.sum(remap_weight[0] * picked, axis=0) - surface
        for substep in range(SUBS):
            padded = extended(field, (("tile", 1),), 1)
            spread = field + rates * (padded[:, :-2] + padded[:, 2:] - 2.0 * field)
            stepped = jnp.dot(matrix, spread, precision=highest, preferred_element_type=jnp.float32)
            stepped = stepped + response * boundary[None, :] + forcing
            field = jnp.where(live_mask[None, :], stepped, field)
        chosen = jnp.take(field, send_cols[period, 0, 0].reshape(-1), axis=1)
        parcel = chosen.T.reshape(tile_count, -1, levels)
        outgoing.append(parcel)
    arrived = lax.all_to_all(
        jnp.stack(outgoing, 1), "tile", split_axis=0, concat_axis=0, tiled=True
    )
    for period in range(STEPS):
        finished.append(
            observe(
                arrived[:, period].reshape(-1, levels),
                occ_slot[period, 0],
                occ_weight[period, 0],
                occ_count[period, 0],
                refraction[0],
                abel_matrix,
                observed[period],
            )
        )
    return (field[None], jnp.stack(finished))


def solution(mesh):
    return jax.shard_map(
        shards,
        mesh=mesh,
        in_specs=(
            P("sec", None, "tile"),
            P("sec", None, "tile"),
            P("sec", None, "tile"),
            P("sec", None, None),
            P("sec", None),
            P("sec", None, "tile"),
            P("sec", None, "tile"),
            P(),
            P(None, "sec", "tile", None, None),
            P(None, "sec", None, "tile"),
            P(None, "sec", None, "tile"),
            P(None, "sec", "tile"),
            P("sec", None, None),
            P(),
            P(None, ("sec", "tile"), None),
        ),
        out_specs=(P("sec", None, "tile"), P(None, ("sec", "tile"), None)),
        check_vma=False,
    )
```

profile of v0, /device:TPU:1, one launch (start us, length us, event | category | flops | bytes accessed | tf_op | source)
XLA Modules:
  0.0 368.1 jit_solution(8621983755176815925)
XLA Ops:
  7.2 1.1 copy.28
  8.3 4.0 %collective-permute-start = (f32[128,1]{0,1:T(1,128)S(1)}, f32[128,1]{0,1:T(1,128)S(1)}, u32[]{:S(2)}, u32[]{:S(2)}) collective-permute-start(f32[128,1]{0,1:T(1,128)S(1)} %get-tuple-element.27), channel_id=1, source_target_pairs={{0,1},{1,2},{2,3},{3,4},{4,5},{5,6},{6,7},{7,8},{8,9},{9,10},{10,1... | collective-permute-start | bytes 1544 | tf_op jit(solution)/shard_map/ppermute | solution.py:16
  12.4 16.2 %collective-permute-start.1 = (f32[128,1]{0,1:T(1,128)S(1)}, f32[128,1]{0,1:T(1,128)S(1)}, u32[]{:S(2)}, u32[]{:S(2)}) collective-permute-start(f32[128,1]{0,1:T(1,128)S(1)} %get-tuple-element.28), channel_id=1, source_target_pairs={{1,0},{2,1},{3,2},{4,3},{5,4},{6,5},{7,6},{8,7},{9,8},{10,9},{11,1... | collective-permute-start | bytes 1544 | tf_op jit(solution)/shard_map/ppermute | solution.py:19
  28.6 0.7 slice.163
  29.4 16.9 %all-gather = f32[4,1,512]{2,1,0:T(1,128)S(1)} all-gather(f32[1,1,512]{2,1,0:T(1,128)S(1)} %slice.163), channel_id=2, replica_groups=mesh['sec'=4,'tile'=128] {'sec'}, dimensions={0}, use_global_device_ids=true | all-gather | bytes 10240 | tf_op jit(solution)/shard_map/all_gather | solution.py:72
  46.3 11.8 %gather_fusion = f32[2048]{0:T(1024)S(1)} fusion(f32[2048]{0:T(1024)S(1)} %bitcast.214, s32[2048]{0:T(1024)S(1)} %broadcast_clamp_fusion), kind=kCustom, calls=%fused_computation.clone | custom fusion | bytes 24576 | tf_op jit(solution)/shard_map/jit(_take)/gather | solution.py:73
  58.4 0.5 copy-done.7
  58.9 0.6 copy-done.12
  59.6 0.6 dynamic_slice.4
  60.1 0.6 iota_compare_fusion.2
  60.9 0.8 copy-done.3
  62.1 0.6 copy-done.11
  62.7 0.4 fusion.23
  63.2 1.9 collective-permute-start.2
  65.1 14.2 %collective-permute-start.3 = (f32[128,1]{0,1:T(1,128)S(1)}, f32[128,1]{0,1:T(1,128)S(1)}, u32[]{:S(2)}, u32[]{:S(2)}) collective-permute-start(f32[128,1]{0,1:T(1,128)S(1)} %get-tuple-element.26), channel_id=1, source_target_pairs={{1,0},{2,1},{3,2},{4,3},{5,4},{6,5},{7,6},{8,7},{9,8},{10,9},{11,1... | collective-permute-start | bytes 1544 | tf_op jit(solution)/shard_map/ppermute | solution.py:19
  79.4 0.7 collective-permute-done.3
  80.0 0.4 fusion.20
  80.5 1.9 collective-permute-start.4
  82.4 14.4 %collective-permute-start.5 = (f32[128,1]{0,1:T(1,128)S(1)}, f32[128,1]{0,1:T(1,128)S(1)}, u32[]{:S(2)}, u32[]{:S(2)}) collective-permute-start(f32[128,1]{0,1:T(1,128)S(1)} %get-tuple-element.24), channel_id=1, source_target_pairs={{1,0},{2,1},{3,2},{4,3},{5,4},{6,5},{7,6},{8,7},{9,8},{10,9},{11,1... | collective-permute-start | bytes 1544 | tf_op jit(solution)/shard_map/ppermute | solution.py:19
  96.9 0.7 collective-permute-done.5
  97.5 0.4 fusion.17
  98.0 1.9 collective-permute-start.6
  99.9 14.4 %collective-permute-start.7 = (f32[128,1]{0,1:T(1,128)S(1)}, f32[128,1]{0,1:T(1,128)S(1)}, u32[]{:S(2)}, u32[]{:S(2)}) collective-permute-start(f32[128,1]{0,1:T(1,128)S(1)} %get-tuple-element.22), channel_id=1, source_target_pairs={{1,0},{2,1},{3,2},{4,3},{5,4},{6,5},{7,6},{8,7},{9,8},{10,9},{11,1... | collective-permute-start | bytes 1544 | tf_op jit(solution)/shard_map/ppermute | solution.py:19
  114.4 0.7 collective-permute-done.7
  115.0 0.4 fusion.14
  115.5 0.2 slice_reduce_fusion
  115.7 17.3 %all-gather.1 = f32[4,1,512]{2,1,0:T(1,128)S(1)} all-gather(f32[1,1,512]{2,1,0:T(1,128)S(1)} %bitcast.226), channel_id=1, replica_groups=mesh['sec'=4,'tile'=128] {'sec'}, dimensions={0}, use_global_device_ids=true | all-gather | bytes 10240 | tf_op jit(solution)/shard_map/all_gather | solution.py:72
  133.0 11.8 %gather_fusion.1 = f32[2048]{0:T(1024)S(1)} fusion(f32[2048]{0:T(1024)S(1)} %bitcast.213, s32[2048]{0:T(1024)S(1)} %broadcast_clamp_fusion), kind=kCustom, calls=%fused_computation.3.clone | custom fusion | bytes 24576 | tf_op jit(solution)/shard_map/jit(_take)/gather | solution.py:73
  145.0 1.9 collective-permute-start.8
  146.9 14.7 %collective-permute-start.9 = (f32[128,1]{0,1:T(1,128)S(1)}, f32[128,1]{0,1:T(1,128)S(1)}, u32[]{:S(2)}, u32[]{:S(2)}) collective-permute-start(f32[128,1]{0,1:T(1,128)S(1)} %get-tuple-element.20), channel_id=1, source_target_pairs={{1,0},{2,1},{3,2},{4,3},{5,4},{6,5},{7,6},{8,7},{9,8},{10,9},{11,1... | collective-permute-start | bytes 1544 | tf_op jit(solution)/shard_map/ppermute | solution.py:19
  161.6 0.2 subtract_reduce_fusion
  161.9 0.5 collective-permute-done.9
  162.3 0.4 fusion.11
  162.8 1.9 collective-permute-start.10
  164.7 14.4 %collective-permute-start.11 = (f32[128,1]{0,1:T(1,128)S(1)}, f32[128,1]{0,1:T(1,128)S(1)}, u32[]{:S(2)}, u32[]{:S(2)}) collective-permute-start(f32[128,1]{0,1:T(1,128)S(1)} %get-tuple-element.18), channel_id=1, source_target_pairs={{1,0},{2,1},{3,2},{4,3},{5,4},{6,5},{7,6},{8,7},{9,8},{10,9},{11,1... | collective-permute-start | bytes 1544 | tf_op jit(solution)/shard_map/ppermute | solution.py:19
  179.2 0.7 collective-permute-done.11
  179.8 0.4 fusion.8
  180.3 1.9 collective-permute-start.12
  182.2 14.4 %collective-permute-start.13 = (f32[128,1]{0,1:T(1,128)S(1)}, f32[128,1]{0,1:T(1,128)S(1)}, u32[]{:S(2)}, u32[]{:S(2)}) collective-permute-start(f32[128,1]{0,1:T(1,128)S(1)} %get-tuple-element.16), channel_id=1, source_target_pairs={{1,0},{2,1},{3,2},{4,3},{5,4},{6,5},{7,6},{8,7},{9,8},{10,9},{11,1... | collective-permute-start | bytes 1544 | tf_op jit(solution)/shard_map/ppermute | solution.py:19
  196.7 1.0 gather_fusion.2
  197.7 0.4 fusion.5
  198.2 1.9 collective-permute-start.14
  200.1 14.2 %collective-permute-start.15 = (f32[128,1]{0,1:T(1,128)S(1)}, f32[128,1]{0,1:T(1,128)S(1)}, u32[]{:S(2)}, u32[]{:S(2)}) collective-permute-start(f32[128,1]{0,1:T(1,128)S(1)} %get-tuple-element.14), channel_id=1, source_target_pairs={{1,0},{2,1},{3,2},{4,3},{5,4},{6,5},{7,6},{8,7},{9,8},{10,9},{11,1... | collective-permute-start | bytes 1544 | tf_op jit(solution)/shard_map/ppermute | solution.py:19
  214.5 0.5 collective-permute-done.15
  215.0 0.4 fusion.2
  215.4 1.0 gather_fusion.3
  216.6 0.9 pad_maximum_fusion
  217.6 16.1 %all-to-all-start = ((f32[128,2,4,128]{3,2,1,0:T(4,128)}), f32[128,2,4,128]{3,2,1,0:T(4,128)S(1)}, u32[]{:S(2)}, u32[]{:S(2)}) async-start(f32[128,2,4,128]{3,2,1,0:T(4,128)} %pad_maximum_fusion), calls=%async_computation | async-start | bytes 1048576 | tf_op jit(solution)/shard_map/all_to_all | solution.py:84
  234.0 0.7 copy-done.10
  234.6 0.7 copy-done.8
  235.3 27.4 %all-to-all-done = f32[128,2,4,128]{3,2,1,0:T(4,128)S(1)} async-done(((f32[128,2,4,128]{3,2,1,0:T(4,128)}), f32[128,2,4,128]{3,2,1,0:T(4,128)S(1)}, u32[]{:S(2)}, u32[]{:S(2)}) %all-to-all-start) | async-done | bytes 524320 | tf_op jit(solution)/shard_map/all_to_all | solution.py:84
  262.8 1.0 gather_fusion.4
  263.8 1.0 gather_fusion.5
  264.9 0.3 fusion.80
  265.2 0.5 copy-done.1
  265.7 0.2 fusion.108
  265.9 0.8 fusion.149
  266.8 0.2 fusion.106
  267.0 0.8 fusion.150
  267.9 0.8 copy.36
  268.7 46.4 %reduce-scatter.3.cloned.1.call-done = f32[16,256]{1,0:T(8,128)} async-done(((f32[64,256]{1,0:T(8,128)}), f32[16,256]{1,0:T(8,128)}) %reduce-scatter.3.cloned.1.call-update) | async-done | bytes 16400 | tf_op jit(solution)/shard_map/reduce_scatter | solution.py:32
  315.1 44.8 %reduce-scatter.5.cloned.1.call-done = f32[16,256]{1,0:T(8,128)} async-done(((f32[64,256]{1,0:T(8,128)}), f32[16,256]{1,0:T(8,128)}) %reduce-scatter.5.cloned.1.call-update) | async-done | bytes 16400 | tf_op jit(solution)/shard_map/reduce_scatter | solution.py:32
  359.9 0.7 fusion.119
  360.6 0.6 pad_maximum_fusion.25
  (76 shorter events, 1.8 us)
Async XLA Ops:
  7.2 258.8 %copy-start = (f32[128,256]{1,0:T(8,128)S(1)}, f32[128,256]{1,0:T(8,128)}, u32[]{:S(2)}) copy-start(f32[128,256]{1,0:T(8,128)} %param.34) | copy-start | bytes 393220
  8.3 21.0 %copy-start.4 = (s32[1,4,512]{2,1,0:T(4,128)S(1)}, s32[1,4,512]{2,1,0:T(4,128)}, u32[]{:S(2)}) copy-start(s32[1,4,512]{2,1,0:T(4,128)} %param.26) | copy-start | bytes 24580
  8.3 53.8 %collective-permute-start = (f32[128,1]{0,1:T(1,128)S(1)}, f32[128,1]{0,1:T(1,128)S(1)}, u32[]{:S(2)}, u32[]{:S(2)}) collective-permute-start(f32[128,1]{0,1:T(1,128)S(1)} %get-tuple-element.27), channel_id=1, source_target_pairs={{0,1},{1,2},{2,3},{3,4},{4,5},{5,6},{6,7},{7,8},{8,9},{9,10},{10,1... | collective-permute-start | bytes 1544 | tf_op jit(solution)/shard_map/ppermute | solution.py:16
  12.4 49.7 %collective-permute-start.1 = (f32[128,1]{0,1:T(1,128)S(1)}, f32[128,1]{0,1:T(1,128)S(1)}, u32[]{:S(2)}, u32[]{:S(2)}) collective-permute-start(f32[128,1]{0,1:T(1,128)S(1)} %get-tuple-element.28), channel_id=1, source_target_pairs={{1,0},{2,1},{3,2},{4,3},{5,4},{6,5},{7,6},{8,7},{9,8},{10,9},{11,1... | collective-permute-start | bytes 1544 | tf_op jit(solution)/shard_map/ppermute | solution.py:19
  46.3 11.8 %copy-start.9 = (s32[2,1,1,128,4]{3,4,2,1,0:T(4,128)S(1)}, s32[2,1,1,128,4]{3,4,2,1,0:T(4,128)}, u32[]{:S(2)}) copy-start(s32[2,1,1,128,4]{3,4,2,1,0:T(4,128)} %param.29) | copy-start | bytes 12292
  58.1 2.7 copy-start.2
  58.1 0.7 copy-start.7
  58.9 0.7 copy-start.12
  60.8 0.9 copy-start.3
  61.8 0.8 copy-start.11
  62.1 0.7 copy-start.13
  63.2 16.1 %collective-permute-start.2 = (f32[128,1]{0,1:T(1,128)S(1)}, f32[128,1]{0,1:T(1,128)S(1)}, u32[]{:S(2)}, u32[]{:S(2)}) collective-permute-start(f32[128,1]{0,1:T(1,128)S(1)} %get-tuple-element.25), channel_id=1, source_target_pairs={{0,1},{1,2},{2,3},{3,4},{4,5},{5,6},{6,7},{7,8},{8,9},{9,10},{10,1... | collective-permute-start | bytes 1544 | tf_op jit(solution)/shard_map/ppermute | solution.py:16
  65.1 14.9 %collective-permute-start.3 = (f32[128,1]{0,1:T(1,128)S(1)}, f32[128,1]{0,1:T(1,128)S(1)}, u32[]{:S(2)}, u32[]{:S(2)}) collective-permute-start(f32[128,1]{0,1:T(1,128)S(1)} %get-tuple-element.26), channel_id=1, source_target_pairs={{1,0},{2,1},{3,2},{4,3},{5,4},{6,5},{7,6},{8,7},{9,8},{10,9},{11,1... | collective-permute-start | bytes 1544 | tf_op jit(solution)/shard_map/ppermute | solution.py:19
  80.5 16.4 %collective-permute-start.4 = (f32[128,1]{0,1:T(1,128)S(1)}, f32[128,1]{0,1:T(1,128)S(1)}, u32[]{:S(2)}, u32[]{:S(2)}) collective-permute-start(f32[128,1]{0,1:T(1,128)S(1)} %get-tuple-element.23), channel_id=1, source_target_pairs={{0,1},{1,2},{2,3},{3,4},{4,5},{5,6},{6,7},{7,8},{8,9},{9,10},{10,1... | collective-permute-start | bytes 1544 | tf_op jit(solution)/shard_map/ppermute | solution.py:16
  82.4 15.1 %collective-permute-start.5 = (f32[128,1]{0,1:T(1,128)S(1)}, f32[128,1]{0,1:T(1,128)S(1)}, u32[]{:S(2)}, u32[]{:S(2)}) collective-permute-start(f32[128,1]{0,1:T(1,128)S(1)} %get-tuple-element.24), channel_id=1, source_target_pairs={{1,0},{2,1},{3,2},{4,3},{5,4},{6,5},{7,6},{8,7},{9,8},{10,9},{11,1... | collective-permute-start | bytes 1544 | tf_op jit(solution)/shard_map/ppermute | solution.py:19
  98.0 16.4 %collective-permute-start.6 = (f32[128,1]{0,1:T(1,128)S(1)}, f32[128,1]{0,1:T(1,128)S(1)}, u32[]{:S(2)}, u32[]{:S(2)}) collective-permute-start(f32[128,1]{0,1:T(1,128)S(1)} %get-tuple-element.21), channel_id=1, source_target_pairs={{0,1},{1,2},{2,3},{3,4},{4,5},{5,6},{6,7},{7,8},{8,9},{9,10},{10,1... | collective-permute-start | bytes 1544 | tf_op jit(solution)/shard_map/ppermute | solution.py:16
  99.9 15.1 %collective-permute-start.7 = (f32[128,1]{0,1:T(1,128)S(1)}, f32[128,1]{0,1:T(1,128)S(1)}, u32[]{:S(2)}, u32[]{:S(2)}) collective-permute-start(f32[128,1]{0,1:T(1,128)S(1)} %get-tuple-element.22), channel_id=1, source_target_pairs={{1,0},{2,1},{3,2},{4,3},{5,4},{6,5},{7,6},{8,7},{9,8},{10,9},{11,1... | collective-permute-start | bytes 1544 | tf_op jit(solution)/shard_map/ppermute | solution.py:19
  145.0 16.9 %collective-permute-start.8 = (f32[128,1]{0,1:T(1,128)S(1)}, f32[128,1]{0,1:T(1,128)S(1)}, u32[]{:S(2)}, u32[]{:S(2)}) collective-permute-start(f32[128,1]{0,1:T(1,128)S(1)} %get-tuple-element.19), channel_id=1, source_target_pairs={{0,1},{1,2},{2,3},{3,4},{4,5},{5,6},{6,7},{7,8},{8,9},{9,10},{10,1... | collective-permute-start | bytes 1544 | tf_op jit(solution)/shard_map/ppermute | solution.py:16
  146.9 15.4 %collective-permute-start.9 = (f32[128,1]{0,1:T(1,128)S(1)}, f32[128,1]{0,1:T(1,128)S(1)}, u32[]{:S(2)}, u32[]{:S(2)}) collective-permute-start(f32[128,1]{0,1:T(1,128)S(1)} %get-tuple-element.20), channel_id=1, source_target_pairs={{1,0},{2,1},{3,2},{4,3},{5,4},{6,5},{7,6},{8,7},{9,8},{10,9},{11,1... | collective-permute-start | bytes 1544 | tf_op jit(solution)/shard_map/ppermute | solution.py:19
  162.8 16.4 %collective-permute-start.10 = (f32[128,1]{0,1:T(1,128)S(1)}, f32[128,1]{0,1:T(1,128)S(1)}, u32[]{:S(2)}, u32[]{:S(2)}) collective-permute-start(f32[128,1]{0,1:T(1,128)S(1)} %get-tuple-element.17), channel_id=1, source_target_pairs={{0,1},{1,2},{2,3},{3,4},{4,5},{5,6},{6,7},{7,8},{8,9},{9,10},{10,1... | collective-permute-start | bytes 1544 | tf_op jit(solution)/shard_map/ppermute | solution.py:16
  164.7 15.1 %collective-permute-start.11 = (f32[128,1]{0,1:T(1,128)S(1)}, f32[128,1]{0,1:T(1,128)S(1)}, u32[]{:S(2)}, u32[]{:S(2)}) collective-permute-start(f32[128,1]{0,1:T(1,128)S(1)} %get-tuple-element.18), channel_id=1, source_target_pairs={{1,0},{2,1},{3,2},{4,3},{5,4},{6,5},{7,6},{8,7},{9,8},{10,9},{11,1... | collective-permute-start | bytes 1544 | tf_op jit(solution)/shard_map/ppermute | solution.py:19
  180.3 17.4 %collective-permute-start.12 = (f32[128,1]{0,1:T(1,128)S(1)}, f32[128,1]{0,1:T(1,128)S(1)}, u32[]{:S(2)}, u32[]{:S(2)}) collective-permute-start(f32[128,1]{0,1:T(1,128)S(1)} %get-tuple-element.15), channel_id=1, source_target_pairs={{0,1},{1,2},{2,3},{3,4},{4,5},{5,6},{6,7},{7,8},{8,9},{9,10},{10,1... | collective-permute-start | bytes 1544 | tf_op jit(solution)/shard_map/ppermute | solution.py:16
  182.2 15.5 %collective-permute-start.13 = (f32[128,1]{0,1:T(1,128)S(1)}, f32[128,1]{0,1:T(1,128)S(1)}, u32[]{:S(2)}, u32[]{:S(2)}) collective-permute-start(f32[128,1]{0,1:T(1,128)S(1)} %get-tuple-element.16), channel_id=1, source_target_pairs={{1,0},{2,1},{3,2},{4,3},{5,4},{6,5},{7,6},{8,7},{9,8},{10,9},{11,1... | collective-permute-start | bytes 1544 | tf_op jit(solution)/shard_map/ppermute | solution.py:19
  198.2 16.3 %collective-permute-start.14 = (f32[128,1]{0,1:T(1,128)S(1)}, f32[128,1]{0,1:T(1,128)S(1)}, u32[]{:S(2)}, u32[]{:S(2)}) collective-permute-start(f32[128,1]{0,1:T(1,128)S(1)} %get-tuple-element.13), channel_id=1, source_target_pairs={{0,1},{1,2},{2,3},{3,4},{4,5},{5,6},{6,7},{7,8},{8,9},{9,10},{10,1... | collective-permute-start | bytes 1544 | tf_op jit(solution)/shard_map/ppermute | solution.py:16
  200.1 14.9 %collective-permute-start.15 = (f32[128,1]{0,1:T(1,128)S(1)}, f32[128,1]{0,1:T(1,128)S(1)}, u32[]{:S(2)}, u32[]{:S(2)}) collective-permute-start(f32[128,1]{0,1:T(1,128)S(1)} %get-tuple-element.14), channel_id=1, source_target_pairs={{1,0},{2,1},{3,2},{4,3},{5,4},{6,5},{7,6},{8,7},{9,8},{10,9},{11,1... | collective-permute-start | bytes 1544 | tf_op jit(solution)/shard_map/ppermute | solution.py:19
  217.6 16.2 %copy-start.6 = (s32[2,1,8,64]{3,2,1,0:T(8,128)S(1)}, s32[2,1,8,64]{3,2,1,0:T(8,128)}, u32[]{:S(2)}) copy-start(s32[2,1,8,64]{3,2,1,0:T(8,128)} %param.30) | copy-start | bytes 12292
  217.6 45.1 %all-to-all-start = ((f32[128,2,4,128]{3,2,1,0:T(4,128)}), f32[128,2,4,128]{3,2,1,0:T(4,128)S(1)}, u32[]{:S(2)}, u32[]{:S(2)}) async-start(f32[128,2,4,128]{3,2,1,0:T(4,128)} %pad_maximum_fusion), calls=%async_computation | async-start | bytes 1048576 | tf_op jit(solution)/shard_map/all_to_all | solution.py:84
  233.7 81.4 %reduce-scatter.3.cloned.1.call-start = ((), (), s32[]{:S(2)}) async-start(), calls=%async_computation.3 | async-start | bytes 81920 | tf_op jit(solution)/shard_map/reduce_scatter | solution.py:32
  233.9 0.7 copy-start.10
  234.6 0.7 copy-start.8
  264.9 0.8 copy-start.1
  266.8 93.1 %reduce-scatter.5.cloned.1.call-start = ((), (), s32[]{:S(2)}) async-start(), calls=%async_computation.4 | async-start | bytes 81920 | tf_op jit(solution)/shard_map/reduce_scatter | solution.py:32
  267.9 92.0 %copy-start.5 = (f32[2,16,256]{2,1,0:T(8,128)S(1)}, f32[2,16,256]{2,1,0:T(8,128)}, u32[]{:S(2)}) copy-start(f32[2,16,256]{2,1,0:T(8,128)} %param.35) | copy-start | bytes 98308
Sparse Core Ops, SparseCore 0:
  266.9 48.1 reduce-scatter.2
  318.3 41.4 reduce-scatter.4
where the time goes:
time: 369 us; the launch traced here: 368 us
  starting transfers between devices  151 us (41%)
  waiting for transfers between devices  122 us (33%)
  local copies, waits for them, and re-layouts  36.7 us (10%)
  blocking collectives  34.3 us (9%)
  between operations  14.7 us (4%)
  matrix products  5.55 us (2%)
  other arithmetic  3.92 us (1%)
    ppermute x8, starting transfers between devices, extended(): lax.ppermute(lax.slice_in_dim(block, 0, width, axis=dim), axis, backward)  117 us
    reduce_scatter x2, waiting for transfers between devices, observe(): owned = lax.psum_scatter(bending, 'sec', scatter_dimension=0, tiled=True)  91.1 us
    all_gather x2, blocking collectives, shards(): surfaces = lax.all_gather(surface[None], 'sec', axis=0, tiled=True)  34.3 us
    all_to_all x1, waiting for transfers between devices, shards(): lax.all_to_all(jnp.stack(outgoing, 1), 'tile', split_axis=0, concat_axis=...  27.4 us
    gather x4, local copies, waits for them, and re-layouts, shards(): picked = jnp.take(surfaces.reshape(-1), position)  23.6 us
    ppermute x8, starting transfers between devices, extended(): lax.ppermute(lax.slice_in_dim(block, block.shape[dim] - width, None, axis...  17.5 us
    all_to_all x1, starting transfers between devices, shards(): lax.all_to_all(jnp.stack(outgoing, 1), 'tile', split_axis=0, concat_axis=...  16.1 us
  transfers between devices with their start and end apart: 19, of which 9 were waited for; matrix products, arithmetic and copies ran while one was open for 5% of the time, Pallas kernels for 0%

commit v1 on v0

v1 whole, which is shorter than its diff:
```python
import jax
import jax.numpy as jnp
from jax import lax
from jax.experimental import pallas as pl
from jax.experimental.pallas import tpu as pltpu
from jax.sharding import PartitionSpec as P

SUBS = 4
STEPS = 2
HALO = 8
LANES = 128
AXES = ("sec", "tile")
f32 = jnp.float32
bf16 = jnp.bfloat16


def call(body, outs, *args, scratch=()):
    in_specs = [
        pl.BlockSpec(memory_space=pltpu.SMEM if a.ndim == 1 else pltpu.VMEM) for a in args
    ]
    single = not isinstance(outs, (tuple, list))
    specs = pl.BlockSpec(memory_space=pltpu.VMEM)
    return pl.pallas_call(
        body,
        out_shape=outs if single else tuple(outs),
        in_specs=in_specs,
        out_specs=specs if single else tuple(specs for _ in outs),
        scratch_shapes=list(scratch),
        compiler_params=pltpu.CompilerParams(vmem_limit_bytes=40 * 2**20),
    )(*args)


def halves(x):
    high = x.astype(bf16)
    return high, (x - high.astype(f32)).astype(bf16)


def left_operand(x):
    high, low = halves(x)
    return jnp.concatenate([high, high, low], axis=1)


def right_operand(x):
    high, low = halves(x)
    return jnp.concatenate([high, low, high], axis=0)


def matmul(left, right):
    return jnp.dot(left, right, preferred_element_type=f32)


def pick(table, position):
    lane = position & (LANES - 1)
    row = position >> 7
    out = jnp.zeros(position.shape, f32)
    for r, values in enumerate(table):
        source = jnp.broadcast_to(values, position.shape)
        found = jnp.take_along_axis(source, lane, axis=1, mode="promise_in_bounds")
        out = jnp.where(row == r, found, out)
    return out


def lane_ids(shape):
    return lax.broadcasted_iota(jnp.int32, shape, len(shape) - 1)


def pack_edges(first, last):
    lane = lane_ids(first.shape)
    return jnp.where(lane < HALO, first, pltpu.roll(last, 2 * HALO, 1))


def prepare(scalars, state, tendency, diffusion, index, weight, out):
    columns = state.shape[1]
    levels = state.shape[0]
    tail = columns - LANES
    offset = scalars[5]
    block = jnp.zeros((levels, LANES), f32)
    lane = lane_ids(block.shape)
    for i, ref in enumerate((state, diffusion, tendency)):
        edges = pack_edges(ref[:, :LANES].astype(f32), ref[:, tail:].astype(f32))
        if i:
            edges = pltpu.roll(edges, 2 * HALO * i, 1)
        inside = (lane >= 2 * HALO * i) & (lane < 2 * HALO * (i + 1))
        block = jnp.where(inside, edges, block)
    out[0:48, :] = block.T[0:48, :]
    for j in range(columns // LANES):
        out[48 + j : 49 + j, :] = state[levels - 1 : levels, j * LANES : (j + 1) * LANES]
    out[52:56, :] = pack_edges(weight[:, :LANES], weight[:, tail:])
    position = (index[...] + offset).astype(f32)
    out[56:60, :] = pack_edges(position[:, :LANES], position[:, tail:])
    out[60:64, :] = jnp.zeros((4, LANES), f32)


def edge_boundary(table, shared, surface_first, surface_last, source):
    position = shared[source, 56:60, :].astype(jnp.int32)
    picked = pick(table, position)
    partner = jnp.sum(shared[source, 52:56, :] * picked, axis=0, keepdims=True)
    return partner - pack_edges(surface_first, surface_last)


def own_boundary(table, index, weight, surface, offset, out):
    for j in range(out.shape[1] // LANES):
        cut = slice(j * LANES, (j + 1) * LANES)
        picked = pick(table, index[:, cut] + offset)
        partner = jnp.sum(weight[:, cut] * picked, axis=0, keepdims=True)
        out[:, cut] = partner - surface(j)


def couple_first(scalars, shared, index, weight, boundary, forward, backward):
    section, offset = scalars[0], scalars[5]
    table = [shared[s, r : r + 1, :] for s in range(shared.shape[0]) for r in range(48, 52)]
    own_boundary(
        table, index, weight, lambda j: shared[section, 48 + j : 49 + j, :], offset, boundary
    )
    for out, source, start in ((forward, scalars[2], HALO), (backward, scalars[3], 0)):
        for i in range(3):
            row = 2 * HALO * i + start
            out[HALO * i : HALO * (i + 1), :] = shared[source, row : row + HALO, :]
        edge = edge_boundary(
            table, shared, shared[source, 48:49, :], shared[source, 51:52, :], source
        )
        out[24:32, :] = jnp.broadcast_to(edge, (8, LANES))


def couple_second(scalars, surfaces, shared, index, weight, boundary, forward, backward):
    section, offset = scalars[0], scalars[5]
    table = [surfaces[s, r : r + 1, :] for s in range(surfaces.shape[0]) for r in range(4)]
    own_boundary(
        table, index, weight, lambda j: surfaces[section, j : j + 1, :], offset, boundary
    )
    for out, source in ((forward, scalars[2]), (backward, scalars[3])):
        edge = edge_boundary(
            table, shared, surfaces[source, 0:1, :], surfaces[source, 3:4, :], source
        )
        out[...] = jnp.broadcast_to(edge, out.shape)


def edge_row(left, right):
    lane = lane_ids(left.shape)
    value = jnp.where(lane < HALO, right, 0.0)
    return jnp.where(lane >= LANES - HALO, pltpu.roll(left, LANES - 2 * HALO, 1), value)


def edge_block(left, right):
    gap = jnp.zeros((LANES - 2 * HALO, left.shape[1]), f32)
    return jnp.concatenate([right, gap, left], axis=0).T


def advance(field, rates, constant, mixing, live_limit):
    width = field.shape[1]
    lane = lane_ids((1, width))
    columns = width - LANES
    column = jnp.where(lane < columns, lane, lane - columns)
    column = jnp.where(lane < width - HALO, column, lane - LANES)
    live = column < live_limit
    left = left_operand(mixing)
    for _ in range(SUBS):
        near = pltpu.roll(field, 1, 1) + pltpu.roll(field, width - 1, 1)
        spread = field + rates * (near - 2.0 * field)
        stepped = matmul(left, right_operand(spread)) + constant
        field = jnp.where(live, stepped, field)
    return field


def forcing(coupling, boundary, edge, tendency):
    response = jnp.broadcast_to(coupling[...], (LANES, coupling.shape[1])).T
    row = jnp.concatenate([boundary[...], edge], axis=1)
    width = row.shape[1]
    parts = [
        response * row[:, j * LANES : (j + 1) * LANES] for j in range(width // LANES)
    ]
    return jnp.concatenate(parts, axis=1) + tendency


def chosen(field, listed):
    columns = field.shape[1] - LANES
    high, low = halves(field[:, :columns])
    stack = jnp.concatenate([high, low], axis=0)
    out = []
    for m in range(listed.shape[0]):
        row = listed[m : m + 1, :]
        column = lax.broadcasted_iota(jnp.int32, (columns, row.shape[1]), 0)
        hit = jnp.where(column == row, 1.0, 0.0).astype(bf16)
        both = matmul(stack, hit)
        levels = field.shape[0]
        out.append((both[:levels] + both[levels:]).T)
    return out


def step_first(
    scalars, state, tendency, diffusion, mixing, coupling, boundary, low, high, listed,
    window, rates_out, forcing_out, surface, parcel,
):
    rates = jnp.concatenate(
        [diffusion[...].astype(f32), edge_block(low[8:16, :], high[8:16, :])], axis=1
    )
    tend = jnp.concatenate(
        [tendency[...].astype(f32), edge_block(low[16:24, :], high[16:24, :])], axis=1
    )
    field = jnp.concatenate([state[...], edge_block(low[0:8, :], high[0:8, :])], axis=1)
    constant = forcing(coupling, boundary, edge_row(low[24:25, :], high[24:25, :]), tend)
    rates_out[...] = rates
    forcing_out[...] = tend
    field = advance(field, rates, constant, mixing[...], scalars[4])
    window[...] = field
    levels = field.shape[0]
    for j in range(4):
        surface[j : j + 1, :] = field[levels - 1 : levels, j * LANES : (j + 1) * LANES]
    for m, rows in enumerate(chosen(field, listed[0])):
        parcel[m] = rows


def step_second(
    scalars, window, rates, tend, mixing, coupling, boundary, low, high, listed, earlier,
    final, parcels,
):
    edge = edge_row(low[0:1, :], high[0:1, :])
    constant = forcing(coupling, boundary, edge, tend[...])
    field = advance(window[...], rates[...], constant, mixing[...], scalars[4])
    final[...] = field[:, : final.shape[1]]
    slots = earlier.shape[0]
    tiles = earlier.shape[1]
    for m in range(slots):
        parcels[pl.ds(m, tiles, stride=2 * slots), :] = earlier[m]
    for m, rows in enumerate(chosen(field, listed[1])):
        parcels[pl.ds(slots + m, tiles, stride=2 * slots), :] = rows


def weigh(slots, weights, counts, out):
    steps, ranks, occultations = slots.shape
    width = out.shape[2]
    tiles = width // 4
    for p in range(steps):
        rank = lax.broadcasted_iota(jnp.int32, (ranks, occultations), 0)
        live = jnp.where(rank < counts[p : p + 1, :], weights[p], 0.0).T
        key = ((slots[p] & 3) * tiles + (slots[p] >> 2)).T
        place = lane_ids((occultations, width))
        total = jnp.zeros((occultations, width), f32)
        for k in range(ranks):
            total = total + jnp.where(key[:, k : k + 1] == place, live[:, k : k + 1], 0.0)
        out[p] = total


def project(arrived, spread, refraction, out):
    steps, occultations, width = spread.shape
    tiles = width // 4
    owners = out.shape[0]
    rows = occultations // owners
    profiles = []
    for p in range(steps):
        values = jnp.concatenate(
            [arrived[pl.ds(4 * p + m, tiles, stride=4 * steps), :] for m in range(4)], axis=0
        )
        profiles.append(matmul(left_operand(spread[p]), right_operand(values)))
    profile = jnp.concatenate(profiles, axis=0)
    projected = matmul(left_operand(profile), right_operand(refraction[...]))
    for p in range(steps):
        for q in range(owners):
            start = p * occultations + q * rows
            out[q, p * rows : (p + 1) * rows, :] = projected[start : start + rows, :]


def depart(received, abel, observed, out):
    total = received[0]
    for s in range(1, received.shape[0]):
        total = total + received[s]
    bending = matmul(left_operand(total), right_operand(abel[...]))
    steps, rows, _ = observed.shape
    for p in range(steps):
        out[p] = observed[p] - bending[p * rows : (p + 1) * rows, :]


def shards(
    state,
    tendency,
    diffusion,
    mixing,
    coupling,
    remap_index,
    remap_weight,
    active_cols,
    send_cols,
    occ_slot,
    occ_weight,
    occ_count,
    refraction,
    abel_matrix,
    observed,
):
    section = lax.axis_index("sec")
    tile = lax.axis_index("tile")
    sections = lax.axis_size("sec")
    tiles = lax.axis_size("tile")
    levels, columns = state.shape[1:]
    half = sections // 2
    other = (section + half) % sections
    scalars = jnp.stack(
        [
            section,
            tile,
            jnp.where(tile == tiles - 1, other, section),
            jnp.where(tile == 0, other, section),
            lax.dynamic_index_in_dim(active_cols, section, 0, keepdims=False),
            jnp.where(section == sections - 1, 0, (sections - 1) * columns),
        ]
    ).astype(jnp.int32)
    forward = []
    for s in range(sections):
        for t in range(tiles):
            seam = t == tiles - 1
            target = ((s + half) % sections if seam else s) * tiles + (t + 1) % tiles
            forward.append((s * tiles + t, target))
    backward = [(target, source) for source, target in forward]
    listed = jnp.transpose(send_cols[:, 0, 0], (0, 2, 1))
    index, weight = remap_index[0], remap_weight[0]
    shape = jax.ShapeDtypeStruct
    width = columns + LANES

    edges = call(
        prepare, shape((64, LANES), f32), scalars, state[0], tendency[0], diffusion[0], index, weight
    )
    shared = lax.all_gather(edges, "sec", axis=0, tiled=False)
    boundary, up, down = call(
        couple_first,
        (shape((1, columns), f32), shape((32, LANES), f32), shape((32, LANES), f32)),
        scalars, shared, index, weight,
    )
    low = lax.ppermute(up, AXES, forward)
    high = lax.ppermute(down, AXES, backward)
    spread = call(
        weigh,
        shape((STEPS, occ_slot.shape[3], 4 * tiles), f32),
        occ_slot[:, 0], occ_weight[:, 0], occ_count[:, 0],
    )
    window, rates, tend, surface, parcel = call(
        step_first,
        (
            shape((levels, width), f32),
            shape((levels, width), f32),
            shape((levels, width), f32),
            shape((4, LANES), f32),
            shape((4, tiles, levels), f32),
        ),
        scalars, state[0], tendency[0], diffusion[0], mixing[0], coupling, boundary, low, high, listed,
    )
    surfaces = lax.all_gather(surface, "sec", axis=0, tiled=False)
    boundary, up, down = call(
        couple_second,
        (shape((1, columns), f32), shape((8, LANES), f32), shape((8, LANES), f32)),
        scalars, surfaces, shared, index, weight,
    )
    low = lax.ppermute(up, AXES, forward)
    high = lax.ppermute(down, AXES, backward)
    final, parcels = call(
        step_second,
        (shape((levels, columns), f32), shape((8 * tiles, levels), f32)),
        scalars, window, rates, tend, mixing[0], coupling, boundary, low, high, listed, parcel,
    )
    arrived = lax.all_to_all(
        parcels.reshape(tiles, 8, levels), "tile", split_axis=0, concat_axis=0, tiled=True
    )
    rows = observed.shape[1]
    partial = call(
        project,
        shape((sections, STEPS * rows, levels), f32),
        arrived.reshape(8 * tiles, levels), spread, refraction[0],
    )
    received = lax.all_to_all(partial, "sec", split_axis=0, concat_axis=0, tiled=True)
    departures = call(
        depart, shape((STEPS, rows, observed.shape[2]), f32), received, abel_matrix, observed
    )
    return (final[None], departures)


def solution(mesh):
    return jax.shard_map(
        shards,
        mesh=mesh,
        in_specs=(
            P("sec", None, "tile"),
            P("sec", None, "tile"),
            P("sec", None, "tile"),
            P("sec", None, None),
            P("sec", None),
            P("sec", None, "tile"),
            P("sec", None, "tile"),
            P(),
            P(None, "sec", "tile", None, None),
            P(None, "sec", None, "tile"),
            P(None, "sec", None, "tile"),
            P(None, "sec", "tile"),
            P("sec", None, None),
            P(),
            P(None, ("sec", "tile"), None),
        ),
        out_specs=(P("sec", None, "tile"), P(None, ("sec", "tile"), None)),
        check_vma=False,
    )
```

time: 369 us -> 143 us (0.39)
  starting transfers between devices: 151 us -> 38.9 us
  waiting for transfers between devices: 122 us -> 29.5 us
  local copies, waits for them, and re-layouts: 36.7 us -> 6.17 us
  blocking collectives: 34.3 us -> 56.6 us
  between operations: 14.7 us -> 0.81 us
  Pallas kernels: 0 us -> 10.4 us
  matrix products: 5.55 us -> 0 us
  other arithmetic: 3.92 us -> 0 us
    ppermute x16 -> x4, starting transfers between devices: 134 us -> 23.9 us  [the longest x2 20.1 us: shards(): high = lax.ppermute(down, AXES, backward)]
    reduce_scatter x2 -> x0, waiting for transfers between devices: 91.1 us -> none  [observe(): owned = lax.psum_scatter(bending, 'sec', scatter_dimension=0, tiled=True)]
    gather x8 -> x0, local copies, waits for them, and re-layouts: 27.7 us -> none  [the longest x4 23.6 us: shards(): picked = jnp.take(surfaces.reshape(-1), position)]
    all_to_all x0 -> x1, blocking collectives: none -> 20.9 us  [shards(): lax.all_to_all(partial, 'sec', split_axis=0, concat_axis=0, tiled=True)]
    pallas_call x0 -> x8, Pallas kernels: none -> 10.4 us  [call(): pl.pallas_call(body, out_shape=outs if single else tuple(outs), in_specs=...]
    dot_general x12 -> x0, matrix products: 5.55 us -> none  [the longest x8 3.52 us: shards(): jnp.dot(matrix, spread, precision=highest, preferred_element_type=jnp.flo...]
  transfers between devices with their start and end apart: 19 -> 5, of which waited for: 9 -> 3; matrix products, arithmetic and copies ran while one was open for 5% -> 0% of each run, Pallas kernels for 0% -> 0%
where the time goes in v1:
time: 143 us; the launch traced here: 142 us
  blocking collectives  56.6 us (40%)
  starting transfers between devices  38.9 us (27%)
  waiting for transfers between devices  29.5 us (21%)
  Pallas kernels  10.4 us (7%)
  local copies, waits for them, and re-layouts  6.17 us (4%)
    all_to_all x1, waiting for transfers between devices, shards(): lax.all_to_all(parcels.reshape(tiles, 8, levels), 'tile', split_axis=0, c...  27.9 us
    all_gather x1, blocking collectives, shards(): shared = lax.all_gather(edges, 'sec', axis=0, tiled=False)  21 us
    all_to_all x1, blocking collectives, shards(): lax.all_to_all(partial, 'sec', split_axis=0, concat_axis=0, tiled=True)  20.9 us
    ppermute x2, starting transfers between devices, shards(): high = lax.ppermute(down, AXES, backward)  20.1 us
    all_to_all x1, starting transfers between devices, shards(): lax.all_to_all(parcels.reshape(tiles, 8, levels), 'tile', split_axis=0, c...  14.9 us
    all_gather x1, blocking collectives, shards(): surfaces = lax.all_gather(surface, 'sec', axis=0, tiled=False)  14.7 us
    pallas_call x8, Pallas kernels, call(): pl.pallas_call(body, out_shape=outs if single else tuple(outs), in_specs=...  10.4 us
    unnamed x32, local copies, waits for them, and re-layouts  4.74 us
  transfers between devices with their start and end apart: 5, of which 3 were waited for; matrix products, arithmetic and copies ran while one was open for 0% of the time, Pallas kernels for 0%

profile of v1, /device:TPU:1, one launch (start us, length us, event | category | flops | bytes accessed | tf_op | source)
XLA Modules:
  0.0 142.3 jit_solution(5511323488747736310)
XLA Ops:
  0.7 0.0 copy-start.15
  0.7 0.6 copy-done.15
  1.3 0.6 dynamic_slice.4
  2.0 0.0 copy-start.6
  2.0 0.0 copy-start.7
  2.0 0.8 stack.24.scalars
  2.7 0.0 copy-done.6
  2.7 0.0 copy-done.7
  2.7 0.0 copy-start
  2.8 0.9 copy-done
  3.7 0.0 copy-start.2
  3.7 0.9 copy-done.2
  4.6 0.0 copy-start.3
  4.6 0.9 copy-done.3
  5.5 0.0 copy-start.4
  5.5 0.8 shard_map.158
  6.3 0.0 copy-start.1
  6.3 21.0 %all-gather = f32[256,128]{1,0:T(8,128)S(1)} all-gather(f32[64,128]{1,0:T(8,128)S(1)} %shard_map.158), channel_id=2, replica_groups=mesh['sec'=4,'tile'=128] {'sec'}, dimensions={0}, use_global_device_ids=true | all-gather | bytes 163840 | tf_op jit(solution)/shard_map/all_gather | solution.py:322
  27.3 0.7 shard_map.159
  28.0 0.0 copy-start.10
  28.0 1.9 %collective-permute-start = (f32[32,128]{1,0:T(8,128)S(1)}, f32[32,128]{1,0:T(8,128)S(1)}, u32[]{:S(2)}, u32[]{:S(2)}) collective-permute-start(f32[32,128]{1,0:T(8,128)S(1)} %get-tuple-element.16), channel_id=1, source_target_pairs={{0,1},{1,2},{2,3},{3,4},{4,5},{5,6},{6,7},{7,8},{8,9},{9,10},{10,1... | collective-permute-start | bytes 49160 | tf_op jit(solution)/shard_map/ppermute | solution.py:328
  29.9 10.7 %collective-permute-start.1 = (f32[32,128]{1,0:T(8,128)S(1)}, f32[32,128]{1,0:T(8,128)S(1)}, u32[]{:S(2)}, u32[]{:S(2)}) collective-permute-start(f32[32,128]{1,0:T(8,128)S(1)} %get-tuple-element.17), channel_id=1, source_target_pairs={{1,0},{2,1},{3,2},{4,3},{5,4},{6,5},{7,6},{8,7},{9,8},{10,9},{11,1... | collective-permute-start | bytes 49160 | tf_op jit(solution)/shard_map/ppermute | solution.py:329
  40.7 0.0 collective-permute-done.low
  40.7 0.8 collective-permute-done.1.high
  41.5 0.0 copy-start.13
  41.5 0.0 copy-done.4
  41.5 0.0 copy-done.1
  41.5 0.0 copy-done.10
  41.6 0.6 copy-done.13
  42.2 2.8 %shard_map.160 = (f32[128,640]{1,0:T(8,128)S(1)}, f32[128,640]{1,0:T(8,128)S(1)}, f32[128,640]{1,0:T(8,128)S(1)}, f32[4,128]{1,0:T(4,128)S(1)}, f32[4,128,128]{2,1,0:T(8,128)S(1)}) custom-call(s32[6]{0:T(128)S(1)} %stack.24.scalars, f32[128,512]{1,0:T(8,128)S(1)} %bitcast.27, bf16[128,512]{1,0:T(8,128)(2,1)S(1)} %bitcast.29, bf16[128,512]{1,0:T(8,128)(2,1)S(1)} %bitcast.31, ...), custom_call_target="tpu_custom_call" | custom-call | tf_op jit(solution)/shard_map/pallas_call | solution.py:23
  45.0 14.7 %all-gather.2.surfaces = f32[4,4,128]{2,1,0:T(4,128)S(1)} all-gather(f32[1,4,128]{2,1,0:T(4,128)S(1)} %bitcast.45), channel_id=3, replica_groups=mesh['sec'=4,'tile'=128] {'sec'}, dimensions={0}, use_global_device_ids=true | all-gather | bytes 10240 | tf_op jit(solution)/shard_map/all_gather | solution.py:346
  59.7 0.7 shard_map.161
  60.4 1.9 %collective-permute-start.2 = (f32[8,128]{1,0:T(8,128)S(1)}, f32[8,128]{1,0:T(8,128)S(1)}, u32[]{:S(2)}, u32[]{:S(2)}) collective-permute-start(f32[8,128]{1,0:T(8,128)S(1)} %get-tuple-element.23), channel_id=1, source_target_pairs={{0,1},{1,2},{2,3},{3,4},{4,5},{5,6},{6,7},{7,8},{8,9},{9,10},{10,1... | collective-permute-start | bytes 12296 | tf_op jit(solution)/shard_map/ppermute | solution.py:352
  62.3 9.4 %collective-permute-start.3 = (f32[8,128]{1,0:T(8,128)S(1)}, f32[8,128]{1,0:T(8,128)S(1)}, u32[]{:S(2)}, u32[]{:S(2)}) collective-permute-start(f32[8,128]{1,0:T(8,128)S(1)} %get-tuple-element.24), channel_id=1, source_target_pairs={{1,0},{2,1},{3,2},{4,3},{5,4},{6,5},{7,6},{8,7},{9,8},{10,9},{11,1... | collective-permute-start | bytes 12296 | tf_op jit(solution)/shard_map/ppermute | solution.py:353
  71.7 0.0 collective-permute-done.2.low
  71.7 0.7 collective-permute-done.3.high
  72.4 3.6 %shard_map.162 = (f32[128,512]{1,0:T(8,128)}, f32[1024,128]{1,0:T(8,128)}) custom-call(s32[6]{0:T(128)S(1)} %stack.24.scalars, f32[128,640]{1,0:T(8,128)S(1)} %get-tuple-element.18.window, f32[128,640]{1,0:T(8,128)S(1)} %get-tuple-element.19.rates, f32[128,640]{1,0:T(8,128)S(1)} %get-tuple-element.20.tend, f32[128,128]{1,0:T(8,128)S(1)} %bitcast.33, ...), custom_call_target="tpu_custom_call" | custom-call | tf_op jit(solution)/shard_map/pallas_call | solution.py:23
  76.1 0.0 copy-start.11
  76.1 0.0 copy-start.12
  76.1 14.9 %all-to-all-start = ((f32[128,8,128]{2,1,0:T(8,128)}), f32[128,8,128]{2,1,0:T(8,128)S(1)}, u32[]{:S(2)}, u32[]{:S(2)}) async-start(f32[128,8,128]{2,1,0:T(8,128)} %bitcast.16), calls=%async_computation | async-start | bytes 1048576 | tf_op jit(solution)/shard_map/all_to_all | solution.py:359
  91.0 0.0 copy-start.14
  91.0 0.0 copy-done.11
  91.0 0.0 copy-done.12
  91.0 0.7 copy-done.14
  91.7 0.0 copy-start.8
  91.7 0.6 shard_map.163.spread
  92.3 27.9 %all-to-all-done = f32[128,8,128]{2,1,0:T(8,128)S(1)} async-done(((f32[128,8,128]{2,1,0:T(8,128)}), f32[128,8,128]{2,1,0:T(8,128)S(1)}, u32[]{:S(2)}, u32[]{:S(2)}) %all-to-all-start) | async-done | bytes 524320 | tf_op jit(solution)/shard_map/all_to_all | solution.py:359
  120.2 0.0 copy-done.8
  120.2 0.0 copy-start.9
  120.2 0.5 shard_map.164
  120.6 0.0 copy-start.5
  120.6 20.9 %all_to_all.10.received = f32[4,32,128]{2,1,0:T(8,128)S(1)} all-to-all(f32[4,32,128]{2,1,0:T(8,128)S(1)} %shard_map.164), channel_id=1, replica_groups=mesh['sec'=4,'tile'=128] {'sec'}, dimensions={0} | all-to-all | bytes 131072 | tf_op jit(solution)/shard_map/all_to_all | solution.py:368
  141.6 0.0 copy-done.9
  141.6 0.0 copy-done.5
  141.6 0.8 shard_map.165
Async XLA Ops:
  0.7 0.7 copy-start.15
  2.0 0.8 copy-start.6
  2.0 0.8 copy-start.7
  2.7 1.0 copy-start
  3.7 0.9 copy-start.2
  4.6 0.9 copy-start.3
  5.5 36.0 %copy-start.4 = (f32[1,128,128]{2,1,0:T(8,128)S(1)}, f32[1,128,128]{2,1,0:T(8,128)}, u32[]{:S(2)}) copy-start(f32[1,128,128]{2,1,0:T(8,128)} %param.18) | copy-start | bytes 196612
  6.3 35.3 %copy-start.1 = (f32[1,128,512]{2,1,0:T(8,128)S(1)}, f32[1,128,512]{2,1,0:T(8,128)}, u32[]{:S(2)}) copy-start(f32[1,128,512]{2,1,0:T(8,128)} %param.15) | copy-start | bytes 786436
  28.0 13.6 %copy-start.10 = (s32[2,1,1,128,4]{3,4,2,1,0:T(4,128)S(1)}, s32[2,1,1,128,4]{3,4,2,1,0:T(4,128)}, u32[]{:S(2)}) copy-start(s32[2,1,1,128,4]{3,4,2,1,0:T(4,128)} %param.23) | copy-start | bytes 12292
  28.0 12.7 %collective-permute-start = (f32[32,128]{1,0:T(8,128)S(1)}, f32[32,128]{1,0:T(8,128)S(1)}, u32[]{:S(2)}, u32[]{:S(2)}) collective-permute-start(f32[32,128]{1,0:T(8,128)S(1)} %get-tuple-element.16), channel_id=1, source_target_pairs={{0,1},{1,2},{2,3},{3,4},{4,5},{5,6},{6,7},{7,8},{8,9},{9,10},{10,1... | collective-permute-start | bytes 49160 | tf_op jit(solution)/shard_map/ppermute | solution.py:328
  29.9 11.6 %collective-permute-start.1 = (f32[32,128]{1,0:T(8,128)S(1)}, f32[32,128]{1,0:T(8,128)S(1)}, u32[]{:S(2)}, u32[]{:S(2)}) collective-permute-start(f32[32,128]{1,0:T(8,128)S(1)} %get-tuple-element.17), channel_id=1, source_target_pairs={{1,0},{2,1},{3,2},{4,3},{5,4},{6,5},{7,6},{8,7},{9,8},{10,9},{11,1... | collective-permute-start | bytes 49160 | tf_op jit(solution)/shard_map/ppermute | solution.py:329
  41.5 0.7 copy-start.13
  60.4 11.3 %collective-permute-start.2 = (f32[8,128]{1,0:T(8,128)S(1)}, f32[8,128]{1,0:T(8,128)S(1)}, u32[]{:S(2)}, u32[]{:S(2)}) collective-permute-start(f32[8,128]{1,0:T(8,128)S(1)} %get-tuple-element.23), channel_id=1, source_target_pairs={{0,1},{1,2},{2,3},{3,4},{4,5},{5,6},{6,7},{7,8},{8,9},{9,10},{10,1... | collective-permute-start | bytes 12296 | tf_op jit(solution)/shard_map/ppermute | solution.py:352
  62.3 10.1 %collective-permute-start.3 = (f32[8,128]{1,0:T(8,128)S(1)}, f32[8,128]{1,0:T(8,128)S(1)}, u32[]{:S(2)}, u32[]{:S(2)}) collective-permute-start(f32[8,128]{1,0:T(8,128)S(1)} %get-tuple-element.24), channel_id=1, source_target_pairs={{1,0},{2,1},{3,2},{4,3},{5,4},{6,5},{7,6},{8,7},{9,8},{10,9},{11,1... | collective-permute-start | bytes 12296 | tf_op jit(solution)/shard_map/ppermute | solution.py:353
  76.1 15.0 %copy-start.11 = (s32[2,1,8,64]{3,2,1,0:T(8,128)S(1)}, s32[2,1,8,64]{3,2,1,0:T(8,128)}, u32[]{:S(2)}) copy-start(s32[2,1,8,64]{3,2,1,0:T(8,128)} %param.24) | copy-start | bytes 12292
  76.1 15.0 %copy-start.12 = (f32[2,1,8,64]{3,2,1,0:T(8,128)S(1)}, f32[2,1,8,64]{3,2,1,0:T(8,128)}, u32[]{:S(2)}) copy-start(f32[2,1,8,64]{3,2,1,0:T(8,128)} %param.25) | copy-start | bytes 12292
  76.1 44.1 %all-to-all-start = ((f32[128,8,128]{2,1,0:T(8,128)}), f32[128,8,128]{2,1,0:T(8,128)S(1)}, u32[]{:S(2)}, u32[]{:S(2)}) async-start(f32[128,8,128]{2,1,0:T(8,128)} %bitcast.16), calls=%async_computation | async-start | bytes 1048576 | tf_op jit(solution)/shard_map/all_to_all | solution.py:359
  91.0 0.7 copy-start.14
  91.7 28.5 %copy-start.8 = (f32[1,128,128]{2,1,0:T(8,128)S(1)}, f32[1,128,128]{2,1,0:T(8,128)}, u32[]{:S(2)}) copy-start(f32[1,128,128]{2,1,0:T(8,128)} %param.27) | copy-start | bytes 196612
  120.2 21.4 %copy-start.9 = (f32[2,16,256]{2,1,0:T(8,128)S(1)}, f32[2,16,256]{2,1,0:T(8,128)}, u32[]{:S(2)}) copy-start(f32[2,16,256]{2,1,0:T(8,128)} %observed.1) | copy-start | bytes 98308
  120.6 20.9 %copy-start.5 = (f32[128,256]{1,0:T(8,128)S(1)}, f32[128,256]{1,0:T(8,128)}, u32[]{:S(2)}) copy-start(f32[128,256]{1,0:T(8,128)} %abel.1) | copy-start | bytes 393220

commit v2 on v1

v2 whole, which is shorter than its diff:
```python
import jax
import jax.numpy as jnp
from jax import lax
from jax.experimental import pallas as pl
from jax.experimental.pallas import tpu as pltpu
from jax.sharding import PartitionSpec as P

SUBS = 4
STEPS = 2
HALO = 8
LANES = 128
AXES = ("sec", "tile")
f32 = jnp.float32
bf16 = jnp.bfloat16


def call(body, outs, *args, scratch=(), space=pltpu.VMEM):
    in_specs = [
        pl.BlockSpec(memory_space=pltpu.SMEM if a.ndim == 1 else space) for a in args
    ]
    single = not isinstance(outs, (tuple, list))
    specs = pl.BlockSpec(memory_space=pltpu.VMEM)
    return pl.pallas_call(
        body,
        out_shape=outs if single else tuple(outs),
        in_specs=in_specs,
        out_specs=specs if single else tuple(specs for _ in outs),
        scratch_shapes=list(scratch),
        compiler_params=pltpu.CompilerParams(vmem_limit_bytes=40 * 2**20),
    )(*args)


def halves(x):
    high = x.astype(bf16)
    return high, (x - high.astype(f32)).astype(bf16)


def left_operand(x):
    high, low = halves(x)
    return jnp.concatenate([high, high, low], axis=1)


def right_operand(x):
    high, low = halves(x)
    return jnp.concatenate([high, low, high], axis=0)


def matmul(left, right):
    return jnp.dot(left, right, preferred_element_type=f32)


def pick(table, position):
    lane = position & (LANES - 1)
    row = position >> 7
    out = jnp.zeros(position.shape, f32)
    for r, values in enumerate(table):
        source = jnp.broadcast_to(values, position.shape)
        found = jnp.take_along_axis(source, lane, axis=1, mode="promise_in_bounds")
        out = jnp.where(row == r, found, out)
    return out


def position_offset(columns):
    ocean = lax.axis_size("sec") - 1
    return jnp.where(lax.axis_index("sec") == ocean, 0, ocean * columns)


def edge_sources():
    section, tile = lax.axis_index("sec"), lax.axis_index("tile")
    sections = lax.axis_size("sec")
    other = section + sections // 2
    other = jnp.where(other >= sections, other - sections, other)
    last = lax.axis_size("tile") - 1
    return jnp.where(tile == last, other, section), jnp.where(tile == 0, other, section)


def lane_ids(shape):
    return lax.broadcasted_iota(jnp.int32, shape, len(shape) - 1)


def pack_edges(first, last):
    lane = lane_ids(first.shape)
    return jnp.where(lane < HALO, first, pltpu.roll(last, 2 * HALO, 1))


def prepare(state, tendency, diffusion, index, weight, out, *scratch):
    levels, columns = state.shape
    tail = columns - LANES
    *ends, bottom, indices, weights, sems = scratch
    pairs = []
    for ref, head, back in zip((state, diffusion, tendency), ends[::2], ends[1::2]):
        pairs.append((ref.at[:, pl.ds(0, LANES)], head))
        pairs.append((ref.at[:, pl.ds(tail, LANES)], back))
    pairs.append((state.at[pl.ds(levels - 8, 8), :], bottom))
    pairs.append((index, indices))
    pairs.append((weight, weights))
    copies = [
        pltpu.make_async_copy(source, target, sems.at[i])
        for i, (source, target) in enumerate(pairs)
    ]
    for copy in copies:
        copy.start()
    for copy in copies:
        copy.wait()
    block = jnp.zeros((levels, LANES), f32)
    lane = lane_ids(block.shape)
    for i in range(3):
        edges = pack_edges(ends[2 * i][...].astype(f32), ends[2 * i + 1][...].astype(f32))
        if i:
            edges = pltpu.roll(edges, 2 * HALO * i, 1)
        inside = (lane >= 2 * HALO * i) & (lane < 2 * HALO * (i + 1))
        block = jnp.where(inside, edges, block)
    out[0:48, :] = block.T[0:48, :]
    for j in range(columns // LANES):
        out[48 + j : 49 + j, :] = bottom[7:8, j * LANES : (j + 1) * LANES]
    out[52:56, :] = pack_edges(weights[:, :LANES], weights[:, tail:])
    position = (indices[...] + position_offset(columns)).astype(f32)
    out[56:60, :] = pack_edges(position[:, :LANES], position[:, tail:])
    out[60:64, :] = jnp.zeros((4, LANES), f32)


def edge_boundary(table, shared, surface_first, surface_last, source):
    position = shared[source, 56:60, :].astype(jnp.int32)
    picked = pick(table, position)
    partner = jnp.sum(shared[source, 52:56, :] * picked, axis=0, keepdims=True)
    return partner - pack_edges(surface_first, surface_last)


def own_boundary(table, index, weight, surface, out):
    offset = position_offset(out.shape[1])
    for j in range(out.shape[1] // LANES):
        cut = slice(j * LANES, (j + 1) * LANES)
        picked = pick(table, index[:, cut] + offset)
        partner = jnp.sum(weight[:, cut] * picked, axis=0, keepdims=True)
        out[:, cut] = partner - surface(j)


def couple_first(shared, index, weight, boundary, forward, backward):
    section = lax.axis_index("sec")
    table = [shared[s, r : r + 1, :] for s in range(shared.shape[0]) for r in range(48, 52)]
    own_boundary(
        table, index, weight, lambda j: shared[section, 48 + j : 49 + j, :], boundary
    )
    for out, source, start in zip((forward, backward), edge_sources(), (HALO, 0)):
        for i in range(3):
            row = 2 * HALO * i + start
            out[HALO * i : HALO * (i + 1), :] = shared[source, row : row + HALO, :]
        edge = edge_boundary(
            table, shared, shared[source, 48:49, :], shared[source, 51:52, :], source
        )
        out[24:32, :] = jnp.broadcast_to(edge, (8, LANES))


def couple_second(surfaces, shared, index, weight, boundary, forward, backward):
    section = lax.axis_index("sec")
    table = [surfaces[s, r : r + 1, :] for s in range(surfaces.shape[0]) for r in range(4)]
    own_boundary(
        table, index, weight, lambda j: surfaces[section, j : j + 1, :], boundary
    )
    for out, source in zip((forward, backward), edge_sources()):
        edge = edge_boundary(
            table, shared, surfaces[source, 0:1, :], surfaces[source, 3:4, :], source
        )
        out[...] = jnp.broadcast_to(edge, out.shape)


def edge_row(left, right):
    lane = lane_ids(left.shape)
    value = jnp.where(lane < HALO, right, 0.0)
    return jnp.where(lane >= LANES - HALO, pltpu.roll(left, LANES - 2 * HALO, 1), value)


def edge_block(left, right):
    gap = jnp.zeros((LANES - 2 * HALO, left.shape[1]), f32)
    return jnp.concatenate([right, gap, left], axis=0).T


def advance(field, rates, constant, left, alive):
    width = field.shape[1]
    live = alive[...] > 0.0
    for _ in range(SUBS):
        near = pltpu.roll(field, 1, 1) + pltpu.roll(field, width - 1, 1)
        spread = field + rates * (near - 2.0 * field)
        stepped = matmul(left, right_operand(spread)) + constant
        field = jnp.where(live, stepped, field)
    return field


def forcing(response, boundary, edge, tendency):
    row = jnp.concatenate([boundary[...], edge], axis=1)
    width = row.shape[1]
    parts = [
        response * row[:, j * LANES : (j + 1) * LANES] for j in range(width // LANES)
    ]
    return jnp.concatenate(parts, axis=1) + tendency


def one_hot(listed, columns):
    row = jnp.concatenate([listed[m : m + 1, :] for m in range(listed.shape[0])], axis=1)
    column = lax.broadcasted_iota(jnp.int32, (columns, row.shape[1]), 0)
    return jnp.where(column == row, 1.0, 0.0).astype(bf16)


def chosen(field, hits):
    levels = field.shape[0]
    high, low = halves(field[:, : hits.shape[0]])
    both = matmul(jnp.concatenate([high, low], axis=0), hits[...])
    both = both[:levels] + both[levels:]
    tiles = hits.shape[1] // 4
    return [both[:, m * tiles : (m + 1) * tiles].T for m in range(4)]


def step_first(
    state, tendency, diffusion, left, response, alive, hits, boundary, low, high,
    window, rates_out, forcing_out, surface, parcel,
):
    rates = jnp.concatenate(
        [diffusion[...].astype(f32), edge_block(low[8:16, :], high[8:16, :])], axis=1
    )
    tend = jnp.concatenate(
        [tendency[...].astype(f32), edge_block(low[16:24, :], high[16:24, :])], axis=1
    )
    field = jnp.concatenate([state[...], edge_block(low[0:8, :], high[0:8, :])], axis=1)
    edge = edge_row(low[24:25, :], high[24:25, :])
    constant = forcing(response[...], boundary, edge, tend)
    rates_out[...] = rates
    forcing_out[...] = tend
    field = advance(field, rates, constant, left[...], alive)
    window[...] = field
    levels = field.shape[0]
    for j in range(4):
        surface[j : j + 1, :] = field[levels - 1 : levels, j * LANES : (j + 1) * LANES]
    for m, rows in enumerate(chosen(field, hits)):
        parcel[m] = rows


def step_second(
    window, rates, tend, left, response, alive, hits, boundary, low, high, earlier,
    final, parcels,
):
    edge = edge_row(low[0:1, :], high[0:1, :])
    constant = forcing(response[...], boundary, edge, tend[...])
    field = advance(window[...], rates[...], constant, left[...], alive)
    final[...] = field[:, : final.shape[1]]
    slots = earlier.shape[0]
    tiles = earlier.shape[1]
    for m in range(slots):
        parcels[pl.ds(m, tiles, stride=2 * slots), :] = earlier[m]
    for m, rows in enumerate(chosen(field, hits)):
        parcels[pl.ds(slots + m, tiles, stride=2 * slots), :] = rows


def ready_first(active, mixing, coupling, listed, left, response, alive, hits):
    width = alive.shape[1]
    lane = lane_ids((1, width))
    column = jnp.where(lane < width - LANES, lane, lane - (width - LANES))
    column = jnp.where(lane < width - HALO, column, lane - LANES)
    alive[...] = jnp.where(column < active[lax.axis_index("sec")], 1.0, 0.0)
    left[...] = left_operand(mixing[...])
    response[...] = jnp.broadcast_to(coupling[...], (LANES, coupling.shape[1])).T
    hits[...] = one_hot(listed[0], hits.shape[0])


def ready_second(listed, slots, weights, counts, refraction, abel, hits, spread, right, right_abel):
    hits[...] = one_hot(listed[1], hits.shape[0])
    right[...] = right_operand(refraction[...])
    right_abel[...] = right_operand(abel[...])
    steps, ranks, occultations = slots.shape
    width = spread.shape[2] // 3
    tiles = width // 4
    for p in range(steps):
        rank = lax.broadcasted_iota(jnp.int32, (ranks, occultations), 0)
        live = jnp.where(rank < counts[p : p + 1, :], weights[p], 0.0).T
        key = ((slots[p] & 3) * tiles + (slots[p] >> 2)).T
        place = lane_ids((occultations, width))
        total = jnp.zeros((occultations, width), f32)
        for k in range(ranks):
            total = total + jnp.where(key[:, k : k + 1] == place, live[:, k : k + 1], 0.0)
        spread[p] = left_operand(total)


def project(arrived, spread, refraction, out):
    steps, occultations, width = spread.shape
    tiles = width // 12
    owners = out.shape[0]
    rows = occultations // owners
    profiles = []
    for p in range(steps):
        values = jnp.concatenate(
            [arrived[pl.ds(4 * p + m, tiles, stride=4 * steps), :] for m in range(4)], axis=0
        )
        profiles.append(matmul(spread[p], right_operand(values)))
    profile = jnp.concatenate(profiles, axis=0)
    projected = matmul(left_operand(profile), refraction[...])
    for p in range(steps):
        for q in range(owners):
            start = p * occultations + q * rows
            out[q, p * rows : (p + 1) * rows, :] = projected[start : start + rows, :]


def depart(received, abel, observed, out):
    total = received[0]
    for s in range(1, received.shape[0]):
        total = total + received[s]
    bending = matmul(left_operand(total), abel[...])
    steps, rows, _ = observed.shape
    for p in range(steps):
        out[p] = observed[p] - bending[p * rows : (p + 1) * rows, :]


def shards(
    state,
    tendency,
    diffusion,
    mixing,
    coupling,
    remap_index,
    remap_weight,
    active_cols,
    send_cols,
    occ_slot,
    occ_weight,
    occ_count,
    refraction,
    abel_matrix,
    observed,
):
    sections = lax.axis_size("sec")
    tiles = lax.axis_size("tile")
    levels, columns = state.shape[1:]
    rows, heights = observed.shape[1:]
    width = columns + LANES
    half = sections // 2
    forward = []
    for s in range(sections):
        for t in range(tiles):
            seam = t == tiles - 1
            target = ((s + half) % sections if seam else s) * tiles + (t + 1) % tiles
            forward.append((s * tiles + t, target))
    backward = [(target, source) for source, target in forward]
    listed = jnp.transpose(send_cols[:, 0, 0], (0, 2, 1))
    index, weight = remap_index[0], remap_weight[0]
    shape = jax.ShapeDtypeStruct
    after = lax.optimization_barrier

    edges = call(
        prepare,
        shape((64, LANES), f32),
        *(
            pltpu.with_memory_space_constraint(x, pltpu.HBM)
            for x in (state[0], tendency[0], diffusion[0], index, weight)
        ),
        space=pltpu.HBM,
        scratch=[pltpu.VMEM((levels, LANES), f32)] * 2
        + [pltpu.VMEM((levels, LANES), bf16)] * 4
        + [
            pltpu.VMEM((8, columns), f32),
            pltpu.VMEM(index.shape, jnp.int32),
            pltpu.VMEM(weight.shape, f32),
            pltpu.SemaphoreType.DMA((9,)),
        ],
    )
    shared = lax.all_gather(edges, "sec", axis=0, tiled=False)
    boundary, up, down = call(
        couple_first,
        (shape((1, columns), f32), shape((32, LANES), f32), shape((32, LANES), f32)),
        shared, index, weight,
    )
    low = lax.ppermute(up, AXES, forward)
    high = lax.ppermute(down, AXES, backward)
    mixing_row, _ = after((mixing[0], boundary))
    left, response, alive, hits = call(
        ready_first,
        (
            shape((levels, 3 * levels), bf16),
            shape((levels, LANES), f32),
            shape((1, width), f32),
            shape((columns, 4 * tiles), bf16),
        ),
        active_cols, mixing_row, coupling, listed,
    )
    window, rates, tend, surface, parcel = call(
        step_first,
        (
            shape((levels, width), f32),
            shape((levels, width), f32),
            shape((levels, width), f32),
            shape((4, LANES), f32),
            shape((4, tiles, levels), f32),
        ),
        state[0], tendency[0], diffusion[0], left, response, alive, hits, boundary, low, high,
    )
    surfaces = lax.all_gather(surface, "sec", axis=0, tiled=False)
    boundary, up, down = call(
        couple_second,
        (shape((1, columns), f32), shape((8, LANES), f32), shape((8, LANES), f32)),
        surfaces, shared, index, weight,
    )
    low = lax.ppermute(up, AXES, forward)
    high = lax.ppermute(down, AXES, backward)
    weights, _ = after((occ_weight[:, 0], boundary))
    hits, spread, right, right_abel = call(
        ready_second,
        (
            shape((columns, 4 * tiles), bf16),
            shape((STEPS, occ_slot.shape[3], 12 * tiles), bf16),
            shape((3 * levels, levels), bf16),
            shape((3 * levels, heights), bf16),
        ),
        listed, occ_slot[:, 0], weights, occ_count[:, 0], refraction[0], abel_matrix,
    )
    final, parcels = call(
        step_second,
        (shape((levels, columns), f32), shape((8 * tiles, levels), f32)),
        window, rates, tend, left, response, alive, hits, boundary, low, high, parcel,
    )
    parcels, spread, right, right_abel, observed = after(
        (parcels, spread, right, right_abel, observed)
    )
    arrived = lax.all_to_all(
        parcels.reshape(tiles, 8, levels), "tile", split_axis=0, concat_axis=0, tiled=True
    )
    partial = call(
        project,
        shape((sections, STEPS * rows, levels), f32),
        arrived.reshape(8 * tiles, levels), spread, right,
    )
    received = lax.all_to_all(partial, "sec", split_axis=0, concat_axis=0, tiled=True)
    departures = call(
        depart, shape((STEPS, rows, heights), f32), received, right_abel, observed
    )
    return (final[None], departures)


def solution(mesh):
    return jax.shard_map(
        shards,
        mesh=mesh,
        in_specs=(
            P("sec", None, "tile"),
            P("sec", None, "tile"),
            P("sec", None, "tile"),
            P("sec", None, None),
            P("sec", None),
            P("sec", None, "tile"),
            P("sec", None, "tile"),
            P(),
            P(None, "sec", "tile", None, None),
            P(None, "sec", None, "tile"),
            P(None, "sec", None, "tile"),
            P(None, "sec", "tile"),
            P("sec", None, None),
            P(),
            P(None, ("sec", "tile"), None),
        ),
        out_specs=(P("sec", None, "tile"), P(None, ("sec", "tile"), None)),
        check_vma=False,
    )
```

time: 143 us -> 134 us (0.937)
  blocking collectives: 56.6 us -> 99.5 us
  waiting for transfers between devices: 29.5 us -> 0.01 us
  starting transfers between devices: 38.9 us -> 23.9 us
  local copies, waits for them, and re-layouts: 6.17 us -> 0.71 us
  Pallas kernels: 10.4 us -> 8.96 us
    all_to_all x0 -> x1, blocking collectives: none -> 43 us  [shards(): lax.all_to_all(parcels.reshape(tiles, 8, levels), 'tile', split_axis=0, c...]
    all_to_all x1 -> x0, waiting for transfers between devices: 27.9 us -> none  [shards(): lax.all_to_all(parcels.reshape(tiles, 8, levels), 'tile', split_axis=0, c...]
    all_to_all x1 -> x0, starting transfers between devices: 14.9 us -> none  [shards(): lax.all_to_all(parcels.reshape(tiles, 8, levels), 'tile', split_axis=0, c...]
    unnamed x32 -> x30, local copies, waits for them, and re-layouts: 4.74 us -> 0.71 us
    ppermute x2, waiting for transfers between devices: 1.56 us -> 0.01 us  [shards(): high = lax.ppermute(down, AXES, backward)]
    pallas_call x8 -> x9, Pallas kernels: 10.4 us -> 8.96 us  [call(): pl.pallas_call(body, out_shape=outs if single else tuple(outs), in_specs=...]
  transfers between devices with their start and end apart: 5 -> 4, of which waited for: 3 -> 0; matrix products, arithmetic and copies ran while one was open for 0% -> 0% of each run, Pallas kernels for 0% -> 1%
where the time goes in v2:
time: 134 us
  blocking collectives  99.5 us (74%)
  starting transfers between devices  23.9 us (18%)
  Pallas kernels  8.96 us (7%)
    all_to_all x1, blocking collectives, shards(): lax.all_to_all(parcels.reshape(tiles, 8, levels), 'tile', split_axis=0, c...  43 us
    all_gather x1, blocking collectives, shards(): shared = lax.all_gather(edges, 'sec', axis=0, tiled=False)  21 us
    all_to_all x1, blocking collectives, shards(): lax.all_to_all(partial, 'sec', split_axis=0, concat_axis=0, tiled=True)  20.8 us
    ppermute x2, starting transfers between devices, shards(): high = lax.ppermute(down, AXES, backward)  20.1 us
    all_gather x1, blocking collectives, shards(): surfaces = lax.all_gather(surface, 'sec', axis=0, tiled=False)  14.8 us
    pallas_call x9, Pallas kernels, call(): pl.pallas_call(body, out_shape=outs if single else tuple(outs), in_specs=...  8.96 us
    ppermute x2, starting transfers between devices, shards(): low = lax.ppermute(up, AXES, forward)  3.84 us
  transfers between devices with their start and end apart: 4, of which 0 were waited for; matrix products, arithmetic and copies ran while one was open for 0% of the time, Pallas kernels for 1%

profile of v2, /device:TPU:1, one launch (start us, length us, event | category | flops | bytes accessed | tf_op | source)
XLA Modules:
  0.0 134.1 jit_solution(5862665251007582401)
XLA Ops:
  0.6 0.0 copy-start.4
  0.6 0.0 copy-start.5
  0.7 0.0 copy-start.6
  0.7 0.0 copy-start.2
  0.7 1.2 shard_map.158
  1.9 0.0 copy-start.9
  1.9 0.0 copy-start.13
  1.9 0.0 copy-start.14
  2.0 0.0 copy-start
  2.0 21.0 %all-gather = f32[256,128]{1,0:T(8,128)S(1)} all-gather(f32[64,128]{1,0:T(8,128)S(1)} %shard_map.158), channel_id=2, replica_groups=mesh['sec'=4,'tile'=128] {'sec'}, dimensions={0}, use_global_device_ids=true | all-gather | bytes 163840 | tf_op jit(solution)/shard_map/all_gather | solution.py:363
  22.9 0.0 copy-start.1
  23.0 0.0 copy-done.4
  23.0 0.0 copy-done.5
  23.0 0.2 shard_map.159
  23.2 1.9 %collective-permute-start = (f32[32,128]{1,0:T(8,128)S(1)}, f32[32,128]{1,0:T(8,128)S(1)}, u32[]{:S(2)}, u32[]{:S(2)}) collective-permute-start(f32[32,128]{1,0:T(8,128)S(1)} %get-tuple-element.36), channel_id=1, source_target_pairs={{0,1},{1,2},{2,3},{3,4},{4,5},{5,6},{6,7},{7,8},{8,9},{9,10},{10,1... | collective-permute-start | bytes 49160 | tf_op jit(solution)/shard_map/ppermute | solution.py:369
  25.1 10.7 %collective-permute-start.1 = (f32[32,128]{1,0:T(8,128)S(1)}, f32[32,128]{1,0:T(8,128)S(1)}, u32[]{:S(2)}, u32[]{:S(2)}) collective-permute-start(f32[32,128]{1,0:T(8,128)S(1)} %get-tuple-element.37), channel_id=1, source_target_pairs={{1,0},{2,1},{3,2},{4,3},{5,4},{6,5},{7,6},{8,7},{9,8},{10,9},{11,1... | collective-permute-start | bytes 49160 | tf_op jit(solution)/shard_map/ppermute | solution.py:370
  35.8 0.0 copy-done.6
  35.9 0.0 copy-done.9
  35.9 0.0 copy-done.13
  35.9 0.0 copy-done.14
  35.9 0.8 shard_map.160
  36.7 0.0 collective-permute-done.low
  36.7 0.0 collective-permute-done.1.high
  36.7 0.0 copy-done.2
  36.7 0.0 copy-done
  36.7 0.0 copy-done.1
  36.8 0.0 copy-start.7
  36.8 2.0 %shard_map.161 = (f32[128,640]{1,0:T(8,128)S(1)}, f32[128,640]{1,0:T(8,128)S(1)}, f32[128,640]{1,0:T(8,128)S(1)}, f32[4,128]{1,0:T(4,128)S(1)}, f32[4,128,128]{2,1,0:T(8,128)S(1)}) custom-call(f32[128,512]{1,0:T(8,128)S(1)} %bitcast.22, bf16[128,512]{1,0:T(8,128)(2,1)S(1)} %bitcast.25, bf16[128,512]{1,0:T(8,128)(2,1)S(1)} %bitcast.27, ...), custom_call_target="tpu_custom_call" | custom-call | tf_op jit(solution)/shard_map/pallas_call | solution.py:23
  38.8 0.0 copy-start.3
  38.8 14.8 %all-gather.2.surfaces = f32[4,4,128]{2,1,0:T(4,128)S(1)} all-gather(f32[1,4,128]{2,1,0:T(4,128)S(1)} %bitcast.40), channel_id=3, replica_groups=mesh['sec'=4,'tile'=128] {'sec'}, dimensions={0}, use_global_device_ids=true | all-gather | bytes 10240 | tf_op jit(solution)/shard_map/all_gather | solution.py:393
  53.6 0.0 copy-start.11
  53.6 0.2 shard_map.162
  53.8 0.0 copy-start.10
  53.8 1.9 %collective-permute-start.2 = (f32[8,128]{1,0:T(8,128)S(1)}, f32[8,128]{1,0:T(8,128)S(1)}, u32[]{:S(2)}, u32[]{:S(2)}) collective-permute-start(f32[8,128]{1,0:T(8,128)S(1)} %get-tuple-element.45), channel_id=1, source_target_pairs={{0,1},{1,2},{2,3},{3,4},{4,5},{5,6},{6,7},{7,8},{8,9},{9,10},{10,1... | collective-permute-start | bytes 12296 | tf_op jit(solution)/shard_map/ppermute | solution.py:399
  55.7 9.4 %collective-permute-start.3 = (f32[8,128]{1,0:T(8,128)S(1)}, f32[8,128]{1,0:T(8,128)S(1)}, u32[]{:S(2)}, u32[]{:S(2)}) collective-permute-start(f32[8,128]{1,0:T(8,128)S(1)} %get-tuple-element.46), channel_id=1, source_target_pairs={{1,0},{2,1},{3,2},{4,3},{5,4},{6,5},{7,6},{8,7},{9,8},{10,9},{11,1... | collective-permute-start | bytes 12296 | tf_op jit(solution)/shard_map/ppermute | solution.py:400
  65.1 0.0 copy-start.12
  65.1 0.0 copy-done.7
  65.1 0.0 copy-done.3
  65.1 0.0 copy-done.11
  65.2 0.0 copy-done.10
  65.2 0.6 copy-done.12
  65.8 0.8 shard_map.163
  66.6 0.0 collective-permute-done.2.low
  66.6 0.0 collective-permute-done.3.high
  66.6 2.5 %shard_map.164 = (f32[128,512]{1,0:T(8,128)}, f32[1024,128]{1,0:T(8,128)S(1)}) custom-call(f32[128,640]{1,0:T(8,128)S(1)} %get-tuple-element.38.window, f32[128,640]{1,0:T(8,128)S(1)} %get-tuple-element.39.rates, f32[128,640]{1,0:T(8,128)S(1)} %get-tuple-element.40.tend, bf16[128,384]{1,0:T(8,128)(2,1)S(1)} %get-tuple-element.32.left, ...), custom_call_target="tpu_custom_call" | custom-call | tf_op jit(solution)/shard_map/pallas_call | solution.py:23
  69.1 43.0 %all_to_all.10 = f32[128,8,128]{2,1,0:T(8,128)S(1)} all-to-all(f32[128,8,128]{2,1,0:T(8,128)S(1)} %bitcast.23), channel_id=1, replica_groups=mesh['sec'=4,'tile'=128] {'tile'}, dimensions={0} | all-to-all | bytes 1048576 | tf_op jit(solution)/shard_map/all_to_all | solution.py:420
  112.1 0.4 shard_map.165
  112.5 0.0 copy-start.8
  112.5 20.8 %all_to_all.11.received = f32[4,32,128]{2,1,0:T(8,128)S(1)} all-to-all(f32[4,32,128]{2,1,0:T(8,128)S(1)} %shard_map.165), channel_id=1, replica_groups=mesh['sec'=4,'tile'=128] {'sec'}, dimensions={0} | all-to-all | bytes 131072 | tf_op jit(solution)/shard_map/all_to_all | solution.py:428
  133.3 0.0 copy-done.8
  133.3 0.8 shard_map.166
Async XLA Ops:
  0.6 22.3 %copy-start.4 = (s32[1,4,512]{2,1,0:T(4,128)S(1)}, s32[1,4,512]{2,1,0:T(4,128)}, u32[]{:S(2)}) copy-start(s32[1,4,512]{2,1,0:T(4,128)} %param.20) | copy-start | bytes 24580
  0.6 22.3 %copy-start.5 = (f32[1,4,512]{2,1,0:T(4,128)S(1)}, f32[1,4,512]{2,1,0:T(4,128)}, u32[]{:S(2)}) copy-start(f32[1,4,512]{2,1,0:T(4,128)} %param.21) | copy-start | bytes 24580
  0.7 35.2 %copy-start.6 = (f32[1,128,128]{2,1,0:T(8,128)S(1)}, f32[1,128,128]{2,1,0:T(8,128)}, u32[]{:S(2)}) copy-start(f32[1,128,128]{2,1,0:T(8,128)} %param.18) | copy-start | bytes 196612
  0.7 36.1 %copy-start.2 = (bf16[1,128,512]{2,1,0:T(8,128)(2,1)S(1)}, bf16[1,128,512]{2,1,0:T(8,128)(2,1)}, u32[]{:S(2)}) copy-start(bf16[1,128,512]{2,1,0:T(8,128)(2,1)} %param.17) | copy-start | bytes 393220
  1.9 33.9 %copy-start.9 = (s32[2,1,1,128,4]{3,4,2,1,0:T(4,128)S(1)}, s32[2,1,1,128,4]{3,4,2,1,0:T(4,128)}, u32[]{:S(2)}) copy-start(s32[2,1,1,128,4]{3,4,2,1,0:T(4,128)} %param.23) | copy-start | bytes 12292
  1.9 33.9 %copy-start.13 = (s32[4]{0:T(128)S(1)}, s32[4]{0:T(128)}, u32[]{:S(2)}) copy-start(s32[4]{0:T(128)} %active.1) | copy-start | bytes 52
  1.9 33.9 %copy-start.14 = (f32[1,128]{1,0:T(1,128)S(1)}, f32[1,128]{1,0:T(1,128)}, u32[]{:S(2)}) copy-start(f32[1,128]{1,0:T(1,128)} %coupling.1) | copy-start | bytes 1540
  2.0 34.8 %copy-start = (f32[1,128,512]{2,1,0:T(8,128)S(1)}, f32[1,128,512]{2,1,0:T(8,128)}, u32[]{:S(2)}) copy-start(f32[1,128,512]{2,1,0:T(8,128)} %param.15) | copy-start | bytes 786436
  22.9 13.8 %copy-start.1 = (bf16[1,128,512]{2,1,0:T(8,128)(2,1)S(1)}, bf16[1,128,512]{2,1,0:T(8,128)(2,1)}, u32[]{:S(2)}) copy-start(bf16[1,128,512]{2,1,0:T(8,128)(2,1)} %param.16) | copy-start | bytes 393220
  23.2 13.5 %collective-permute-start = (f32[32,128]{1,0:T(8,128)S(1)}, f32[32,128]{1,0:T(8,128)S(1)}, u32[]{:S(2)}, u32[]{:S(2)}) collective-permute-start(f32[32,128]{1,0:T(8,128)S(1)} %get-tuple-element.36), channel_id=1, source_target_pairs={{0,1},{1,2},{2,3},{3,4},{4,5},{5,6},{6,7},{7,8},{8,9},{9,10},{10,1... | collective-permute-start | bytes 49160 | tf_op jit(solution)/shard_map/ppermute | solution.py:369
  25.1 11.6 %collective-permute-start.1 = (f32[32,128]{1,0:T(8,128)S(1)}, f32[32,128]{1,0:T(8,128)S(1)}, u32[]{:S(2)}, u32[]{:S(2)}) collective-permute-start(f32[32,128]{1,0:T(8,128)S(1)} %get-tuple-element.37), channel_id=1, source_target_pairs={{1,0},{2,1},{3,2},{4,3},{5,4},{6,5},{7,6},{8,7},{9,8},{10,9},{11,1... | collective-permute-start | bytes 49160 | tf_op jit(solution)/shard_map/ppermute | solution.py:370
  36.8 28.4 %copy-start.7 = (f32[1,128,128]{2,1,0:T(8,128)S(1)}, f32[1,128,128]{2,1,0:T(8,128)}, u32[]{:S(2)}) copy-start(f32[1,128,128]{2,1,0:T(8,128)} %param.27) | copy-start | bytes 196612
  38.8 26.3 %copy-start.3 = (f32[128,256]{1,0:T(8,128)S(1)}, f32[128,256]{1,0:T(8,128)}, u32[]{:S(2)}) copy-start(f32[128,256]{1,0:T(8,128)} %abel.1) | copy-start | bytes 393220
  53.6 11.5 %copy-start.11 = (f32[2,1,8,64]{3,2,1,0:T(8,128)S(1)}, f32[2,1,8,64]{3,2,1,0:T(8,128)}, u32[]{:S(2)}) copy-start(f32[2,1,8,64]{3,2,1,0:T(8,128)} %param.25) | copy-start | bytes 12292
  53.8 11.4 %copy-start.10 = (s32[2,1,8,64]{3,2,1,0:T(8,128)S(1)}, s32[2,1,8,64]{3,2,1,0:T(8,128)}, u32[]{:S(2)}) copy-start(s32[2,1,8,64]{3,2,1,0:T(8,128)} %param.24) | copy-start | bytes 12292
  53.8 12.8 %collective-permute-start.2 = (f32[8,128]{1,0:T(8,128)S(1)}, f32[8,128]{1,0:T(8,128)S(1)}, u32[]{:S(2)}, u32[]{:S(2)}) collective-permute-start(f32[8,128]{1,0:T(8,128)S(1)} %get-tuple-element.45), channel_id=1, source_target_pairs={{0,1},{1,2},{2,3},{3,4},{4,5},{5,6},{6,7},{7,8},{8,9},{9,10},{10,1... | collective-permute-start | bytes 12296 | tf_op jit(solution)/shard_map/ppermute | solution.py:399
  55.7 10.9 %collective-permute-start.3 = (f32[8,128]{1,0:T(8,128)S(1)}, f32[8,128]{1,0:T(8,128)S(1)}, u32[]{:S(2)}, u32[]{:S(2)}) collective-permute-start(f32[8,128]{1,0:T(8,128)S(1)} %get-tuple-element.46), channel_id=1, source_target_pairs={{1,0},{2,1},{3,2},{4,3},{5,4},{6,5},{7,6},{8,7},{9,8},{10,9},{11,1... | collective-permute-start | bytes 12296 | tf_op jit(solution)/shard_map/ppermute | solution.py:400
  65.1 0.7 copy-start.12
  112.5 20.8 %copy-start.8 = (f32[2,16,256]{2,1,0:T(8,128)S(1)}, f32[2,16,256]{2,1,0:T(8,128)}, u32[]{:S(2)}) copy-start(f32[2,16,256]{2,1,0:T(8,128)} %observed) | copy-start | bytes 98308

commit v3 on v2

--- a/solution.py
+++ b/solution.py
@@ -72,6 +72,25 @@
     other = jnp.where(other >= sections, other - sections, other)
     last = lax.axis_size("tile") - 1
     return jnp.where(tile == last, other, section), jnp.where(tile == 0, other, section)
+
+
+def even_tile():
+    return lax.rem(lax.axis_index("tile"), 2) == 0
+
+
+def sent_edges():
+    up, down = edge_sources()
+    even = even_tile()
+    return (
+        (jnp.where(even, down, up), jnp.where(even, 0, HALO)),
+        (jnp.where(even, up, down), jnp.where(even, HALO, 0)),
+    )
+
+
+def sides(odd, even, start, rows):
+    first, second = odd[start : start + rows, :], even[start : start + rows, :]
+    here = even_tile()
+    return jnp.where(here, first, second), jnp.where(here, second, first)
 
 
 def lane_ids(shape):
@@ -135,29 +154,29 @@
         out[:, cut] = partner - surface(j)
 
 
-def couple_first(shared, index, weight, boundary, forward, backward):
+def couple_first(shared, index, weight, boundary, odd, even):
     section = lax.axis_index("sec")
     table = [shared[s, r : r + 1, :] for s in range(shared.shape[0]) for r in range(48, 52)]
     own_boundary(
         table, index, weight, lambda j: shared[section, 48 + j : 49 + j, :], boundary
     )
-    for out, source, start in zip((forward, backward), edge_sources(), (HALO, 0)):
+    for out, (source, start) in zip((odd, even), sent_edges()):
         for i in range(3):
-            row = 2 * HALO * i + start
-            out[HALO * i : HALO * (i + 1), :] = shared[source, row : row + HALO, :]
+            row = pl.multiple_of(2 * HALO * i + start, HALO)
+            out[HALO * i : HALO * (i + 1), :] = shared[source, pl.ds(row, HALO), :]
         edge = edge_boundary(
             table, shared, shared[source, 48:49, :], shared[source, 51:52, :], source
         )
         out[24:32, :] = jnp.broadcast_to(edge, (8, LANES))
 
 
-def couple_second(surfaces, shared, index, weight, boundary, forward, backward):
+def couple_second(surfaces, shared, index, weight, boundary, odd, even):
     section = lax.axis_index("sec")
     table = [surfaces[s, r : r + 1, :] for s in range(surfaces.shape[0]) for r in range(4)]
     own_boundary(
         table, index, weight, lambda j: surfaces[section, j : j + 1, :], boundary
     )
-    for out, source in zip((forward, backward), edge_sources()):
+    for out, (source, _) in zip((odd, even), sent_edges()):
         edge = edge_boundary(
             table, shared, surfaces[source, 0:1, :], surfaces[source, 3:4, :], source
         )
@@ -211,17 +230,17 @@
 
 
 def step_first(
-    state, tendency, diffusion, left, response, alive, hits, boundary, low, high,
+    state, tendency, diffusion, left, response, alive, hits, boundary, odd, even,
     window, rates_out, forcing_out, surface, parcel,
 ):
     rates = jnp.concatenate(
-        [diffusion[...].astype(f32), edge_block(low[8:16, :], high[8:16, :])], axis=1
+        [diffusion[...].astype(f32), edge_block(*sides(odd, even, 8, 8))], axis=1
     )
     tend = jnp.concatenate(
-        [tendency[...].astype(f32), edge_block(low[16:24, :], high[16:24, :])], axis=1
-    )
-    field = jnp.concatenate([state[...], edge_block(low[0:8, :], high[0:8, :])], axis=1)
-    edge = edge_row(low[24:25, :], high[24:25, :])
+        [tendency[...].astype(f32), edge_block(*sides(odd, even, 16, 8))], axis=1
+    )
+    field = jnp.concatenate([state[...], edge_block(*sides(odd, even, 0, 8))], axis=1)
+    edge = edge_row(*sides(odd, even, 24, 1))
     constant = forcing(response[...], boundary, edge, tend)
     rates_out[...] = rates
     forcing_out[...] = tend
@@ -235,10 +254,10 @@
 
 
 def step_second(
-    window, rates, tend, left, response, alive, hits, boundary, low, high, earlier,
+    window, rates, tend, left, response, alive, hits, boundary, odd, even, earlier,
     final, parcels,
 ):
-    edge = edge_row(low[0:1, :], high[0:1, :])
+    edge = edge_row(*sides(odd, even, 0, 1))
     constant = forcing(response[...], boundary, edge, tend[...])
     field = advance(window[...], rates[...], constant, left[...], alive)
     final[...] = field[:, : final.shape[1]]
@@ -331,13 +350,12 @@
     rows, heights = observed.shape[1:]
     width = columns + LANES
     half = sections // 2
-    forward = []
+    swaps = ([], [])
     for s in range(sections):
         for t in range(tiles):
-            seam = t == tiles - 1
-            target = ((s + half) % sections if seam else s) * tiles + (t + 1) % tiles
-            forward.append((s * tiles + t, target))
-    backward = [(target, source) for source, target in forward]
+            target = ((s + half) % sections if t == tiles - 1 else s) * tiles + (t + 1) % tiles
+            swaps[t % 2].extend([(s * tiles + t, target), (target, s * tiles + t)])
+    above_even, above_odd = swaps
     listed = jnp.transpose(send_cols[:, 0, 0], (0, 2, 1))
     index, weight = remap_index[0], remap_weight[0]
     shape = jax.ShapeDtypeStruct
@@ -361,13 +379,13 @@
         ],
     )
     shared = lax.all_gather(edges, "sec", axis=0, tiled=False)
-    boundary, up, down = call(
+    boundary, odd, even = call(
         couple_first,
         (shape((1, columns), f32), shape((32, LANES), f32), shape((32, LANES), f32)),
         shared, index, weight,
     )
-    low = lax.ppermute(up, AXES, forward)
-    high = lax.ppermute(down, AXES, backward)
+    odd = lax.ppermute(odd, AXES, above_odd)
+    even = lax.ppermute(even, AXES, above_even)
     mixing_row, _ = after((mixing[0], boundary))
     left, response, alive, hits = call(
         ready_first,
@@ -388,16 +406,16 @@
             shape((4, LANES), f32),
             shape((4, tiles, levels), f32),
         ),
-        state[0], tendency[0], diffusion[0], left, response, alive, hits, boundary, low, high,
+        state[0], tendency[0], diffusion[0], left, response, alive, hits, boundary, odd, even,
     )
     surfaces = lax.all_gather(surface, "sec", axis=0, tiled=False)
-    boundary, up, down = call(
+    boundary, odd, even = call(
         couple_second,
         (shape((1, columns), f32), shape((8, LANES), f32), shape((8, LANES), f32)),
         surfaces, shared, index, weight,
     )
-    low = lax.ppermute(up, AXES, forward)
-    high = lax.ppermute(down, AXES, backward)
+    odd = lax.ppermute(odd, AXES, above_odd)
+    even = lax.ppermute(even, AXES, above_even)
     weights, _ = after((occ_weight[:, 0], boundary))
     hits, spread, right, right_abel = call(
         ready_second,
@@ -412,11 +430,9 @@
     final, parcels = call(
         step_second,
         (shape((levels, columns), f32), shape((8 * tiles, levels), f32)),
-        window, rates, tend, left, response, alive, hits, boundary, low, high, parcel,
-    )
-    parcels, spread, right, right_abel, observed = after(
-        (parcels, spread, right, right_abel, observed)
-    )
+        window, rates, tend, left, response, alive, hits, boundary, odd, even, parcel,
+    )
+    parcels, spread, right, right_abel = after((parcels, spread, right, right_abel))
     arrived = lax.all_to_all(
         parcels.reshape(tiles, 8, levels), "tile", split_axis=0, concat_axis=0, tiled=True
     )

time: 134 us -> 131 us (0.978)
  starting transfers between devices: 23.9 us -> 19.7 us
  waiting for transfers between devices: 0.01 us -> 2.93 us
  blocking collectives: 99.5 us -> 97.4 us
    all_to_all x1, blocking collectives: 43 us -> 37.5 us  [shards(): lax.all_to_all(parcels.reshape(tiles, 8, levels), 'tile', split_axis=0, c...]
    ppermute x4, starting transfers between devices: 23.9 us -> 19.7 us  [the longest x2 15.9 us: shards(): odd = lax.ppermute(odd, AXES, above_odd)]
    ppermute x4, waiting for transfers between devices: 0.01 us -> 2.93 us  [the longest x2 1.71 us: shards(): even = lax.ppermute(even, AXES, above_even)]
    all_to_all x1, blocking collectives: 20.8 us -> 23.5 us  [shards(): lax.all_to_all(partial, 'sec', split_axis=0, concat_axis=0, tiled=True)]
  transfers between devices with their start and end apart: 4 -> 4, of which waited for: 0 -> 2; matrix products, arithmetic and copies ran while one was open for 0% -> 0% of each run, Pallas kernels for 1% -> 1%
where the time goes in v3:
time: 131 us
  blocking collectives  97.4 us (74%)
  starting transfers between devices  19.7 us (15%)
  Pallas kernels  8.97 us (7%)
  waiting for transfers between devices  2.93 us (2%)
    all_to_all x1, blocking collectives, shards(): lax.all_to_all(parcels.reshape(tiles, 8, levels), 'tile', split_axis=0, c...  37.5 us
    all_to_all x1, blocking collectives, shards(): lax.all_to_all(partial, 'sec', split_axis=0, concat_axis=0, tiled=True)  23.5 us
    all_gather x1, blocking collectives, shards(): shared = lax.all_gather(edges, 'sec', axis=0, tiled=False)  21 us
    ppermute x2, starting transfers between devices, shards(): odd = lax.ppermute(odd, AXES, above_odd)  15.9 us
    all_gather x1, blocking collectives, shards(): surfaces = lax.all_gather(surface, 'sec', axis=0, tiled=False)  15.4 us
    pallas_call x9, Pallas kernels, call(): pl.pallas_call(body, out_shape=outs if single else tuple(outs), in_specs=...  8.97 us
    ppermute x2, starting transfers between devices, shards(): even = lax.ppermute(even, AXES, above_even)  3.84 us
  transfers between devices with their start and end apart: 4, of which 2 were waited for; matrix products, arithmetic and copies ran while one was open for 0% of the time, Pallas kernels for 1%

profile of v3, /device:TPU:1, one launch (start us, length us, event | category | flops | bytes accessed | tf_op | source)
XLA Modules:
  0.0 130.7 jit_solution(13535337063133623847)
XLA Ops:
  0.6 0.0 copy-start.4
  0.6 0.0 copy-start.5
  0.7 0.0 copy-start.6
  0.7 0.0 copy-start.2
  0.7 1.2 shard_map.158
  1.9 0.0 copy-start.9
  1.9 0.0 copy-start.13
  1.9 0.0 copy-start.14
  2.0 0.0 copy-start
  2.0 21.0 %all-gather = f32[256,128]{1,0:T(8,128)S(1)} all-gather(f32[64,128]{1,0:T(8,128)S(1)} %shard_map.158), channel_id=2, replica_groups=mesh['sec'=4,'tile'=128] {'sec'}, dimensions={0}, use_global_device_ids=true | all-gather | bytes 163840 | tf_op jit(solution)/shard_map/all_gather | solution.py:381
  22.9 0.0 copy-start.1
  23.0 0.0 copy-done.4
  23.0 0.0 copy-done.5
  23.0 0.2 shard_map.159
  23.2 10.7 %collective-permute-start = (f32[32,128]{1,0:T(8,128)S(1)}, f32[32,128]{1,0:T(8,128)S(1)}, u32[]{:S(2)}, u32[]{:S(2)}) collective-permute-start(f32[32,128]{1,0:T(8,128)S(1)} %get-tuple-element.35), channel_id=1, source_target_pairs={{1,2},{2,1},{3,4},{4,3},{5,6},{6,5},{7,8},{8,7},{9,10},{10,9},{11,... | collective-permute-start | bytes 49160 | tf_op jit(solution)/shard_map/ppermute | solution.py:387
  33.9 1.9 %collective-permute-start.1 = (f32[32,128]{1,0:T(8,128)S(1)}, f32[32,128]{1,0:T(8,128)S(1)}, u32[]{:S(2)}, u32[]{:S(2)}) collective-permute-start(f32[32,128]{1,0:T(8,128)S(1)} %get-tuple-element.36), channel_id=1, source_target_pairs={{0,1},{1,0},{2,3},{3,2},{4,5},{5,4},{6,7},{7,6},{8,9},{9,8},{10,11... | collective-permute-start | bytes 49160 | tf_op jit(solution)/shard_map/ppermute | solution.py:388
  35.8 0.0 copy-done.6
  35.9 0.0 copy-done.9
  35.9 0.0 copy-done.13
  35.9 0.0 copy-done.14
  35.9 0.8 shard_map.160
  36.7 0.0 collective-permute-done.odd
  36.7 1.7 %collective-permute-done.1.even = f32[32,128]{1,0:T(8,128)S(1)} collective-permute-done((f32[32,128]{1,0:T(8,128)S(1)}, f32[32,128]{1,0:T(8,128)S(1)}, u32[]{:S(2)}, u32[]{:S(2)}) %collective-permute-start.1) | collective-permute-done | bytes 16416 | tf_op jit(solution)/shard_map/ppermute | solution.py:388
  38.4 0.0 copy-done.2
  38.4 0.0 copy-done
  38.4 0.0 copy-done.1
  38.4 0.0 copy-start.7
  38.4 2.1 %shard_map.161 = (f32[128,640]{1,0:T(8,128)S(1)}, f32[128,640]{1,0:T(8,128)S(1)}, f32[128,640]{1,0:T(8,128)S(1)}, f32[4,128]{1,0:T(4,128)S(1)}, f32[4,128,128]{2,1,0:T(8,128)S(1)}) custom-call(f32[128,512]{1,0:T(8,128)S(1)} %bitcast.22, bf16[128,512]{1,0:T(8,128)(2,1)S(1)} %bitcast.25, bf16[128,512]{1,0:T(8,128)(2,1)S(1)} %bitcast.27, ...), custom_call_target="tpu_custom_call" | custom-call | tf_op jit(solution)/shard_map/pallas_call | solution.py:23
  40.5 0.0 copy-start.3
  40.5 15.4 %all-gather.2.surfaces = f32[4,4,128]{2,1,0:T(4,128)S(1)} all-gather(f32[1,4,128]{2,1,0:T(4,128)S(1)} %bitcast.40), channel_id=3, replica_groups=mesh['sec'=4,'tile'=128] {'sec'}, dimensions={0}, use_global_device_ids=true | all-gather | bytes 10240 | tf_op jit(solution)/shard_map/all_gather | solution.py:411
  55.9 0.0 copy-start.11
  55.9 0.2 shard_map.162
  56.1 0.0 copy-start.10
  56.1 5.2 %collective-permute-start.2 = (f32[8,128]{1,0:T(8,128)S(1)}, f32[8,128]{1,0:T(8,128)S(1)}, u32[]{:S(2)}, u32[]{:S(2)}) collective-permute-start(f32[8,128]{1,0:T(8,128)S(1)} %get-tuple-element.44), channel_id=1, source_target_pairs={{1,2},{2,1},{3,4},{4,3},{5,6},{6,5},{7,8},{8,7},{9,10},{10,9},{11,... | collective-permute-start | bytes 12296 | tf_op jit(solution)/shard_map/ppermute | solution.py:417
  61.3 1.9 %collective-permute-start.3 = (f32[8,128]{1,0:T(8,128)S(1)}, f32[8,128]{1,0:T(8,128)S(1)}, u32[]{:S(2)}, u32[]{:S(2)}) collective-permute-start(f32[8,128]{1,0:T(8,128)S(1)} %get-tuple-element.45), channel_id=1, source_target_pairs={{0,1},{1,0},{2,3},{3,2},{4,5},{5,4},{6,7},{7,6},{8,9},{9,8},{10,11... | collective-permute-start | bytes 12296 | tf_op jit(solution)/shard_map/ppermute | solution.py:418
  63.2 0.0 copy-start.12
  63.2 0.0 copy-done.7
  63.2 0.0 copy-done.3
  63.2 0.0 copy-done.11
  63.2 0.0 copy-done.10
  63.3 0.6 copy-done.12
  63.9 0.8 shard_map.163
  64.7 1.2 collective-permute-done.2.odd
  65.9 0.0 collective-permute-done.3.even
  65.9 2.5 %shard_map.164 = (f32[128,512]{1,0:T(8,128)}, f32[1024,128]{1,0:T(8,128)S(1)}) custom-call(f32[128,640]{1,0:T(8,128)S(1)} %get-tuple-element.37.window, f32[128,640]{1,0:T(8,128)S(1)} %get-tuple-element.38.rates, f32[128,640]{1,0:T(8,128)S(1)} %get-tuple-element.39.tend, bf16[128,384]{1,0:T(8,128)(2,1)S(1)} %get-tuple-element.31.left, ...), custom_call_target="tpu_custom_call" | custom-call | tf_op jit(solution)/shard_map/pallas_call | solution.py:23
  68.4 37.5 %all_to_all.10 = f32[128,8,128]{2,1,0:T(8,128)S(1)} all-to-all(f32[128,8,128]{2,1,0:T(8,128)S(1)} %bitcast.23), channel_id=1, replica_groups=mesh['sec'=4,'tile'=128] {'tile'}, dimensions={0} | all-to-all | bytes 1048576 | tf_op jit(solution)/shard_map/all_to_all | solution.py:436
  105.9 0.4 shard_map.165
  106.3 0.0 copy-start.8
  106.4 23.5 %all_to_all.11.received = f32[4,32,128]{2,1,0:T(8,128)S(1)} all-to-all(f32[4,32,128]{2,1,0:T(8,128)S(1)} %shard_map.165), channel_id=1, replica_groups=mesh['sec'=4,'tile'=128] {'sec'}, dimensions={0} | all-to-all | bytes 131072 | tf_op jit(solution)/shard_map/all_to_all | solution.py:444
  129.9 0.0 copy-done.8
  129.9 0.8 shard_map.166
Async XLA Ops:
  0.6 22.3 %copy-start.4 = (s32[1,4,512]{2,1,0:T(4,128)S(1)}, s32[1,4,512]{2,1,0:T(4,128)}, u32[]{:S(2)}) copy-start(s32[1,4,512]{2,1,0:T(4,128)} %param.20) | copy-start | bytes 24580
  0.6 22.3 %copy-start.5 = (f32[1,4,512]{2,1,0:T(4,128)S(1)}, f32[1,4,512]{2,1,0:T(4,128)}, u32[]{:S(2)}) copy-start(f32[1,4,512]{2,1,0:T(4,128)} %param.21) | copy-start | bytes 24580
  0.7 35.2 %copy-start.6 = (f32[1,128,128]{2,1,0:T(8,128)S(1)}, f32[1,128,128]{2,1,0:T(8,128)}, u32[]{:S(2)}) copy-start(f32[1,128,128]{2,1,0:T(8,128)} %param.18) | copy-start | bytes 196612
  0.7 37.7 %copy-start.2 = (bf16[1,128,512]{2,1,0:T(8,128)(2,1)S(1)}, bf16[1,128,512]{2,1,0:T(8,128)(2,1)}, u32[]{:S(2)}) copy-start(bf16[1,128,512]{2,1,0:T(8,128)(2,1)} %param.17) | copy-start | bytes 393220
  1.9 33.9 %copy-start.9 = (s32[2,1,1,128,4]{3,4,2,1,0:T(4,128)S(1)}, s32[2,1,1,128,4]{3,4,2,1,0:T(4,128)}, u32[]{:S(2)}) copy-start(s32[2,1,1,128,4]{3,4,2,1,0:T(4,128)} %param.23) | copy-start | bytes 12292
  1.9 33.9 %copy-start.13 = (s32[4]{0:T(128)S(1)}, s32[4]{0:T(128)}, u32[]{:S(2)}) copy-start(s32[4]{0:T(128)} %active.1) | copy-start | bytes 52
  1.9 33.9 %copy-start.14 = (f32[1,128]{1,0:T(1,128)S(1)}, f32[1,128]{1,0:T(1,128)}, u32[]{:S(2)}) copy-start(f32[1,128]{1,0:T(1,128)} %coupling.1) | copy-start | bytes 1540
  2.0 36.5 %copy-start = (f32[1,128,512]{2,1,0:T(8,128)S(1)}, f32[1,128,512]{2,1,0:T(8,128)}, u32[]{:S(2)}) copy-start(f32[1,128,512]{2,1,0:T(8,128)} %param.15) | copy-start | bytes 786436
  22.9 15.5 %copy-start.1 = (bf16[1,128,512]{2,1,0:T(8,128)(2,1)S(1)}, bf16[1,128,512]{2,1,0:T(8,128)(2,1)}, u32[]{:S(2)}) copy-start(bf16[1,128,512]{2,1,0:T(8,128)(2,1)} %param.16) | copy-start | bytes 393220
  23.2 13.5 %collective-permute-start = (f32[32,128]{1,0:T(8,128)S(1)}, f32[32,128]{1,0:T(8,128)S(1)}, u32[]{:S(2)}, u32[]{:S(2)}) collective-permute-start(f32[32,128]{1,0:T(8,128)S(1)} %get-tuple-element.35), channel_id=1, source_target_pairs={{1,2},{2,1},{3,4},{4,3},{5,6},{6,5},{7,8},{8,7},{9,10},{10,9},{11,... | collective-permute-start | bytes 49160 | tf_op jit(solution)/shard_map/ppermute | solution.py:387
  33.9 4.5 %collective-permute-start.1 = (f32[32,128]{1,0:T(8,128)S(1)}, f32[32,128]{1,0:T(8,128)S(1)}, u32[]{:S(2)}, u32[]{:S(2)}) collective-permute-start(f32[32,128]{1,0:T(8,128)S(1)} %get-tuple-element.36), channel_id=1, source_target_pairs={{0,1},{1,0},{2,3},{3,2},{4,5},{5,4},{6,7},{7,6},{8,9},{9,8},{10,11... | collective-permute-start | bytes 49160 | tf_op jit(solution)/shard_map/ppermute | solution.py:388
  38.4 24.8 %copy-start.7 = (f32[1,128,128]{2,1,0:T(8,128)S(1)}, f32[1,128,128]{2,1,0:T(8,128)}, u32[]{:S(2)}) copy-start(f32[1,128,128]{2,1,0:T(8,128)} %param.27) | copy-start | bytes 196612
  40.5 22.7 %copy-start.3 = (f32[128,256]{1,0:T(8,128)S(1)}, f32[128,256]{1,0:T(8,128)}, u32[]{:S(2)}) copy-start(f32[128,256]{1,0:T(8,128)} %abel.1) | copy-start | bytes 393220
  55.9 7.3 %copy-start.11 = (f32[2,1,8,64]{3,2,1,0:T(8,128)S(1)}, f32[2,1,8,64]{3,2,1,0:T(8,128)}, u32[]{:S(2)}) copy-start(f32[2,1,8,64]{3,2,1,0:T(8,128)} %param.25) | copy-start | bytes 12292
  56.1 7.1 %copy-start.10 = (s32[2,1,8,64]{3,2,1,0:T(8,128)S(1)}, s32[2,1,8,64]{3,2,1,0:T(8,128)}, u32[]{:S(2)}) copy-start(s32[2,1,8,64]{3,2,1,0:T(8,128)} %param.24) | copy-start | bytes 12292
  56.1 9.8 %collective-permute-start.2 = (f32[8,128]{1,0:T(8,128)S(1)}, f32[8,128]{1,0:T(8,128)S(1)}, u32[]{:S(2)}, u32[]{:S(2)}) collective-permute-start(f32[8,128]{1,0:T(8,128)S(1)} %get-tuple-element.44), channel_id=1, source_target_pairs={{1,2},{2,1},{3,4},{4,3},{5,6},{6,5},{7,8},{8,7},{9,10},{10,9},{11,... | collective-permute-start | bytes 12296 | tf_op jit(solution)/shard_map/ppermute | solution.py:417
  61.3 4.6 %collective-permute-start.3 = (f32[8,128]{1,0:T(8,128)S(1)}, f32[8,128]{1,0:T(8,128)S(1)}, u32[]{:S(2)}, u32[]{:S(2)}) collective-permute-start(f32[8,128]{1,0:T(8,128)S(1)} %get-tuple-element.45), channel_id=1, source_target_pairs={{0,1},{1,0},{2,3},{3,2},{4,5},{5,4},{6,7},{7,6},{8,9},{9,8},{10,11... | collective-permute-start | bytes 12296 | tf_op jit(solution)/shard_map/ppermute | solution.py:418
  63.2 0.7 copy-start.12
  106.3 23.5 %copy-start.8 = (f32[2,16,256]{2,1,0:T(8,128)S(1)}, f32[2,16,256]{2,1,0:T(8,128)}, u32[]{:S(2)}) copy-start(f32[2,16,256]{2,1,0:T(8,128)} %observed.1) | copy-start | bytes 98308

commit v4 on v3

--- a/solution.py
+++ b/solution.py
@@ -7,6 +7,7 @@
 
 SUBS = 4
 STEPS = 2
+PARTS = 2
 HALO = 8
 LANES = 128
 AXES = ("sec", "tile")
@@ -261,15 +262,26 @@
     constant = forcing(response[...], boundary, edge, tend[...])
     field = advance(window[...], rates[...], constant, left[...], alive)
     final[...] = field[:, : final.shape[1]]
-    slots = earlier.shape[0]
-    tiles = earlier.shape[1]
-    for m in range(slots):
-        parcels[pl.ds(m, tiles, stride=2 * slots), :] = earlier[m]
-    for m, rows in enumerate(chosen(field, hits)):
-        parcels[pl.ds(slots + m, tiles, stride=2 * slots), :] = rows
-
-
-def ready_first(active, mixing, coupling, listed, left, response, alive, hits):
+    slots, tiles, _ = earlier.shape
+    part = tiles // PARTS
+    width = PARTS * STEPS * slots
+    for m, later in enumerate(chosen(field, hits)):
+        for o in range(PARTS):
+            for p, rows in enumerate((earlier[m], later)):
+                first = (o * STEPS + p) * slots + m
+                owned = rows[o * part : (o + 1) * part]
+                parcels[pl.ds(first, part, stride=width), :] = owned
+
+
+def ready_first(
+    active, mixing, coupling, listed, slots, weights, counts, left, response, alive, hits, lists
+):
+    steps, ranks, occultations = slots.shape
+    for p in range(steps):
+        rank = lax.broadcasted_iota(jnp.int32, (ranks, occultations), 0)
+        lists[p * ranks : (p + 1) * ranks, :] = slots[p].astype(f32)
+        live = jnp.where(rank < counts[p : p + 1, :], weights[p], 0.0)
+        lists[(steps + p) * ranks : (steps + p + 1) * ranks, :] = live
     width = alive.shape[1]
     lane = lane_ids((1, width))
     column = jnp.where(lane < width - LANES, lane, lane - (width - LANES))
@@ -280,41 +292,59 @@
     hits[...] = one_hot(listed[0], hits.shape[0])
 
 
-def ready_second(listed, slots, weights, counts, refraction, abel, hits, spread, right, right_abel):
+def ready_second(listed, lists, mirrored, refraction, abel, hits, spread, right, right_abel):
     hits[...] = one_hot(listed[1], hits.shape[0])
     right[...] = right_operand(refraction[...])
     right_abel[...] = right_operand(abel[...])
-    steps, ranks, occultations = slots.shape
-    width = spread.shape[2] // 3
-    tiles = width // 4
-    for p in range(steps):
-        rank = lax.broadcasted_iota(jnp.int32, (ranks, occultations), 0)
-        live = jnp.where(rank < counts[p : p + 1, :], weights[p], 0.0).T
-        key = ((slots[p] & 3) * tiles + (slots[p] >> 2)).T
-        place = lane_ids((occultations, width))
-        total = jnp.zeros((occultations, width), f32)
-        for k in range(ranks):
-            total = total + jnp.where(key[:, k : k + 1] == place, live[:, k : k + 1], 0.0)
-        spread[p] = left_operand(total)
-
-
-def project(arrived, spread, refraction, out):
-    steps, occultations, width = spread.shape
-    tiles = width // 12
-    owners = out.shape[0]
-    rows = occultations // owners
+    occultations, width = spread.shape[2], spread.shape[3] // 3
+    ranks = lists.shape[0] // (2 * STEPS)
+    part = width // 4
+    here = jnp.where(lax.axis_index("tile") >= part, 1, 0)
+    place = lane_ids((occultations, width))
+    for o in range(PARTS):
+        owned = jnp.where(here == o, lists[...], mirrored[...])
+        for p in range(STEPS):
+            slot = owned[p * ranks : (p + 1) * ranks].astype(jnp.int32)
+            live = owned[(STEPS + p) * ranks : (STEPS + p + 1) * ranks].T
+            source = (slot >> 2) - here * part
+            inside = (source >= 0) & (source < part)
+            key = jnp.where(inside, (slot & 3) * part + source, -1).T
+            total = jnp.zeros((occultations, width), f32)
+            for k in range(ranks):
+                hit = key[:, k : k + 1] == place
+                total = total + jnp.where(hit, live[:, k : k + 1], 0.0)
+            spread[o, p] = left_operand(total)
+
+
+def project(arrived, spread, refraction, kept, sent):
+    occultations, width = spread.shape[2:]
+    part = width // 12
     profiles = []
-    for p in range(steps):
-        values = jnp.concatenate(
-            [arrived[pl.ds(4 * p + m, tiles, stride=4 * steps), :] for m in range(4)], axis=0
-        )
-        profiles.append(matmul(spread[p], right_operand(values)))
+    for o in range(PARTS):
+        for p in range(STEPS):
+            first = 4 * (o * STEPS + p)
+            values = jnp.concatenate(
+                [
+                    arrived[pl.ds(first + m, part, stride=4 * PARTS * STEPS), :]
+                    for m in range(4)
+                ],
+                axis=0,
+            )
+            profiles.append(matmul(spread[o, p], right_operand(values)))
     profile = jnp.concatenate(profiles, axis=0)
     projected = matmul(left_operand(profile), refraction[...])
-    for p in range(steps):
-        for q in range(owners):
-            start = p * occultations + q * rows
-            out[q, p * rows : (p + 1) * rows, :] = projected[start : start + rows, :]
+    pairs = kept.shape[0] // PARTS
+    rows = occultations // (2 * pairs)
+    first_core = lax.rem(lax.axis_index("sec"), 2) == 0
+    for o in range(PARTS):
+        for p in range(STEPS):
+            for pair in range(pairs):
+                start = (o * STEPS + p) * occultations + 2 * pair * rows
+                low = projected[start : start + rows]
+                high = projected[start + rows : start + 2 * rows]
+                target = (pair * PARTS + o, slice(p * rows, (p + 1) * rows))
+                kept[target] = jnp.where(first_core, low, high)
+                sent[target] = jnp.where(first_core, high, low)
 
 
 def depart(received, abel, observed, out):
@@ -350,6 +380,8 @@
     rows, heights = observed.shape[1:]
     width = columns + LANES
     half = sections // 2
+    part = tiles // PARTS
+    ranks, owned = occ_slot.shape[2:]
     swaps = ([], [])
     for s in range(sections):
         for t in range(tiles):
@@ -387,15 +419,19 @@
     odd = lax.ppermute(odd, AXES, above_odd)
     even = lax.ppermute(even, AXES, above_even)
     mixing_row, _ = after((mixing[0], boundary))
-    left, response, alive, hits = call(
+    left, response, alive, hits, lists = call(
         ready_first,
         (
             shape((levels, 3 * levels), bf16),
             shape((levels, LANES), f32),
             shape((1, width), f32),
             shape((columns, 4 * tiles), bf16),
+            shape((2 * STEPS * ranks, owned), f32),
         ),
-        active_cols, mixing_row, coupling, listed,
+        active_cols, mixing_row, coupling, listed, occ_slot[:, 0], occ_weight[:, 0], occ_count[:, 0],
+    )
+    mirrored = lax.ppermute(
+        lists, "tile", [(t, (t + part) % tiles) for t in range(tiles)]
     )
     window, rates, tend, surface, parcel = call(
         step_first,
@@ -416,16 +452,16 @@
     )
     odd = lax.ppermute(odd, AXES, above_odd)
     even = lax.ppermute(even, AXES, above_even)
-    weights, _ = after((occ_weight[:, 0], boundary))
+    mirrored, _ = after((mirrored, boundary))
     hits, spread, right, right_abel = call(
         ready_second,
         (
             shape((columns, 4 * tiles), bf16),
-            shape((STEPS, occ_slot.shape[3], 12 * tiles), bf16),
+            shape((PARTS, STEPS, owned, 12 * part), bf16),
             shape((3 * levels, levels), bf16),
             shape((3 * levels, heights), bf16),
         ),
-        listed, occ_slot[:, 0], weights, occ_count[:, 0], refraction[0], abel_matrix,
+        listed, lists, mirrored, refraction[0], abel_matrix,
     )
     final, parcels = call(
         step_second,
@@ -434,14 +470,30 @@
     )
     parcels, spread, right, right_abel = after((parcels, spread, right, right_abel))
     arrived = lax.all_to_all(
-        parcels.reshape(tiles, 8, levels), "tile", split_axis=0, concat_axis=0, tiled=True
-    )
-    partial = call(
-        project,
-        shape((sections, STEPS * rows, levels), f32),
-        arrived.reshape(8 * tiles, levels), spread, right,
-    )
-    received = lax.all_to_all(partial, "sec", split_axis=0, concat_axis=0, tiled=True)
+        parcels.reshape(part, 8 * PARTS, levels),
+        "tile",
+        split_axis=0,
+        concat_axis=0,
+        axis_index_groups=[[o * part + i for i in range(part)] for o in range(PARTS)],
+        tiled=True,
+    )
+    block = shape((half * PARTS, STEPS * rows, levels), f32)
+    kept, sent = call(
+        project, (block, block), arrived.reshape(8 * PARTS * part, levels), spread, right
+    )
+    got = lax.ppermute(sent, "sec", [(s, s ^ 1) for s in range(sections)])
+    received = lax.all_to_all(
+        kept + got,
+        AXES,
+        split_axis=0,
+        concat_axis=0,
+        axis_index_groups=[
+            [(2 * z + core) * tiles + o * part + i for z in range(half) for o in range(PARTS)]
+            for core in range(2)
+            for i in range(part)
+        ],
+        tiled=True,
+    )
     departures = call(
         depart, shape((STEPS, rows, heights), f32), received, right_abel, observed
     )

time: 131 us -> 117 us (0.89)
  blocking collectives: 97.4 us -> 76.2 us
  starting transfers between devices: 19.7 us -> 27.2 us
    all_to_all x2, blocking collectives: 61 us -> 40.1 us  [the longest x1 23.2 us: shards(): lax.all_to_all(parcels.reshape(part, 8 * PARTS, levels), 'tile', split_ax...]
    ppermute x0 -> x2, starting transfers between devices: none -> 7.14 us  [the longest x1 5.22 us: shards(): got = lax.ppermute(sent, 'sec', [(s, s ^ 1) for s in range(sections)])]
    ppermute x2, waiting for transfers between devices: 1.71 us -> 0.31 us  [shards(): even = lax.ppermute(even, AXES, above_even)]
  transfers between devices with their start and end apart: 4 -> 6, of which waited for: 2 -> 3; matrix products, arithmetic and copies ran while one was open for 0% -> 0% of each run, Pallas kernels for 1% -> 4%
where the time goes in v4:
time: 117 us; the launch traced here: 116 us
  blocking collectives  76.2 us (65%)
  starting transfers between devices  27.2 us (23%)
  Pallas kernels  9.23 us (8%)
  waiting for transfers between devices  2.53 us (2%)
    all_to_all x1, blocking collectives, shards(): lax.all_to_all(parcels.reshape(part, 8 * PARTS, levels), 'tile', split_ax...  23.2 us
    all_gather x1, blocking collectives, shards(): shared = lax.all_gather(edges, 'sec', axis=0, tiled=False)  21 us
    all_to_all x1, blocking collectives, shards(): lax.all_to_all(kept + got, AXES, split_axis=0, concat_axis=0, axis_index_...  16.9 us
    ppermute x2, starting transfers between devices, shards(): odd = lax.ppermute(odd, AXES, above_odd)  16.2 us
    all_gather x1, blocking collectives, shards(): surfaces = lax.all_gather(surface, 'sec', axis=0, tiled=False)  15.1 us
    pallas_call x9, Pallas kernels, call(): pl.pallas_call(body, out_shape=outs if single else tuple(outs), in_specs=...  9.23 us
    ppermute x1, starting transfers between devices, shards(): got = lax.ppermute(sent, 'sec', [(s, s ^ 1) for s in range(sections)])  5.22 us
    ppermute x2, starting transfers between devices, shards(): even = lax.ppermute(even, AXES, above_even)  3.84 us
  transfers between devices with their start and end apart: 6, of which 3 were waited for; matrix products, arithmetic and copies ran while one was open for 0% of the time, Pallas kernels for 4%

profile of v4, /device:TPU:1, one launch (start us, length us, event | category | flops | bytes accessed | tf_op | source)
XLA Modules:
  0.0 116.1 jit_solution(939325924221314019)
XLA Ops:
  0.6 0.0 copy-start.4
  0.6 0.0 copy-start.5
  0.7 0.0 copy-start.7
  0.7 0.0 copy-start.2
  0.7 1.2 %shard_map.158 = f32[64,128]{1,0:T(8,128)S(1)} custom-call(f32[128,512]{1,0:T(8,128)} %bitcast.21, bf16[128,512]{1,0:T(8,128)(2,1)} %bitcast.24, bf16[128,512]{1,0:T(8,128)(2,1)} %bitcast.26, s32[4,512]{1,0:T(4,128)} %bitcast.28, f32[4,512]{1,0:T(4,128)} %bitcast.31), custom_call_target="tpu_custom_call" | custom-call | tf_op jit(solution)/shard_map/pallas_call | solution.py:24
  1.9 0.0 copy-start.9
  1.9 0.0 copy-start.10
  1.9 0.0 copy-start.11
  2.0 0.0 copy-start.12
  2.0 0.0 copy-start.13
  2.0 0.0 copy-start.14
  2.0 0.0 copy-start
  2.0 21.0 %all-gather = f32[256,128]{1,0:T(8,128)S(1)} all-gather(f32[64,128]{1,0:T(8,128)S(1)} %shard_map.158), channel_id=2, replica_groups=mesh['sec'=4,'tile'=128] {'sec'}, dimensions={0}, use_global_device_ids=true | all-gather | bytes 163840 | tf_op jit(solution)/shard_map/all_gather | solution.py:413
  23.0 0.0 copy-start.1
  23.0 0.0 copy-done.4
  23.0 0.0 copy-done.5
  23.0 0.2 shard_map.159
  23.2 10.7 %collective-permute-start = (f32[32,128]{1,0:T(8,128)S(1)}, f32[32,128]{1,0:T(8,128)S(1)}, u32[]{:S(2)}, u32[]{:S(2)}) collective-permute-start(f32[32,128]{1,0:T(8,128)S(1)} %get-tuple-element.38), channel_id=1, source_target_pairs={{1,2},{2,1},{3,4},{4,3},{5,6},{6,5},{7,8},{8,7},{9,10},{10,9},{11,... | collective-permute-start | bytes 49160 | tf_op jit(solution)/shard_map/ppermute | solution.py:419
  34.0 1.9 %collective-permute-start.1 = (f32[32,128]{1,0:T(8,128)S(1)}, f32[32,128]{1,0:T(8,128)S(1)}, u32[]{:S(2)}, u32[]{:S(2)}) collective-permute-start(f32[32,128]{1,0:T(8,128)S(1)} %get-tuple-element.39), channel_id=1, source_target_pairs={{0,1},{1,0},{2,3},{3,2},{4,5},{5,4},{6,7},{7,6},{8,9},{9,8},{10,11... | collective-permute-start | bytes 49160 | tf_op jit(solution)/shard_map/ppermute | solution.py:420
  35.9 0.0 copy-done.7
  35.9 0.0 copy-done.9
  35.9 0.0 copy-done.10
  35.9 0.0 copy-done.11
  35.9 0.0 copy-done.12
  35.9 0.0 copy-done.13
  35.9 0.0 copy-done.14
  36.0 0.8 shard_map.160
  36.8 1.9 %collective-permute-start.2 = (f32[32,64]{1,0:T(8,128)S(1)}, f32[32,64]{1,0:T(8,128)S(1)}, u32[]{:S(2)}, u32[]{:S(2)}) collective-permute-start(f32[32,64]{1,0:T(8,128)S(1)} %get-tuple-element.43.lists), channel_id=1, source_target_pairs={{0,64},{1,65},{2,66},{3,67},{4,68},{5,69},{6,70},{7,71},{8,72},{9,... | collective-permute-start | bytes 24584 | tf_op jit(solution)/shard_map/ppermute | solution.py:433
  38.7 0.0 collective-permute-done.odd
  38.7 0.0 collective-permute-done.1.even
  38.7 0.0 copy-done.2
  38.7 0.0 copy-done
  38.7 0.0 copy-done.1
  38.8 0.0 copy-start.6
  38.8 2.1 %shard_map.161 = (f32[128,640]{1,0:T(8,128)S(1)}, f32[128,640]{1,0:T(8,128)S(1)}, f32[128,640]{1,0:T(8,128)S(1)}, f32[4,128]{1,0:T(4,128)S(1)}, f32[4,128,128]{2,1,0:T(8,128)S(1)}) custom-call(f32[128,512]{1,0:T(8,128)S(1)} %bitcast.22, bf16[128,512]{1,0:T(8,128)(2,1)S(1)} %bitcast.25, bf16[128,512]{1,0:T(8,128)(2,1)S(1)} %bitcast.27, ...), custom_call_target="tpu_custom_call" | custom-call | tf_op jit(solution)/shard_map/pallas_call | solution.py:24
  40.8 0.0 copy-start.3
  40.9 15.1 %all-gather.2.surfaces = f32[4,4,128]{2,1,0:T(4,128)S(1)} all-gather(f32[1,4,128]{2,1,0:T(4,128)S(1)} %bitcast.40), channel_id=3, replica_groups=mesh['sec'=4,'tile'=128] {'sec'}, dimensions={0}, use_global_device_ids=true | all-gather | bytes 10240 | tf_op jit(solution)/shard_map/all_gather | solution.py:447
  55.9 0.2 shard_map.162
  56.2 5.4 %collective-permute-start.3 = (f32[8,128]{1,0:T(8,128)S(1)}, f32[8,128]{1,0:T(8,128)S(1)}, u32[]{:S(2)}, u32[]{:S(2)}) collective-permute-start(f32[8,128]{1,0:T(8,128)S(1)} %get-tuple-element.48), channel_id=1, source_target_pairs={{1,2},{2,1},{3,4},{4,3},{5,6},{6,5},{7,8},{8,7},{9,10},{10,9},{11,... | collective-permute-start | bytes 12296 | tf_op jit(solution)/shard_map/ppermute | solution.py:453
  61.6 1.9 %collective-permute-start.4 = (f32[8,128]{1,0:T(8,128)S(1)}, f32[8,128]{1,0:T(8,128)S(1)}, u32[]{:S(2)}, u32[]{:S(2)}) collective-permute-start(f32[8,128]{1,0:T(8,128)S(1)} %get-tuple-element.49), channel_id=1, source_target_pairs={{0,1},{1,0},{2,3},{3,2},{4,5},{5,4},{6,7},{7,6},{8,9},{9,8},{10,11... | collective-permute-start | bytes 12296 | tf_op jit(solution)/shard_map/ppermute | solution.py:454
  63.5 0.0 collective-permute-done.2.mirrored
  63.5 0.0 copy-done.6
  63.5 0.0 copy-done.3
  63.6 1.0 shard_map.163
  64.6 1.3 %collective-permute-done.3.odd = f32[8,128]{1,0:T(8,128)S(1)} collective-permute-done((f32[8,128]{1,0:T(8,128)S(1)}, f32[8,128]{1,0:T(8,128)S(1)}, u32[]{:S(2)}, u32[]{:S(2)}) %collective-permute-start.3) | collective-permute-done | bytes 4128 | tf_op jit(solution)/shard_map/ppermute | solution.py:453
  65.9 0.3 collective-permute-done.4.even
  66.2 2.4 %shard_map.164 = (f32[128,512]{1,0:T(8,128)}, f32[1024,128]{1,0:T(8,128)S(1)}) custom-call(f32[128,640]{1,0:T(8,128)S(1)} %get-tuple-element.40.window, f32[128,640]{1,0:T(8,128)S(1)} %get-tuple-element.41.rates, f32[128,640]{1,0:T(8,128)S(1)} %get-tuple-element.42.tend, bf16[128,384]{1,0:T(8,128)(2,1)S(1)} %get-tuple-element.34.left, ...), custom_call_target="tpu_custom_call" | custom-call | tf_op jit(solution)/shard_map/pallas_call | solution.py:24
  68.7 23.2 %all_to_all.10 = f32[64,16,128]{2,1,0:T(8,128)S(1)} all-to-all(f32[64,16,128]{2,1,0:T(8,128)S(1)} %bitcast.23), channel_id=1, replica_groups={{0,1,2,3,4,5,6,7,8,9,10,11,12,13,14,15,16,17,18,19,20,21,22,23,24,25,26..., dimensions={0} | all-to-all | bytes 1048576 | tf_op jit(solution)/shard_map/all_to_all | solution.py:472
  91.9 0.5 shard_map.165
  92.4 5.2 %collective-permute-start.5 = (f32[4,32,128]{2,1,0:T(8,128)S(1)}, f32[4,32,128]{2,1,0:T(8,128)S(1)}, u32[]{:S(2)}, u32[]{:S(2)}) collective-permute-start(f32[4,32,128]{2,1,0:T(8,128)S(1)} %get-tuple-element.60), channel_id=1, source_target_pairs={{0,128},{128,0},{256,384},{384,256},{1,129},{129,1},{257,385},{385... | collective-permute-start | bytes 196616 | tf_op jit(solution)/shard_map/ppermute | solution.py:484
  97.6 0.9 collective-permute-done.5
  98.5 0.0 copy-start.8
  98.5 16.9 %all_to_all.11.received = f32[4,32,128]{2,1,0:T(8,128)S(1)} all-to-all(f32[4,32,128]{2,1,0:T(8,128)S(1)} %add.3), channel_id=1, replica_groups={{0,64,256,320},{1,65,257,321},{2,66,258,322},{3,67,259,323},{4,68,260,3..., dimensions={0} | all-to-all | bytes 131072 | tf_op jit(solution)/shard_map/all_to_all | solution.py:485
  115.4 0.0 copy-done.8
  115.4 0.8 shard_map.166
  (1 shorter events, 0.0 us)
Async XLA Ops:
  0.6 22.4 %copy-start.4 = (s32[1,4,512]{2,1,0:T(4,128)S(1)}, s32[1,4,512]{2,1,0:T(4,128)}, u32[]{:S(2)}) copy-start(s32[1,4,512]{2,1,0:T(4,128)} %param.20) | copy-start | bytes 24580
  0.6 22.4 %copy-start.5 = (f32[1,4,512]{2,1,0:T(4,128)S(1)}, f32[1,4,512]{2,1,0:T(4,128)}, u32[]{:S(2)}) copy-start(f32[1,4,512]{2,1,0:T(4,128)} %param.21) | copy-start | bytes 24580
  0.7 35.2 %copy-start.7 = (f32[1,128,128]{2,1,0:T(8,128)S(1)}, f32[1,128,128]{2,1,0:T(8,128)}, u32[]{:S(2)}) copy-start(f32[1,128,128]{2,1,0:T(8,128)} %param.18) | copy-start | bytes 196612
  0.7 38.1 %copy-start.2 = (bf16[1,128,512]{2,1,0:T(8,128)(2,1)S(1)}, bf16[1,128,512]{2,1,0:T(8,128)(2,1)}, u32[]{:S(2)}) copy-start(bf16[1,128,512]{2,1,0:T(8,128)(2,1)} %param.17) | copy-start | bytes 393220
  1.9 34.0 %copy-start.9 = (s32[2,1,1,128,4]{3,4,2,1,0:T(4,128)S(1)}, s32[2,1,1,128,4]{3,4,2,1,0:T(4,128)}, u32[]{:S(2)}) copy-start(s32[2,1,1,128,4]{3,4,2,1,0:T(4,128)} %param.23) | copy-start | bytes 12292
  1.9 34.0 %copy-start.10 = (s32[2,1,8,64]{3,2,1,0:T(8,128)S(1)}, s32[2,1,8,64]{3,2,1,0:T(8,128)}, u32[]{:S(2)}) copy-start(s32[2,1,8,64]{3,2,1,0:T(8,128)} %param.24) | copy-start | bytes 12292
  1.9 34.0 %copy-start.11 = (f32[2,1,8,64]{3,2,1,0:T(8,128)S(1)}, f32[2,1,8,64]{3,2,1,0:T(8,128)}, u32[]{:S(2)}) copy-start(f32[2,1,8,64]{3,2,1,0:T(8,128)} %param.25) | copy-start | bytes 12292
  2.0 34.0 %copy-start.12 = (s32[2,1,64]{2,1,0:T(1,128)S(1)}, s32[2,1,64]{2,1,0:T(1,128)}, u32[]{:S(2)}) copy-start(s32[2,1,64]{2,1,0:T(1,128)} %param.26) | copy-start | bytes 1540
  2.0 34.0 %copy-start.13 = (s32[4]{0:T(128)S(1)}, s32[4]{0:T(128)}, u32[]{:S(2)}) copy-start(s32[4]{0:T(128)} %active.1) | copy-start | bytes 52
  2.0 34.0 %copy-start.14 = (f32[1,128]{1,0:T(1,128)S(1)}, f32[1,128]{1,0:T(1,128)}, u32[]{:S(2)}) copy-start(f32[1,128]{1,0:T(1,128)} %coupling.1) | copy-start | bytes 1540
  2.0 36.7 %copy-start = (f32[1,128,512]{2,1,0:T(8,128)S(1)}, f32[1,128,512]{2,1,0:T(8,128)}, u32[]{:S(2)}) copy-start(f32[1,128,512]{2,1,0:T(8,128)} %param.15) | copy-start | bytes 786436
  23.0 15.8 %copy-start.1 = (bf16[1,128,512]{2,1,0:T(8,128)(2,1)S(1)}, bf16[1,128,512]{2,1,0:T(8,128)(2,1)}, u32[]{:S(2)}) copy-start(bf16[1,128,512]{2,1,0:T(8,128)(2,1)} %param.16) | copy-start | bytes 393220
  23.2 15.5 %collective-permute-start = (f32[32,128]{1,0:T(8,128)S(1)}, f32[32,128]{1,0:T(8,128)S(1)}, u32[]{:S(2)}, u32[]{:S(2)}) collective-permute-start(f32[32,128]{1,0:T(8,128)S(1)} %get-tuple-element.38), channel_id=1, source_target_pairs={{1,2},{2,1},{3,4},{4,3},{5,6},{6,5},{7,8},{8,7},{9,10},{10,9},{11,... | collective-permute-start | bytes 49160 | tf_op jit(solution)/shard_map/ppermute | solution.py:419
  34.0 4.8 %collective-permute-start.1 = (f32[32,128]{1,0:T(8,128)S(1)}, f32[32,128]{1,0:T(8,128)S(1)}, u32[]{:S(2)}, u32[]{:S(2)}) collective-permute-start(f32[32,128]{1,0:T(8,128)S(1)} %get-tuple-element.39), channel_id=1, source_target_pairs={{0,1},{1,0},{2,3},{3,2},{4,5},{5,4},{6,7},{7,6},{8,9},{9,8},{10,11... | collective-permute-start | bytes 49160 | tf_op jit(solution)/shard_map/ppermute | solution.py:420
  36.8 26.7 %collective-permute-start.2 = (f32[32,64]{1,0:T(8,128)S(1)}, f32[32,64]{1,0:T(8,128)S(1)}, u32[]{:S(2)}, u32[]{:S(2)}) collective-permute-start(f32[32,64]{1,0:T(8,128)S(1)} %get-tuple-element.43.lists), channel_id=1, source_target_pairs={{0,64},{1,65},{2,66},{3,67},{4,68},{5,69},{6,70},{7,71},{8,72},{9,... | collective-permute-start | bytes 24584 | tf_op jit(solution)/shard_map/ppermute | solution.py:433
  38.8 24.8 %copy-start.6 = (f32[1,128,128]{2,1,0:T(8,128)S(1)}, f32[1,128,128]{2,1,0:T(8,128)}, u32[]{:S(2)}) copy-start(f32[1,128,128]{2,1,0:T(8,128)} %param.27) | copy-start | bytes 196612
  40.8 22.7 %copy-start.3 = (f32[128,256]{1,0:T(8,128)S(1)}, f32[128,256]{1,0:T(8,128)}, u32[]{:S(2)}) copy-start(f32[128,256]{1,0:T(8,128)} %abel.1) | copy-start | bytes 393220
  56.2 9.8 %collective-permute-start.3 = (f32[8,128]{1,0:T(8,128)S(1)}, f32[8,128]{1,0:T(8,128)S(1)}, u32[]{:S(2)}, u32[]{:S(2)}) collective-permute-start(f32[8,128]{1,0:T(8,128)S(1)} %get-tuple-element.48), channel_id=1, source_target_pairs={{1,2},{2,1},{3,4},{4,3},{5,6},{6,5},{7,8},{8,7},{9,10},{10,9},{11,... | collective-permute-start | bytes 12296 | tf_op jit(solution)/shard_map/ppermute | solution.py:453
  61.6 4.6 %collective-permute-start.4 = (f32[8,128]{1,0:T(8,128)S(1)}, f32[8,128]{1,0:T(8,128)S(1)}, u32[]{:S(2)}, u32[]{:S(2)}) collective-permute-start(f32[8,128]{1,0:T(8,128)S(1)} %get-tuple-element.49), channel_id=1, source_target_pairs={{0,1},{1,0},{2,3},{3,2},{4,5},{5,4},{6,7},{7,6},{8,9},{9,8},{10,11... | collective-permute-start | bytes 12296 | tf_op jit(solution)/shard_map/ppermute | solution.py:454
  92.4 6.1 %collective-permute-start.5 = (f32[4,32,128]{2,1,0:T(8,128)S(1)}, f32[4,32,128]{2,1,0:T(8,128)S(1)}, u32[]{:S(2)}, u32[]{:S(2)}) collective-permute-start(f32[4,32,128]{2,1,0:T(8,128)S(1)} %get-tuple-element.60), channel_id=1, source_target_pairs={{0,128},{128,0},{256,384},{384,256},{1,129},{129,1},{257,385},{385... | collective-permute-start | bytes 196616 | tf_op jit(solution)/shard_map/ppermute | solution.py:484
  98.5 16.9 %copy-start.8 = (f32[2,16,256]{2,1,0:T(8,128)S(1)}, f32[2,16,256]{2,1,0:T(8,128)}, u32[]{:S(2)}) copy-start(f32[2,16,256]{2,1,0:T(8,128)} %observed.1) | copy-start | bytes 98308

commit v5 on v4

--- a/solution.py
+++ b/solution.py
@@ -155,7 +155,15 @@
         out[:, cut] = partner - surface(j)
 
 
-def couple_first(shared, index, weight, boundary, odd, even):
+def couple_first(
+    shared, index, weight, slots, weights, counts, boundary, odd, lists, even
+):
+    steps, ranks, occultations = slots.shape
+    for p in range(steps):
+        rank = lax.broadcasted_iota(jnp.int32, (ranks, occultations), 0)
+        lists[p * ranks : (p + 1) * ranks, :] = slots[p].astype(f32)
+        live = jnp.where(rank < counts[p : p + 1, :], weights[p], 0.0)
+        lists[(steps + p) * ranks : (steps + p + 1) * ranks, :] = live
     section = lax.axis_index("sec")
     table = [shared[s, r : r + 1, :] for s in range(shared.shape[0]) for r in range(48, 52)]
     own_boundary(
@@ -273,15 +281,7 @@
                 parcels[pl.ds(first, part, stride=width), :] = owned
 
 
-def ready_first(
-    active, mixing, coupling, listed, slots, weights, counts, left, response, alive, hits, lists
-):
-    steps, ranks, occultations = slots.shape
-    for p in range(steps):
-        rank = lax.broadcasted_iota(jnp.int32, (ranks, occultations), 0)
-        lists[p * ranks : (p + 1) * ranks, :] = slots[p].astype(f32)
-        live = jnp.where(rank < counts[p : p + 1, :], weights[p], 0.0)
-        lists[(steps + p) * ranks : (steps + p + 1) * ranks, :] = live
+def ready_first(active, mixing, coupling, listed, left, response, alive, hits):
     width = alive.shape[1]
     lane = lane_ids((1, width))
     column = jnp.where(lane < width - LANES, lane, lane - (width - LANES))
@@ -411,27 +411,29 @@
         ],
     )
     shared = lax.all_gather(edges, "sec", axis=0, tiled=False)
-    boundary, odd, even = call(
+    boundary, odd, lists, even = call(
         couple_first,
-        (shape((1, columns), f32), shape((32, LANES), f32), shape((32, LANES), f32)),
-        shared, index, weight,
+        (
+            shape((1, columns), f32),
+            shape((32, LANES), f32),
+            shape((2 * STEPS * ranks, owned), f32),
+            shape((32, LANES), f32),
+        ),
+        shared, index, weight, occ_slot[:, 0], occ_weight[:, 0], occ_count[:, 0],
     )
     odd = lax.ppermute(odd, AXES, above_odd)
+    mirrored = lax.ppermute(lists, "tile", [(t, (t + part) % tiles) for t in range(tiles)])
     even = lax.ppermute(even, AXES, above_even)
     mixing_row, _ = after((mixing[0], boundary))
-    left, response, alive, hits, lists = call(
+    left, response, alive, hits = call(
         ready_first,
         (
             shape((levels, 3 * levels), bf16),
             shape((levels, LANES), f32),
             shape((1, width), f32),
             shape((columns, 4 * tiles), bf16),
-            shape((2 * STEPS * ranks, owned), f32),
         ),
-        active_cols, mixing_row, coupling, listed, occ_slot[:, 0], occ_weight[:, 0], occ_count[:, 0],
-    )
-    mirrored = lax.ppermute(
-        lists, "tile", [(t, (t + part) % tiles) for t in range(tiles)]
+        active_cols, mixing_row, coupling, listed,
     )
     window, rates, tend, surface, parcel = call(
         step_first,

time: 117 us -> 117 us (level)
  no operation moved by 1% of the time
where the time goes in v5:
time: 117 us; the launch traced here: 116 us
  blocking collectives  76.2 us (65%)
  starting transfers between devices  27.1 us (23%)
  Pallas kernels  9.25 us (8%)
  waiting for transfers between devices  2.53 us (2%)
    all_to_all x1, blocking collectives, shards(): lax.all_to_all(parcels.reshape(part, 8 * PARTS, levels), 'tile', split_ax...  23.2 us
    all_gather x1, blocking collectives, shards(): shared = lax.all_gather(edges, 'sec', axis=0, tiled=False)  21 us
    all_to_all x1, blocking collectives, shards(): lax.all_to_all(kept + got, AXES, split_axis=0, concat_axis=0, axis_index_...  16.9 us
    ppermute x2, starting transfers between devices, shards(): odd = lax.ppermute(odd, AXES, above_odd)  16.1 us
    all_gather x1, blocking collectives, shards(): surfaces = lax.all_gather(surface, 'sec', axis=0, tiled=False)  15.1 us
    pallas_call x9, Pallas kernels, call(): pl.pallas_call(body, out_shape=outs if single else tuple(outs), in_specs=...  9.25 us
    ppermute x1, starting transfers between devices, shards(): got = lax.ppermute(sent, 'sec', [(s, s ^ 1) for s in range(sections)])  5.22 us
    ppermute x2, starting transfers between devices, shards(): even = lax.ppermute(even, AXES, above_even)  3.84 us
  transfers between devices with their start and end apart: 6, of which 3 were waited for; matrix products, arithmetic and copies ran while one was open for 0% of the time, Pallas kernels for 4%

profile of v5, /device:TPU:1, one launch (start us, length us, event | category | flops | bytes accessed | tf_op | source)
XLA Modules:
  0.0 116.1 jit_solution(8758655756807573245)
XLA Ops:
  0.6 0.0 copy-start.4
  0.6 0.0 copy-start.5
  0.7 0.0 copy-start.10
  0.7 0.0 copy-start.11
  0.7 0.0 copy-start.12
  0.7 0.0 copy-start.7
  0.7 0.0 copy-start.2
  0.7 1.3 %shard_map.158 = f32[64,128]{1,0:T(8,128)S(1)} custom-call(f32[128,512]{1,0:T(8,128)} %bitcast.21, bf16[128,512]{1,0:T(8,128)(2,1)} %bitcast.24, bf16[128,512]{1,0:T(8,128)(2,1)} %bitcast.26, s32[4,512]{1,0:T(4,128)} %bitcast.28, f32[4,512]{1,0:T(4,128)} %bitcast.31), custom_call_target="tpu_custom_call" | custom-call | tf_op jit(solution)/shard_map/pallas_call | solution.py:24
  2.0 0.0 copy-start.9
  2.0 0.0 copy-start.13
  2.0 0.0 copy-start.14
  2.0 0.0 copy-start
  2.0 21.0 %all-gather = f32[256,128]{1,0:T(8,128)S(1)} all-gather(f32[64,128]{1,0:T(8,128)S(1)} %shard_map.158), channel_id=2, replica_groups=mesh['sec'=4,'tile'=128] {'sec'}, dimensions={0}, use_global_device_ids=true | all-gather | bytes 163840 | tf_op jit(solution)/shard_map/all_gather | solution.py:413
  23.0 0.0 copy-start.1
  23.0 0.0 copy-done.4
  23.0 0.0 copy-done.5
  23.0 0.0 copy-done.10
  23.0 0.0 copy-done.11
  23.0 0.0 copy-done.12
  23.0 0.2 shard_map.159
  23.2 10.7 %collective-permute-start = (f32[32,128]{1,0:T(8,128)S(1)}, f32[32,128]{1,0:T(8,128)S(1)}, u32[]{:S(2)}, u32[]{:S(2)}) collective-permute-start(f32[32,128]{1,0:T(8,128)S(1)} %get-tuple-element.38), channel_id=1, source_target_pairs={{1,2},{2,1},{3,4},{4,3},{5,6},{6,5},{7,8},{8,7},{9,10},{10,9},{11,... | collective-permute-start | bytes 49160 | tf_op jit(solution)/shard_map/ppermute | solution.py:424
  34.0 1.9 %collective-permute-start.1 = (f32[32,128]{1,0:T(8,128)S(1)}, f32[32,128]{1,0:T(8,128)S(1)}, u32[]{:S(2)}, u32[]{:S(2)}) collective-permute-start(f32[32,128]{1,0:T(8,128)S(1)} %get-tuple-element.39), channel_id=1, source_target_pairs={{0,1},{1,0},{2,3},{3,2},{4,5},{5,4},{6,7},{7,6},{8,9},{9,8},{10,11... | collective-permute-start | bytes 49160 | tf_op jit(solution)/shard_map/ppermute | solution.py:426
  35.9 1.9 %collective-permute-start.2 = (f32[32,64]{1,0:T(8,128)S(1)}, f32[32,64]{1,0:T(8,128)S(1)}, u32[]{:S(2)}, u32[]{:S(2)}) collective-permute-start(f32[32,64]{1,0:T(8,128)S(1)} %get-tuple-element.43.lists), channel_id=1, source_target_pairs={{0,64},{1,65},{2,66},{3,67},{4,68},{5,69},{6,70},{7,71},{8,72},{9,... | collective-permute-start | bytes 24584 | tf_op jit(solution)/shard_map/ppermute | solution.py:425
  37.9 0.0 copy-done.7
  37.9 0.0 copy-done.9
  37.9 0.0 copy-done.13
  37.9 0.0 copy-done.14
  37.9 0.8 shard_map.160
  38.7 0.0 collective-permute-done.odd
  38.7 0.0 collective-permute-done.1.even
  38.7 0.0 copy-done.2
  38.7 0.0 copy-done
  38.8 0.0 copy-done.1
  38.8 0.0 copy-start.6
  38.8 2.1 %shard_map.161 = (f32[128,640]{1,0:T(8,128)S(1)}, f32[128,640]{1,0:T(8,128)S(1)}, f32[128,640]{1,0:T(8,128)S(1)}, f32[4,128]{1,0:T(4,128)S(1)}, f32[4,128,128]{2,1,0:T(8,128)S(1)}) custom-call(f32[128,512]{1,0:T(8,128)S(1)} %bitcast.22, bf16[128,512]{1,0:T(8,128)(2,1)S(1)} %bitcast.25, bf16[128,512]{1,0:T(8,128)(2,1)S(1)} %bitcast.27, ...), custom_call_target="tpu_custom_call" | custom-call | tf_op jit(solution)/shard_map/pallas_call | solution.py:24
  40.9 0.0 copy-start.3
  40.9 15.1 %all-gather.2.surfaces = f32[4,4,128]{2,1,0:T(4,128)S(1)} all-gather(f32[1,4,128]{2,1,0:T(4,128)S(1)} %bitcast.40), channel_id=3, replica_groups=mesh['sec'=4,'tile'=128] {'sec'}, dimensions={0}, use_global_device_ids=true | all-gather | bytes 10240 | tf_op jit(solution)/shard_map/all_gather | solution.py:449
  56.0 0.2 shard_map.162
  56.2 5.4 %collective-permute-start.3 = (f32[8,128]{1,0:T(8,128)S(1)}, f32[8,128]{1,0:T(8,128)S(1)}, u32[]{:S(2)}, u32[]{:S(2)}) collective-permute-start(f32[8,128]{1,0:T(8,128)S(1)} %get-tuple-element.48), channel_id=1, source_target_pairs={{1,2},{2,1},{3,4},{4,3},{5,6},{6,5},{7,8},{8,7},{9,10},{10,9},{11,... | collective-permute-start | bytes 12296 | tf_op jit(solution)/shard_map/ppermute | solution.py:455
  61.6 1.9 %collective-permute-start.4 = (f32[8,128]{1,0:T(8,128)S(1)}, f32[8,128]{1,0:T(8,128)S(1)}, u32[]{:S(2)}, u32[]{:S(2)}) collective-permute-start(f32[8,128]{1,0:T(8,128)S(1)} %get-tuple-element.49), channel_id=1, source_target_pairs={{0,1},{1,0},{2,3},{3,2},{4,5},{5,4},{6,7},{7,6},{8,9},{9,8},{10,11... | collective-permute-start | bytes 12296 | tf_op jit(solution)/shard_map/ppermute | solution.py:456
  63.5 0.0 collective-permute-done.2.mirrored
  63.5 0.0 copy-done.6
  63.5 0.0 copy-done.3
  63.6 1.0 shard_map.163
  64.6 1.4 %collective-permute-done.3.odd = f32[8,128]{1,0:T(8,128)S(1)} collective-permute-done((f32[8,128]{1,0:T(8,128)S(1)}, f32[8,128]{1,0:T(8,128)S(1)}, u32[]{:S(2)}, u32[]{:S(2)}) %collective-permute-start.3) | collective-permute-done | bytes 4128 | tf_op jit(solution)/shard_map/ppermute | solution.py:455
  66.0 0.3 collective-permute-done.4.even
  66.2 2.4 %shard_map.164 = (f32[128,512]{1,0:T(8,128)}, f32[1024,128]{1,0:T(8,128)S(1)}) custom-call(f32[128,640]{1,0:T(8,128)S(1)} %get-tuple-element.40.window, f32[128,640]{1,0:T(8,128)S(1)} %get-tuple-element.41.rates, f32[128,640]{1,0:T(8,128)S(1)} %get-tuple-element.42.tend, bf16[128,384]{1,0:T(8,128)(2,1)S(1)} %get-tuple-element.34.left, ...), custom_call_target="tpu_custom_call" | custom-call | tf_op jit(solution)/shard_map/pallas_call | solution.py:24
  68.7 23.2 %all_to_all.10 = f32[64,16,128]{2,1,0:T(8,128)S(1)} all-to-all(f32[64,16,128]{2,1,0:T(8,128)S(1)} %bitcast.23), channel_id=1, replica_groups={{0,1,2,3,4,5,6,7,8,9,10,11,12,13,14,15,16,17,18,19,20,21,22,23,24,25,26..., dimensions={0} | all-to-all | bytes 1048576 | tf_op jit(solution)/shard_map/all_to_all | solution.py:474
  91.9 0.5 shard_map.165
  92.4 5.2 %collective-permute-start.5 = (f32[4,32,128]{2,1,0:T(8,128)S(1)}, f32[4,32,128]{2,1,0:T(8,128)S(1)}, u32[]{:S(2)}, u32[]{:S(2)}) collective-permute-start(f32[4,32,128]{2,1,0:T(8,128)S(1)} %get-tuple-element.60), channel_id=1, source_target_pairs={{0,128},{128,0},{256,384},{384,256},{1,129},{129,1},{257,385},{385... | collective-permute-start | bytes 196616 | tf_op jit(solution)/shard_map/ppermute | solution.py:486
  97.6 0.9 collective-permute-done.5
  98.5 0.0 copy-start.8
  98.5 16.9 %all_to_all.11.received = f32[4,32,128]{2,1,0:T(8,128)S(1)} all-to-all(f32[4,32,128]{2,1,0:T(8,128)S(1)} %add.3), channel_id=1, replica_groups={{0,64,256,320},{1,65,257,321},{2,66,258,322},{3,67,259,323},{4,68,260,3..., dimensions={0} | all-to-all | bytes 131072 | tf_op jit(solution)/shard_map/all_to_all | solution.py:487
  115.4 0.0 copy-done.8
  115.4 0.8 shard_map.166
  (1 shorter events, 0.0 us)
Async XLA Ops:
  0.6 22.4 %copy-start.4 = (s32[1,4,512]{2,1,0:T(4,128)S(1)}, s32[1,4,512]{2,1,0:T(4,128)}, u32[]{:S(2)}) copy-start(s32[1,4,512]{2,1,0:T(4,128)} %param.20) | copy-start | bytes 24580
  0.6 22.4 %copy-start.5 = (f32[1,4,512]{2,1,0:T(4,128)S(1)}, f32[1,4,512]{2,1,0:T(4,128)}, u32[]{:S(2)}) copy-start(f32[1,4,512]{2,1,0:T(4,128)} %param.21) | copy-start | bytes 24580
  0.7 22.4 %copy-start.10 = (s32[2,1,8,64]{3,2,1,0:T(8,128)S(1)}, s32[2,1,8,64]{3,2,1,0:T(8,128)}, u32[]{:S(2)}) copy-start(s32[2,1,8,64]{3,2,1,0:T(8,128)} %param.24) | copy-start | bytes 12292
  0.7 22.4 %copy-start.11 = (f32[2,1,8,64]{3,2,1,0:T(8,128)S(1)}, f32[2,1,8,64]{3,2,1,0:T(8,128)}, u32[]{:S(2)}) copy-start(f32[2,1,8,64]{3,2,1,0:T(8,128)} %param.25) | copy-start | bytes 12292
  0.7 22.4 %copy-start.12 = (s32[2,1,64]{2,1,0:T(1,128)S(1)}, s32[2,1,64]{2,1,0:T(1,128)}, u32[]{:S(2)}) copy-start(s32[2,1,64]{2,1,0:T(1,128)} %param.26) | copy-start | bytes 1540
  0.7 37.2 %copy-start.7 = (f32[1,128,128]{2,1,0:T(8,128)S(1)}, f32[1,128,128]{2,1,0:T(8,128)}, u32[]{:S(2)}) copy-start(f32[1,128,128]{2,1,0:T(8,128)} %param.18) | copy-start | bytes 196612
  0.7 38.0 %copy-start.2 = (bf16[1,128,512]{2,1,0:T(8,128)(2,1)S(1)}, bf16[1,128,512]{2,1,0:T(8,128)(2,1)}, u32[]{:S(2)}) copy-start(bf16[1,128,512]{2,1,0:T(8,128)(2,1)} %param.17) | copy-start | bytes 393220
  2.0 35.9 %copy-start.9 = (s32[2,1,1,128,4]{3,4,2,1,0:T(4,128)S(1)}, s32[2,1,1,128,4]{3,4,2,1,0:T(4,128)}, u32[]{:S(2)}) copy-start(s32[2,1,1,128,4]{3,4,2,1,0:T(4,128)} %param.23) | copy-start | bytes 12292
  2.0 35.9 %copy-start.13 = (s32[4]{0:T(128)S(1)}, s32[4]{0:T(128)}, u32[]{:S(2)}) copy-start(s32[4]{0:T(128)} %active.1) | copy-start | bytes 52
  2.0 35.9 %copy-start.14 = (f32[1,128]{1,0:T(1,128)S(1)}, f32[1,128]{1,0:T(1,128)}, u32[]{:S(2)}) copy-start(f32[1,128]{1,0:T(1,128)} %coupling.1) | copy-start | bytes 1540
  2.0 36.7 %copy-start = (f32[1,128,512]{2,1,0:T(8,128)S(1)}, f32[1,128,512]{2,1,0:T(8,128)}, u32[]{:S(2)}) copy-start(f32[1,128,512]{2,1,0:T(8,128)} %param.15) | copy-start | bytes 786436
  23.0 15.8 %copy-start.1 = (bf16[1,128,512]{2,1,0:T(8,128)(2,1)S(1)}, bf16[1,128,512]{2,1,0:T(8,128)(2,1)}, u32[]{:S(2)}) copy-start(bf16[1,128,512]{2,1,0:T(8,128)(2,1)} %param.16) | copy-start | bytes 393220
  23.2 15.5 %collective-permute-start = (f32[32,128]{1,0:T(8,128)S(1)}, f32[32,128]{1,0:T(8,128)S(1)}, u32[]{:S(2)}, u32[]{:S(2)}) collective-permute-start(f32[32,128]{1,0:T(8,128)S(1)} %get-tuple-element.38), channel_id=1, source_target_pairs={{1,2},{2,1},{3,4},{4,3},{5,6},{6,5},{7,8},{8,7},{9,10},{10,9},{11,... | collective-permute-start | bytes 49160 | tf_op jit(solution)/shard_map/ppermute | solution.py:424
  34.0 4.7 %collective-permute-start.1 = (f32[32,128]{1,0:T(8,128)S(1)}, f32[32,128]{1,0:T(8,128)S(1)}, u32[]{:S(2)}, u32[]{:S(2)}) collective-permute-start(f32[32,128]{1,0:T(8,128)S(1)} %get-tuple-element.39), channel_id=1, source_target_pairs={{0,1},{1,0},{2,3},{3,2},{4,5},{5,4},{6,7},{7,6},{8,9},{9,8},{10,11... | collective-permute-start | bytes 49160 | tf_op jit(solution)/shard_map/ppermute | solution.py:426
  35.9 27.6 %collective-permute-start.2 = (f32[32,64]{1,0:T(8,128)S(1)}, f32[32,64]{1,0:T(8,128)S(1)}, u32[]{:S(2)}, u32[]{:S(2)}) collective-permute-start(f32[32,64]{1,0:T(8,128)S(1)} %get-tuple-element.43.lists), channel_id=1, source_target_pairs={{0,64},{1,65},{2,66},{3,67},{4,68},{5,69},{6,70},{7,71},{8,72},{9,... | collective-permute-start | bytes 24584 | tf_op jit(solution)/shard_map/ppermute | solution.py:425
  38.8 24.8 %copy-start.6 = (f32[1,128,128]{2,1,0:T(8,128)S(1)}, f32[1,128,128]{2,1,0:T(8,128)}, u32[]{:S(2)}) copy-start(f32[1,128,128]{2,1,0:T(8,128)} %param.27) | copy-start | bytes 196612
  40.9 22.7 %copy-start.3 = (f32[128,256]{1,0:T(8,128)S(1)}, f32[128,256]{1,0:T(8,128)}, u32[]{:S(2)}) copy-start(f32[128,256]{1,0:T(8,128)} %abel.1) | copy-start | bytes 393220
  56.2 9.8 %collective-permute-start.3 = (f32[8,128]{1,0:T(8,128)S(1)}, f32[8,128]{1,0:T(8,128)S(1)}, u32[]{:S(2)}, u32[]{:S(2)}) collective-permute-start(f32[8,128]{1,0:T(8,128)S(1)} %get-tuple-element.48), channel_id=1, source_target_pairs={{1,2},{2,1},{3,4},{4,3},{5,6},{6,5},{7,8},{8,7},{9,10},{10,9},{11,... | collective-permute-start | bytes 12296 | tf_op jit(solution)/shard_map/ppermute | solution.py:455
  61.6 4.6 %collective-permute-start.4 = (f32[8,128]{1,0:T(8,128)S(1)}, f32[8,128]{1,0:T(8,128)S(1)}, u32[]{:S(2)}, u32[]{:S(2)}) collective-permute-start(f32[8,128]{1,0:T(8,128)S(1)} %get-tuple-element.49), channel_id=1, source_target_pairs={{0,1},{1,0},{2,3},{3,2},{4,5},{5,4},{6,7},{7,6},{8,9},{9,8},{10,11... | collective-permute-start | bytes 12296 | tf_op jit(solution)/shard_map/ppermute | solution.py:456
  92.4 6.1 %collective-permute-start.5 = (f32[4,32,128]{2,1,0:T(8,128)S(1)}, f32[4,32,128]{2,1,0:T(8,128)S(1)}, u32[]{:S(2)}, u32[]{:S(2)}) collective-permute-start(f32[4,32,128]{2,1,0:T(8,128)S(1)} %get-tuple-element.60), channel_id=1, source_target_pairs={{0,128},{128,0},{256,384},{384,256},{1,129},{129,1},{257,385},{385... | collective-permute-start | bytes 196616 | tf_op jit(solution)/shard_map/ppermute | solution.py:486
  98.5 16.9 %copy-start.8 = (f32[2,16,256]{2,1,0:T(8,128)S(1)}, f32[2,16,256]{2,1,0:T(8,128)}, u32[]{:S(2)}) copy-start(f32[2,16,256]{2,1,0:T(8,128)} %observed.1) | copy-start | bytes 98308

commit v6 on v5

--- a/solution.py
+++ b/solution.py
@@ -192,108 +192,121 @@
         out[...] = jnp.broadcast_to(edge, out.shape)
 
 
-def edge_row(left, right):
-    lane = lane_ids(left.shape)
-    value = jnp.where(lane < HALO, right, 0.0)
-    return jnp.where(lane >= LANES - HALO, pltpu.roll(left, LANES - 2 * HALO, 1), value)
-
-
-def edge_block(left, right):
-    gap = jnp.zeros((LANES - 2 * HALO, left.shape[1]), f32)
-    return jnp.concatenate([right, gap, left], axis=0).T
-
-
-def advance(field, rates, constant, left, alive):
-    width = field.shape[1]
+def edge_row(low, high):
+    return jnp.where(lane_ids(low.shape) < HALO, high, low)
+
+
+def halo_rows(odd, even, start):
+    low, high = sides(odd, even, start, HALO)
+    return jnp.concatenate([high, low], axis=0)
+
+
+def turned(x):
+    x = x.astype(f32)
+    return [x[:, j * LANES : (j + 1) * LANES].T for j in range(x.shape[1] // LANES)]
+
+
+def advance(field, rates, constant, right, alive):
+    count = field.shape[0]
     live = alive[...] > 0.0
     for _ in range(SUBS):
-        near = pltpu.roll(field, 1, 1) + pltpu.roll(field, width - 1, 1)
+        near = pltpu.roll(field, 1, 0) + pltpu.roll(field, count - 1, 0)
         spread = field + rates * (near - 2.0 * field)
-        stepped = matmul(left, right_operand(spread)) + constant
+        stepped = matmul(left_operand(spread), right) + constant
         field = jnp.where(live, stepped, field)
     return field
 
 
 def forcing(response, boundary, edge, tendency):
-    row = jnp.concatenate([boundary[...], edge], axis=1)
-    width = row.shape[1]
-    parts = [
-        response * row[:, j * LANES : (j + 1) * LANES] for j in range(width // LANES)
-    ]
-    return jnp.concatenate(parts, axis=1) + tendency
+    count = boundary.shape[1] // LANES
+    rows = [boundary[:, j * LANES : (j + 1) * LANES] for j in range(count)]
+    rows += [edge, jnp.zeros((7 - count, LANES), f32)]
+    values = jnp.concatenate(rows, axis=0).T
+    parts = [values[:, j : j + 1] * response for j in range(count)]
+    parts.append(values[: 2 * HALO, count : count + 1] * response)
+    return jnp.concatenate(parts, axis=0) + tendency
 
 
 def one_hot(listed, columns):
-    row = jnp.concatenate([listed[m : m + 1, :] for m in range(listed.shape[0])], axis=1)
-    column = lax.broadcasted_iota(jnp.int32, (columns, row.shape[1]), 0)
-    return jnp.where(column == row, 1.0, 0.0).astype(bf16)
+    return jnp.concatenate(
+        [
+            jnp.where(listed[:, m : m + 1] == lane_ids((listed.shape[0], columns)), 1.0, 0.0)
+            for m in range(listed.shape[1])
+        ],
+        axis=0,
+    ).astype(bf16)
 
 
 def chosen(field, hits):
-    levels = field.shape[0]
-    high, low = halves(field[:, : hits.shape[0]])
-    both = matmul(jnp.concatenate([high, low], axis=0), hits[...])
-    both = both[:levels] + both[levels:]
-    tiles = hits.shape[1] // 4
-    return [both[:, m * tiles : (m + 1) * tiles].T for m in range(4)]
+    high, low = halves(field)
+    both = matmul(hits, jnp.concatenate([high, low], axis=1))
+    levels = field.shape[1]
+    both = both[:, :levels] + both[:, levels:]
+    tiles = hits.shape[0] // 4
+    return [both[m * tiles : (m + 1) * tiles] for m in range(4)]
 
 
 def step_first(
-    state, tendency, diffusion, left, response, alive, hits, boundary, odd, even,
-    window, rates_out, forcing_out, surface, parcel,
+    state, tendency, diffusion, right, response, alive, boundary, odd, even,
+    window, rates_out, forcing_out, surface,
 ):
-    rates = jnp.concatenate(
-        [diffusion[...].astype(f32), edge_block(*sides(odd, even, 8, 8))], axis=1
-    )
-    tend = jnp.concatenate(
-        [tendency[...].astype(f32), edge_block(*sides(odd, even, 16, 8))], axis=1
-    )
-    field = jnp.concatenate([state[...], edge_block(*sides(odd, even, 0, 8))], axis=1)
+    rates = jnp.concatenate(turned(diffusion[...]) + [halo_rows(odd, even, 8)], axis=0)
+    tend = jnp.concatenate(turned(tendency[...]) + [halo_rows(odd, even, 16)], axis=0)
+    field = jnp.concatenate(turned(state[...]) + [halo_rows(odd, even, 0)], axis=0)
     edge = edge_row(*sides(odd, even, 24, 1))
-    constant = forcing(response[...], boundary, edge, tend)
+    constant = forcing(response[0:1, :], boundary, edge, tend)
     rates_out[...] = rates
     forcing_out[...] = tend
-    field = advance(field, rates, constant, left[...], alive)
+    field = advance(field, rates, constant, right[...], alive)
     window[...] = field
-    levels = field.shape[0]
-    for j in range(4):
-        surface[j : j + 1, :] = field[levels - 1 : levels, j * LANES : (j + 1) * LANES]
-    for m, rows in enumerate(chosen(field, hits)):
-        parcel[m] = rows
+    for j in range(surface.shape[0]):
+        block = field[j * LANES : (j + 1) * LANES].T
+        surface[j : j + 1, :] = block[block.shape[0] - 1 :, :]
 
 
 def step_second(
-    window, rates, tend, left, response, alive, hits, boundary, odd, even, earlier,
+    window, rates, tend, right, response, alive, hits, boundary, odd, even, earlier,
     final, parcels,
 ):
     edge = edge_row(*sides(odd, even, 0, 1))
-    constant = forcing(response[...], boundary, edge, tend[...])
-    field = advance(window[...], rates[...], constant, left[...], alive)
-    final[...] = field[:, : final.shape[1]]
+    constant = forcing(response[0:1, :], boundary, edge, tend[...])
+    field = advance(window[...], rates[...], constant, right[...], alive)
+    columns = final.shape[1]
     slots, tiles, _ = earlier.shape
     part = tiles // PARTS
     width = PARTS * STEPS * slots
-    for m, later in enumerate(chosen(field, hits)):
+    for m, later in enumerate(chosen(field[:columns], hits[...])):
         for o in range(PARTS):
             for p, rows in enumerate((earlier[m], later)):
                 first = (o * STEPS + p) * slots + m
                 owned = rows[o * part : (o + 1) * part]
                 parcels[pl.ds(first, part, stride=width), :] = owned
-
-
-def ready_first(active, mixing, coupling, listed, left, response, alive, hits):
-    width = alive.shape[1]
-    lane = lane_ids((1, width))
-    column = jnp.where(lane < width - LANES, lane, lane - (width - LANES))
-    column = jnp.where(lane < width - HALO, column, lane - LANES)
+    for j in range(columns // LANES):
+        cut = slice(j * LANES, (j + 1) * LANES)
+        final[:, cut] = field[cut].T
+
+
+def ready_first(active, mixing, coupling, right, response, alive):
+    right[...] = right_operand(mixing[...].T)
+    response[...] = jnp.broadcast_to(coupling[...], response.shape)
+    row = lax.broadcasted_iota(jnp.int32, alive.shape, 0)
+    columns = alive.shape[0] - 2 * HALO
+    column = jnp.where(row < columns, row, row - columns)
+    column = jnp.where(row < columns + HALO, column, row - 2 * HALO)
     alive[...] = jnp.where(column < active[lax.axis_index("sec")], 1.0, 0.0)
-    left[...] = left_operand(mixing[...])
-    response[...] = jnp.broadcast_to(coupling[...], (LANES, coupling.shape[1])).T
-    hits[...] = one_hot(listed[0], hits.shape[0])
-
-
-def ready_second(listed, lists, mirrored, refraction, abel, hits, spread, right, right_abel):
-    hits[...] = one_hot(listed[1], hits.shape[0])
+
+
+def ready_second(
+    listed, window, lists, mirrored, refraction, abel, hits, parcel, spread, right, right_abel
+):
+    columns = hits.shape[1]
+    slots = parcel.shape[0]
+    places = jnp.concatenate([listed[p] for p in range(STEPS)], axis=0).T
+    for m, rows in enumerate(
+        chosen(window[0:columns, :], one_hot(places[:, :slots], columns))
+    ):
+        parcel[m] = rows
+    hits[...] = one_hot(places[:, slots : 2 * slots], columns)
     right[...] = right_operand(refraction[...])
     right_abel[...] = right_operand(abel[...])
     occultations, width = spread.shape[2], spread.shape[3] // 3
@@ -378,7 +391,7 @@
     tiles = lax.axis_size("tile")
     levels, columns = state.shape[1:]
     rows, heights = observed.shape[1:]
-    width = columns + LANES
+    width = columns + 2 * HALO
     half = sections // 2
     part = tiles // PARTS
     ranks, owned = occ_slot.shape[2:]
@@ -425,26 +438,24 @@
     mirrored = lax.ppermute(lists, "tile", [(t, (t + part) % tiles) for t in range(tiles)])
     even = lax.ppermute(even, AXES, above_even)
     mixing_row, _ = after((mixing[0], boundary))
-    left, response, alive, hits = call(
+    right, response, alive = call(
         ready_first,
         (
-            shape((levels, 3 * levels), bf16),
-            shape((levels, LANES), f32),
-            shape((1, width), f32),
-            shape((columns, 4 * tiles), bf16),
+            shape((3 * levels, levels), bf16),
+            shape((8, levels), f32),
+            shape((width, levels), f32),
         ),
-        active_cols, mixing_row, coupling, listed,
-    )
-    window, rates, tend, surface, parcel = call(
+        active_cols, mixing_row, coupling,
+    )
+    window, rates, tend, surface = call(
         step_first,
         (
-            shape((levels, width), f32),
-            shape((levels, width), f32),
-            shape((levels, width), f32),
-            shape((4, LANES), f32),
-            shape((4, tiles, levels), f32),
+            shape((width, levels), f32),
+            shape((width, levels), f32),
+            shape((width, levels), f32),
+            shape((columns // LANES, LANES), f32),
         ),
-        state[0], tendency[0], diffusion[0], left, response, alive, hits, boundary, odd, even,
+        state[0], tendency[0], diffusion[0], right, response, alive, boundary, odd, even,
     )
     surfaces = lax.all_gather(surface, "sec", axis=0, tiled=False)
     boundary, odd, even = call(
@@ -455,22 +466,23 @@
     odd = lax.ppermute(odd, AXES, above_odd)
     even = lax.ppermute(even, AXES, above_even)
     mirrored, _ = after((mirrored, boundary))
-    hits, spread, right, right_abel = call(
+    hits, parcel, spread, refract, bend = call(
         ready_second,
         (
-            shape((columns, 4 * tiles), bf16),
+            shape((4 * tiles, columns), bf16),
+            shape((4, tiles, levels), f32),
             shape((PARTS, STEPS, owned, 12 * part), bf16),
             shape((3 * levels, levels), bf16),
             shape((3 * levels, heights), bf16),
         ),
-        listed, lists, mirrored, refraction[0], abel_matrix,
+        listed, window, lists, mirrored, refraction[0], abel_matrix,
     )
     final, parcels = call(
         step_second,
         (shape((levels, columns), f32), shape((8 * tiles, levels), f32)),
-        window, rates, tend, left, response, alive, hits, boundary, odd, even, parcel,
-    )
-    parcels, spread, right, right_abel = after((parcels, spread, right, right_abel))
+        window, rates, tend, right, response, alive, hits, boundary, odd, even, parcel,
+    )
+    parcels, spread, refract, bend = after((parcels, spread, refract, bend))
     arrived = lax.all_to_all(
         parcels.reshape(part, 8 * PARTS, levels),
         "tile",
@@ -481,7 +493,7 @@
     )
     block = shape((half * PARTS, STEPS * rows, levels), f32)
     kept, sent = call(
-        project, (block, block), arrived.reshape(8 * PARTS * part, levels), spread, right
+        project, (block, block), arrived.reshape(8 * PARTS * part, levels), spread, refract
     )
     got = lax.ppermute(sent, "sec", [(s, s ^ 1) for s in range(sections)])
     received = lax.all_to_all(
@@ -497,7 +509,7 @@
         tiled=True,
     )
     departures = call(
-        depart, shape((STEPS, rows, heights), f32), received, right_abel, observed
+        depart, shape((STEPS, rows, heights), f32), received, bend, observed
     )
     return (final[None], departures)
 

time: 117 us -> 116 us (level)
  transfers between devices with their start and end apart: 6 -> 6, of which waited for: 3 -> 3; matrix products, arithmetic and copies ran while one was open for 0% -> 0% of each run, Pallas kernels for 4% -> 3%
where the time goes in v6:
time: 116 us
  blocking collectives  76.4 us (66%)
  starting transfers between devices  26.9 us (23%)
  Pallas kernels  9.12 us (8%)
  waiting for transfers between devices  2.47 us (2%)
    all_to_all x1, blocking collectives, shards(): lax.all_to_all(parcels.reshape(part, 8 * PARTS, levels), 'tile', split_ax...  23.2 us
    all_gather x1, blocking collectives, shards(): shared = lax.all_gather(edges, 'sec', axis=0, tiled=False)  21 us
    all_to_all x1, blocking collectives, shards(): lax.all_to_all(kept + got, AXES, split_axis=0, concat_axis=0, axis_index_...  16.9 us
    ppermute x2, starting transfers between devices, shards(): odd = lax.ppermute(odd, AXES, above_odd)  16 us
    all_gather x1, blocking collectives, shards(): surfaces = lax.all_gather(surface, 'sec', axis=0, tiled=False)  15.3 us
    pallas_call x9, Pallas kernels, call(): pl.pallas_call(body, out_shape=outs if single else tuple(outs), in_specs=...  9.12 us
    ppermute x1, starting transfers between devices, shards(): got = lax.ppermute(sent, 'sec', [(s, s ^ 1) for s in range(sections)])  5.2 us
    ppermute x2, starting transfers between devices, shards(): even = lax.ppermute(even, AXES, above_even)  3.84 us
  transfers between devices with their start and end apart: 6, of which 3 were waited for; matrix products, arithmetic and copies ran while one was open for 0% of the time, Pallas kernels for 3%

profile of v6, /device:TPU:1, one launch (start us, length us, event | category | flops | bytes accessed | tf_op | source)
XLA Modules:
  0.0 116.0 jit_solution(14534599188753156172)
XLA Ops:
  0.6 0.0 copy-start.4
  0.6 0.0 copy-start.5
  0.7 0.0 copy-start.9
  0.7 0.0 copy-start.10
  0.7 0.0 copy-start.12
  0.7 0.0 copy-start.7
  0.7 0.0 copy-start.2
  0.7 1.3 %shard_map.158 = f32[64,128]{1,0:T(8,128)S(1)} custom-call(f32[128,512]{1,0:T(8,128)} %bitcast.21, bf16[128,512]{1,0:T(8,128)(2,1)} %bitcast.24, bf16[128,512]{1,0:T(8,128)(2,1)} %bitcast.26, s32[4,512]{1,0:T(4,128)} %bitcast.28, f32[4,512]{1,0:T(4,128)} %bitcast.31), custom_call_target="tpu_custom_call" | custom-call | tf_op jit(solution)/shard_map/pallas_call | solution.py:24
  2.0 0.0 copy-start.13
  2.0 0.0 copy-start.14
  2.0 0.0 copy-start
  2.0 21.0 %all-gather = f32[256,128]{1,0:T(8,128)S(1)} all-gather(f32[64,128]{1,0:T(8,128)S(1)} %shard_map.158), channel_id=2, replica_groups=mesh['sec'=4,'tile'=128] {'sec'}, dimensions={0}, use_global_device_ids=true | all-gather | bytes 163840 | tf_op jit(solution)/shard_map/all_gather | solution.py:426
  23.0 0.0 copy-start.1
  23.0 0.0 copy-done.4
  23.0 0.0 copy-done.5
  23.0 0.0 copy-done.9
  23.0 0.0 copy-done.10
  23.0 0.0 copy-done.12
  23.0 0.2 shard_map.159
  23.2 10.7 %collective-permute-start = (f32[32,128]{1,0:T(8,128)S(1)}, f32[32,128]{1,0:T(8,128)S(1)}, u32[]{:S(2)}, u32[]{:S(2)}) collective-permute-start(f32[32,128]{1,0:T(8,128)S(1)} %get-tuple-element.36), channel_id=1, source_target_pairs={{1,2},{2,1},{3,4},{4,3},{5,6},{6,5},{7,8},{8,7},{9,10},{10,9},{11,... | collective-permute-start | bytes 49160 | tf_op jit(solution)/shard_map/ppermute | solution.py:437
  34.0 1.9 %collective-permute-start.1 = (f32[32,128]{1,0:T(8,128)S(1)}, f32[32,128]{1,0:T(8,128)S(1)}, u32[]{:S(2)}, u32[]{:S(2)}) collective-permute-start(f32[32,128]{1,0:T(8,128)S(1)} %get-tuple-element.37), channel_id=1, source_target_pairs={{0,1},{1,0},{2,3},{3,2},{4,5},{5,4},{6,7},{7,6},{8,9},{9,8},{10,11... | collective-permute-start | bytes 49160 | tf_op jit(solution)/shard_map/ppermute | solution.py:439
  35.9 1.9 %collective-permute-start.2 = (f32[32,64]{1,0:T(8,128)S(1)}, f32[32,64]{1,0:T(8,128)S(1)}, u32[]{:S(2)}, u32[]{:S(2)}) collective-permute-start(f32[32,64]{1,0:T(8,128)S(1)} %get-tuple-element.41.lists), channel_id=1, source_target_pairs={{0,64},{1,65},{2,66},{3,67},{4,68},{5,69},{6,70},{7,71},{8,72},{9,... | collective-permute-start | bytes 24584 | tf_op jit(solution)/shard_map/ppermute | solution.py:438
  37.8 0.0 copy-done.7
  37.9 0.0 copy-done.13
  37.9 0.0 copy-done.14
  37.9 0.6 shard_map.160
  38.5 0.0 collective-permute-done.odd
  38.5 0.0 collective-permute-done.1.even
  38.5 0.0 copy-done.2
  38.6 0.0 copy-done
  38.6 0.0 copy-done.1
  38.6 0.0 copy-start.6
  38.6 1.8 %shard_map.161 = (f32[528,128]{1,0:T(8,128)S(1)}, f32[528,128]{1,0:T(8,128)S(1)}, f32[528,128]{1,0:T(8,128)S(1)}, f32[4,128]{1,0:T(4,128)S(1)}) custom-call(f32[128,512]{1,0:T(8,128)S(1)} %bitcast.22, bf16[128,512]{1,0:T(8,128)(2,1)S(1)} %bitcast.25, bf16[128,512]{1,0:T(8,128)(2,1)S(1)} %bitcast.27, bf16[384,128]{1,0:T(8,128)(2,1)S(1)} %get-tuple-element.33.right, ...), custom_call_target="tpu_custom_call" | custom-call | tf_op jit(solution)/shard_map/pallas_call | solution.py:24
  40.4 0.0 copy-start.3
  40.4 15.3 %all-gather.2.surfaces = f32[4,4,128]{2,1,0:T(4,128)S(1)} all-gather(f32[1,4,128]{2,1,0:T(4,128)S(1)} %bitcast.39), channel_id=3, replica_groups=mesh['sec'=4,'tile'=128] {'sec'}, dimensions={0}, use_global_device_ids=true | all-gather | bytes 10240 | tf_op jit(solution)/shard_map/all_gather | solution.py:460
  55.7 0.2 shard_map.162
  55.9 5.2 %collective-permute-start.3 = (f32[8,128]{1,0:T(8,128)S(1)}, f32[8,128]{1,0:T(8,128)S(1)}, u32[]{:S(2)}, u32[]{:S(2)}) collective-permute-start(f32[8,128]{1,0:T(8,128)S(1)} %get-tuple-element.46), channel_id=1, source_target_pairs={{1,2},{2,1},{3,4},{4,3},{5,6},{6,5},{7,8},{8,7},{9,10},{10,9},{11,... | collective-permute-start | bytes 12296 | tf_op jit(solution)/shard_map/ppermute | solution.py:466
  61.1 0.0 copy-start.11
  61.1 1.9 %collective-permute-start.4 = (f32[8,128]{1,0:T(8,128)S(1)}, f32[8,128]{1,0:T(8,128)S(1)}, u32[]{:S(2)}, u32[]{:S(2)}) collective-permute-start(f32[8,128]{1,0:T(8,128)S(1)} %get-tuple-element.47), channel_id=1, source_target_pairs={{0,1},{1,0},{2,3},{3,2},{4,5},{5,4},{6,7},{7,6},{8,9},{9,8},{10,11... | collective-permute-start | bytes 12296 | tf_op jit(solution)/shard_map/ppermute | solution.py:467
  63.1 0.0 collective-permute-done.2.mirrored
  63.1 0.0 copy-done.6
  63.1 0.0 copy-done.3
  63.1 0.0 copy-done.11
  63.1 1.1 shard_map.163
  64.2 1.5 %collective-permute-done.3.odd = f32[8,128]{1,0:T(8,128)S(1)} collective-permute-done((f32[8,128]{1,0:T(8,128)S(1)}, f32[8,128]{1,0:T(8,128)S(1)}, u32[]{:S(2)}, u32[]{:S(2)}) %collective-permute-start.3) | collective-permute-done | bytes 4128 | tf_op jit(solution)/shard_map/ppermute | solution.py:466
  65.7 0.1 collective-permute-done.4.even
  65.8 2.7 %shard_map.164 = (f32[128,512]{1,0:T(8,128)}, f32[1024,128]{1,0:T(8,128)S(1)}) custom-call(f32[528,128]{1,0:T(8,128)S(1)} %get-tuple-element.38.window, f32[528,128]{1,0:T(8,128)S(1)} %get-tuple-element.39.rates, f32[528,128]{1,0:T(8,128)S(1)} %get-tuple-element.40.tend, bf16[384,128]{1,0:T(8,128)(2,1)S(1)} %get-tuple-element.33.right, ...), custom_call_target="tpu_custom_call" | custom-call | tf_op jit(solution)/shard_map/pallas_call | solution.py:24
  68.5 23.2 %all_to_all.10 = f32[64,16,128]{2,1,0:T(8,128)S(1)} all-to-all(f32[64,16,128]{2,1,0:T(8,128)S(1)} %bitcast.23), channel_id=1, replica_groups={{0,1,2,3,4,5,6,7,8,9,10,11,12,13,14,15,16,17,18,19,20,21,22,23,24,25,26..., dimensions={0} | all-to-all | bytes 1048576 | tf_op jit(solution)/shard_map/all_to_all | solution.py:486
  91.7 0.5 shard_map.165
  92.2 5.2 %collective-permute-start.5 = (f32[4,32,128]{2,1,0:T(8,128)S(1)}, f32[4,32,128]{2,1,0:T(8,128)S(1)}, u32[]{:S(2)}, u32[]{:S(2)}) collective-permute-start(f32[4,32,128]{2,1,0:T(8,128)S(1)} %get-tuple-element.58), channel_id=1, source_target_pairs={{0,128},{128,0},{256,384},{384,256},{1,129},{129,1},{257,385},{385... | collective-permute-start | bytes 196616 | tf_op jit(solution)/shard_map/ppermute | solution.py:498
  97.4 0.9 collective-permute-done.5
  98.3 0.0 copy-start.8
  98.3 16.9 %all_to_all.11.received = f32[4,32,128]{2,1,0:T(8,128)S(1)} all-to-all(f32[4,32,128]{2,1,0:T(8,128)S(1)} %add.3), channel_id=1, replica_groups={{0,64,256,320},{1,65,257,321},{2,66,258,322},{3,67,259,323},{4,68,260,3..., dimensions={0} | all-to-all | bytes 131072 | tf_op jit(solution)/shard_map/all_to_all | solution.py:499
  115.2 0.0 copy-done.8
  115.2 0.8 shard_map.166
  (1 shorter events, 0.0 us)
Async XLA Ops:
  0.6 22.4 %copy-start.4 = (s32[1,4,512]{2,1,0:T(4,128)S(1)}, s32[1,4,512]{2,1,0:T(4,128)}, u32[]{:S(2)}) copy-start(s32[1,4,512]{2,1,0:T(4,128)} %param.20) | copy-start | bytes 24580
  0.6 22.4 %copy-start.5 = (f32[1,4,512]{2,1,0:T(4,128)S(1)}, f32[1,4,512]{2,1,0:T(4,128)}, u32[]{:S(2)}) copy-start(f32[1,4,512]{2,1,0:T(4,128)} %param.21) | copy-start | bytes 24580
  0.7 22.3 %copy-start.9 = (s32[2,1,8,64]{3,2,1,0:T(8,128)S(1)}, s32[2,1,8,64]{3,2,1,0:T(8,128)}, u32[]{:S(2)}) copy-start(s32[2,1,8,64]{3,2,1,0:T(8,128)} %param.24) | copy-start | bytes 12292
  0.7 22.3 %copy-start.10 = (f32[2,1,8,64]{3,2,1,0:T(8,128)S(1)}, f32[2,1,8,64]{3,2,1,0:T(8,128)}, u32[]{:S(2)}) copy-start(f32[2,1,8,64]{3,2,1,0:T(8,128)} %param.25) | copy-start | bytes 12292
  0.7 22.3 %copy-start.12 = (s32[2,1,64]{2,1,0:T(1,128)S(1)}, s32[2,1,64]{2,1,0:T(1,128)}, u32[]{:S(2)}) copy-start(s32[2,1,64]{2,1,0:T(1,128)} %param.26) | copy-start | bytes 1540
  0.7 37.2 %copy-start.7 = (f32[1,128,128]{2,1,0:T(8,128)S(1)}, f32[1,128,128]{2,1,0:T(8,128)}, u32[]{:S(2)}) copy-start(f32[1,128,128]{2,1,0:T(8,128)} %param.18) | copy-start | bytes 196612
  0.7 37.9 %copy-start.2 = (bf16[1,128,512]{2,1,0:T(8,128)(2,1)S(1)}, bf16[1,128,512]{2,1,0:T(8,128)(2,1)}, u32[]{:S(2)}) copy-start(bf16[1,128,512]{2,1,0:T(8,128)(2,1)} %param.17) | copy-start | bytes 393220
  2.0 35.9 %copy-start.13 = (s32[4]{0:T(128)S(1)}, s32[4]{0:T(128)}, u32[]{:S(2)}) copy-start(s32[4]{0:T(128)} %active.1) | copy-start | bytes 52
  2.0 35.9 %copy-start.14 = (f32[1,128]{1,0:T(1,128)S(1)}, f32[1,128]{1,0:T(1,128)}, u32[]{:S(2)}) copy-start(f32[1,128]{1,0:T(1,128)} %coupling.1) | copy-start | bytes 1540
  2.0 36.6 %copy-start = (f32[1,128,512]{2,1,0:T(8,128)S(1)}, f32[1,128,512]{2,1,0:T(8,128)}, u32[]{:S(2)}) copy-start(f32[1,128,512]{2,1,0:T(8,128)} %param.15) | copy-start | bytes 786436
  23.0 15.6 %copy-start.1 = (bf16[1,128,512]{2,1,0:T(8,128)(2,1)S(1)}, bf16[1,128,512]{2,1,0:T(8,128)(2,1)}, u32[]{:S(2)}) copy-start(bf16[1,128,512]{2,1,0:T(8,128)(2,1)} %param.16) | copy-start | bytes 393220
  23.2 15.3 %collective-permute-start = (f32[32,128]{1,0:T(8,128)S(1)}, f32[32,128]{1,0:T(8,128)S(1)}, u32[]{:S(2)}, u32[]{:S(2)}) collective-permute-start(f32[32,128]{1,0:T(8,128)S(1)} %get-tuple-element.36), channel_id=1, source_target_pairs={{1,2},{2,1},{3,4},{4,3},{5,6},{6,5},{7,8},{8,7},{9,10},{10,9},{11,... | collective-permute-start | bytes 49160 | tf_op jit(solution)/shard_map/ppermute | solution.py:437
  34.0 4.5 %collective-permute-start.1 = (f32[32,128]{1,0:T(8,128)S(1)}, f32[32,128]{1,0:T(8,128)S(1)}, u32[]{:S(2)}, u32[]{:S(2)}) collective-permute-start(f32[32,128]{1,0:T(8,128)S(1)} %get-tuple-element.37), channel_id=1, source_target_pairs={{0,1},{1,0},{2,3},{3,2},{4,5},{5,4},{6,7},{7,6},{8,9},{9,8},{10,11... | collective-permute-start | bytes 49160 | tf_op jit(solution)/shard_map/ppermute | solution.py:439
  35.9 27.1 %collective-permute-start.2 = (f32[32,64]{1,0:T(8,128)S(1)}, f32[32,64]{1,0:T(8,128)S(1)}, u32[]{:S(2)}, u32[]{:S(2)}) collective-permute-start(f32[32,64]{1,0:T(8,128)S(1)} %get-tuple-element.41.lists), channel_id=1, source_target_pairs={{0,64},{1,65},{2,66},{3,67},{4,68},{5,69},{6,70},{7,71},{8,72},{9,... | collective-permute-start | bytes 24584 | tf_op jit(solution)/shard_map/ppermute | solution.py:438
  38.6 24.5 %copy-start.6 = (f32[1,128,128]{2,1,0:T(8,128)S(1)}, f32[1,128,128]{2,1,0:T(8,128)}, u32[]{:S(2)}) copy-start(f32[1,128,128]{2,1,0:T(8,128)} %param.27) | copy-start | bytes 196612
  40.4 22.7 %copy-start.3 = (f32[128,256]{1,0:T(8,128)S(1)}, f32[128,256]{1,0:T(8,128)}, u32[]{:S(2)}) copy-start(f32[128,256]{1,0:T(8,128)} %abel.1) | copy-start | bytes 393220
  55.9 9.8 %collective-permute-start.3 = (f32[8,128]{1,0:T(8,128)S(1)}, f32[8,128]{1,0:T(8,128)S(1)}, u32[]{:S(2)}, u32[]{:S(2)}) collective-permute-start(f32[8,128]{1,0:T(8,128)S(1)} %get-tuple-element.46), channel_id=1, source_target_pairs={{1,2},{2,1},{3,4},{4,3},{5,6},{6,5},{7,8},{8,7},{9,10},{10,9},{11,... | collective-permute-start | bytes 12296 | tf_op jit(solution)/shard_map/ppermute | solution.py:466
  61.1 2.0 %copy-start.11 = (s32[2,1,1,128,4]{3,4,2,1,0:T(4,128)S(1)}, s32[2,1,1,128,4]{3,4,2,1,0:T(4,128)}, u32[]{:S(2)}) copy-start(s32[2,1,1,128,4]{3,4,2,1,0:T(4,128)} %param.23) | copy-start | bytes 12292
  61.1 4.6 %collective-permute-start.4 = (f32[8,128]{1,0:T(8,128)S(1)}, f32[8,128]{1,0:T(8,128)S(1)}, u32[]{:S(2)}, u32[]{:S(2)}) collective-permute-start(f32[8,128]{1,0:T(8,128)S(1)} %get-tuple-element.47), channel_id=1, source_target_pairs={{0,1},{1,0},{2,3},{3,2},{4,5},{5,4},{6,7},{7,6},{8,9},{9,8},{10,11... | collective-permute-start | bytes 12296 | tf_op jit(solution)/shard_map/ppermute | solution.py:467
  92.2 6.1 %collective-permute-start.5 = (f32[4,32,128]{2,1,0:T(8,128)S(1)}, f32[4,32,128]{2,1,0:T(8,128)S(1)}, u32[]{:S(2)}, u32[]{:S(2)}) collective-permute-start(f32[4,32,128]{2,1,0:T(8,128)S(1)} %get-tuple-element.58), channel_id=1, source_target_pairs={{0,128},{128,0},{256,384},{384,256},{1,129},{129,1},{257,385},{385... | collective-permute-start | bytes 196616 | tf_op jit(solution)/shard_map/ppermute | solution.py:498
  98.3 16.9 %copy-start.8 = (f32[2,16,256]{2,1,0:T(8,128)S(1)}, f32[2,16,256]{2,1,0:T(8,128)}, u32[]{:S(2)}) copy-start(f32[2,16,256]{2,1,0:T(8,128)} %observed.1) | copy-start | bytes 98308

commit v7 on v6

--- a/solution.py
+++ b/solution.py
@@ -246,6 +246,16 @@
     return [both[m * tiles : (m + 1) * tiles] for m in range(4)]
 
 
+def place(parcels, period, picked):
+    slots = len(picked)
+    part = picked[0].shape[0] // PARTS
+    width = PARTS * STEPS * slots
+    for m, rows in enumerate(picked):
+        for o in range(PARTS):
+            first = (o * STEPS + period) * slots + m
+            parcels[pl.ds(first, part, stride=width), :] = rows[o * part : (o + 1) * part]
+
+
 def step_first(
     state, tendency, diffusion, right, response, alive, boundary, odd, even,
     window, rates_out, forcing_out, surface,
@@ -266,24 +276,21 @@
 
 def step_second(
     window, rates, tend, right, response, alive, hits, boundary, odd, even, earlier,
-    final, parcels,
+    last, parcels,
 ):
     edge = edge_row(*sides(odd, even, 0, 1))
     constant = forcing(response[0:1, :], boundary, edge, tend[...])
     field = advance(window[...], rates[...], constant, right[...], alive)
-    columns = final.shape[1]
-    slots, tiles, _ = earlier.shape
-    part = tiles // PARTS
-    width = PARTS * STEPS * slots
-    for m, later in enumerate(chosen(field[:columns], hits[...])):
-        for o in range(PARTS):
-            for p, rows in enumerate((earlier[m], later)):
-                first = (o * STEPS + p) * slots + m
-                owned = rows[o * part : (o + 1) * part]
-                parcels[pl.ds(first, part, stride=width), :] = owned
-    for j in range(columns // LANES):
+    own = field[: last.shape[0]]
+    last[...] = own
+    parcels[...] = earlier[...]
+    place(parcels, 1, chosen(own, hits[...]))
+
+
+def finish(last, final):
+    for j in range(final.shape[1] // LANES):
         cut = slice(j * LANES, (j + 1) * LANES)
-        final[:, cut] = field[cut].T
+        final[:, cut] = last[cut, :].T
 
 
 def ready_first(active, mixing, coupling, right, response, alive):
@@ -297,15 +304,12 @@
 
 
 def ready_second(
-    listed, window, lists, mirrored, refraction, abel, hits, parcel, spread, right, right_abel
+    listed, window, lists, mirrored, refraction, abel, hits, parcels, spread, right, right_abel
 ):
     columns = hits.shape[1]
-    slots = parcel.shape[0]
+    slots = listed.shape[1]
     places = jnp.concatenate([listed[p] for p in range(STEPS)], axis=0).T
-    for m, rows in enumerate(
-        chosen(window[0:columns, :], one_hot(places[:, :slots], columns))
-    ):
-        parcel[m] = rows
+    place(parcels, 0, chosen(window[0:columns, :], one_hot(places[:, :slots], columns)))
     hits[...] = one_hot(places[:, slots : 2 * slots], columns)
     right[...] = right_operand(refraction[...])
     right_abel[...] = right_operand(abel[...])
@@ -313,7 +317,7 @@
     ranks = lists.shape[0] // (2 * STEPS)
     part = width // 4
     here = jnp.where(lax.axis_index("tile") >= part, 1, 0)
-    place = lane_ids((occultations, width))
+    position = lane_ids((occultations, width))
     for o in range(PARTS):
         owned = jnp.where(here == o, lists[...], mirrored[...])
         for p in range(STEPS):
@@ -324,7 +328,7 @@
             key = jnp.where(inside, (slot & 3) * part + source, -1).T
             total = jnp.zeros((occultations, width), f32)
             for k in range(ranks):
-                hit = key[:, k : k + 1] == place
+                hit = key[:, k : k + 1] == position
                 total = total + jnp.where(hit, live[:, k : k + 1], 0.0)
             spread[o, p] = left_operand(total)
 
@@ -466,21 +470,21 @@
     odd = lax.ppermute(odd, AXES, above_odd)
     even = lax.ppermute(even, AXES, above_even)
     mirrored, _ = after((mirrored, boundary))
-    hits, parcel, spread, refract, bend = call(
+    hits, parcels, spread, refract, bend = call(
         ready_second,
         (
             shape((4 * tiles, columns), bf16),
-            shape((4, tiles, levels), f32),
+            shape((8 * tiles, levels), f32),
             shape((PARTS, STEPS, owned, 12 * part), bf16),
             shape((3 * levels, levels), bf16),
             shape((3 * levels, heights), bf16),
         ),
         listed, window, lists, mirrored, refraction[0], abel_matrix,
     )
-    final, parcels = call(
+    last, parcels = call(
         step_second,
-        (shape((levels, columns), f32), shape((8 * tiles, levels), f32)),
-        window, rates, tend, right, response, alive, hits, boundary, odd, even, parcel,
+        (shape((columns, levels), f32), shape((8 * tiles, levels), f32)),
+        window, rates, tend, right, response, alive, hits, boundary, odd, even, parcels,
     )
     parcels, spread, refract, bend = after((parcels, spread, refract, bend))
     arrived = lax.all_to_all(
@@ -496,6 +500,9 @@
         project, (block, block), arrived.reshape(8 * PARTS * part, levels), spread, refract
     )
     got = lax.ppermute(sent, "sec", [(s, s ^ 1) for s in range(sections)])
+    last, _ = after((last, kept))
+    final = call(finish, shape((levels, columns), f32), last)
+    got, final = after((got, final))
     received = lax.all_to_all(
         kept + got,
         AXES,

time: 116 us -> 116 us (level)
    pallas_call x9 -> x10, Pallas kernels: 9.12 us -> 9.21 us  [call(): pl.pallas_call(body, out_shape=outs if single else tuple(outs), in_specs=...]
  transfers between devices with their start and end apart: 6 -> 6, of which waited for: 3 -> 2; matrix products, arithmetic and copies ran while one was open for 0% -> 0% of each run, Pallas kernels for 3% -> 4%
where the time goes in v7:
time: 116 us; the launch traced here: 115 us
  blocking collectives  76.4 us (66%)
  starting transfers between devices  26.9 us (23%)
  Pallas kernels  9.21 us (8%)
  waiting for transfers between devices  1.59 us (1%)
    all_to_all x1, blocking collectives, shards(): lax.all_to_all(parcels.reshape(part, 8 * PARTS, levels), 'tile', split_ax...  23.3 us
    all_gather x1, blocking collectives, shards(): shared = lax.all_gather(edges, 'sec', axis=0, tiled=False)  21 us
    all_to_all x1, blocking collectives, shards(): lax.all_to_all(kept + got, AXES, split_axis=0, concat_axis=0, axis_index_...  16.9 us
    ppermute x2, starting transfers between devices, shards(): odd = lax.ppermute(odd, AXES, above_odd)  16 us
    all_gather x1, blocking collectives, shards(): surfaces = lax.all_gather(surface, 'sec', axis=0, tiled=False)  15.3 us
    pallas_call x10, Pallas kernels, call(): pl.pallas_call(body, out_shape=outs if single else tuple(outs), in_specs=...  9.21 us
    ppermute x1, starting transfers between devices, shards(): got = lax.ppermute(sent, 'sec', [(s, s ^ 1) for s in range(sections)])  5.2 us
    ppermute x2, starting transfers between devices, shards(): even = lax.ppermute(even, AXES, above_even)  3.84 us
  transfers between devices with their start and end apart: 6, of which 2 were waited for; matrix products, arithmetic and copies ran while one was open for 0% of the time, Pallas kernels for 4%

profile of v7, /device:TPU:1, one launch (start us, length us, event | category | flops | bytes accessed | tf_op | source)
XLA Modules:
  0.0 115.2 jit_solution(7684075062132925130)
XLA Ops:
  0.6 0.0 copy-start.4
  0.6 0.0 copy-start.5
  0.7 0.0 copy-start.9
  0.7 0.0 copy-start.10
  0.7 0.0 copy-start.12
  0.7 0.0 copy-start.7
  0.7 0.0 copy-start.2
  0.7 1.3 %shard_map.158 = f32[64,128]{1,0:T(8,128)S(1)} custom-call(f32[128,512]{1,0:T(8,128)} %bitcast.21, bf16[128,512]{1,0:T(8,128)(2,1)} %bitcast.24, bf16[128,512]{1,0:T(8,128)(2,1)} %bitcast.26, s32[4,512]{1,0:T(4,128)} %bitcast.28, f32[4,512]{1,0:T(4,128)} %bitcast.31), custom_call_target="tpu_custom_call" | custom-call | tf_op jit(solution)/shard_map/pallas_call | solution.py:24
  2.0 0.0 copy-start.13
  2.0 0.0 copy-start.14
  2.0 0.0 copy-start
  2.0 21.0 %all-gather = f32[256,128]{1,0:T(8,128)S(1)} all-gather(f32[64,128]{1,0:T(8,128)S(1)} %shard_map.158), channel_id=2, replica_groups=mesh['sec'=4,'tile'=128] {'sec'}, dimensions={0}, use_global_device_ids=true | all-gather | bytes 163840 | tf_op jit(solution)/shard_map/all_gather | solution.py:430
  23.0 0.0 copy-start.1
  23.0 0.0 copy-done.4
  23.0 0.0 copy-done.5
  23.0 0.0 copy-done.9
  23.0 0.0 copy-done.10
  23.0 0.0 copy-done.12
  23.0 0.2 shard_map.159
  23.2 10.7 %collective-permute-start = (f32[32,128]{1,0:T(8,128)S(1)}, f32[32,128]{1,0:T(8,128)S(1)}, u32[]{:S(2)}, u32[]{:S(2)}) collective-permute-start(f32[32,128]{1,0:T(8,128)S(1)} %get-tuple-element.39), channel_id=1, source_target_pairs={{1,2},{2,1},{3,4},{4,3},{5,6},{6,5},{7,8},{8,7},{9,10},{10,9},{11,... | collective-permute-start | bytes 49160 | tf_op jit(solution)/shard_map/ppermute | solution.py:441
  34.0 1.9 %collective-permute-start.1 = (f32[32,128]{1,0:T(8,128)S(1)}, f32[32,128]{1,0:T(8,128)S(1)}, u32[]{:S(2)}, u32[]{:S(2)}) collective-permute-start(f32[32,128]{1,0:T(8,128)S(1)} %get-tuple-element.40), channel_id=1, source_target_pairs={{0,1},{1,0},{2,3},{3,2},{4,5},{5,4},{6,7},{7,6},{8,9},{9,8},{10,11... | collective-permute-start | bytes 49160 | tf_op jit(solution)/shard_map/ppermute | solution.py:443
  35.9 1.9 %collective-permute-start.2 = (f32[32,64]{1,0:T(8,128)S(1)}, f32[32,64]{1,0:T(8,128)S(1)}, u32[]{:S(2)}, u32[]{:S(2)}) collective-permute-start(f32[32,64]{1,0:T(8,128)S(1)} %get-tuple-element.44.lists), channel_id=1, source_target_pairs={{0,64},{1,65},{2,66},{3,67},{4,68},{5,69},{6,70},{7,71},{8,72},{9,... | collective-permute-start | bytes 24584 | tf_op jit(solution)/shard_map/ppermute | solution.py:442
  37.8 0.0 copy-done.7
  37.9 0.0 copy-done.13
  37.9 0.0 copy-done.14
  37.9 0.6 shard_map.160
  38.5 0.0 collective-permute-done.odd
  38.5 0.0 collective-permute-done.1.even
  38.5 0.0 copy-done.2
  38.6 0.0 copy-done
  38.6 0.0 copy-done.1
  38.6 0.0 copy-start.6
  38.6 1.8 %shard_map.161 = (f32[528,128]{1,0:T(8,128)S(1)}, f32[528,128]{1,0:T(8,128)S(1)}, f32[528,128]{1,0:T(8,128)S(1)}, f32[4,128]{1,0:T(4,128)S(1)}) custom-call(f32[128,512]{1,0:T(8,128)S(1)} %bitcast.22, bf16[128,512]{1,0:T(8,128)(2,1)S(1)} %bitcast.25, bf16[128,512]{1,0:T(8,128)(2,1)S(1)} %bitcast.27, bf16[384,128]{1,0:T(8,128)(2,1)S(1)} %get-tuple-element.36.right, ...), custom_call_target="tpu_custom_call" | custom-call | tf_op jit(solution)/shard_map/pallas_call | solution.py:24
  40.4 0.0 copy-start.3
  40.4 15.3 %all-gather.2.surfaces = f32[4,4,128]{2,1,0:T(4,128)S(1)} all-gather(f32[1,4,128]{2,1,0:T(4,128)S(1)} %bitcast.39), channel_id=3, replica_groups=mesh['sec'=4,'tile'=128] {'sec'}, dimensions={0}, use_global_device_ids=true | all-gather | bytes 10240 | tf_op jit(solution)/shard_map/all_gather | solution.py:464
  55.7 0.2 shard_map.162
  55.9 5.2 %collective-permute-start.3 = (f32[8,128]{1,0:T(8,128)S(1)}, f32[8,128]{1,0:T(8,128)S(1)}, u32[]{:S(2)}, u32[]{:S(2)}) collective-permute-start(f32[8,128]{1,0:T(8,128)S(1)} %get-tuple-element.49), channel_id=1, source_target_pairs={{1,2},{2,1},{3,4},{4,3},{5,6},{6,5},{7,8},{8,7},{9,10},{10,9},{11,... | collective-permute-start | bytes 12296 | tf_op jit(solution)/shard_map/ppermute | solution.py:470
  61.1 0.0 copy-start.11
  61.1 1.9 %collective-permute-start.4 = (f32[8,128]{1,0:T(8,128)S(1)}, f32[8,128]{1,0:T(8,128)S(1)}, u32[]{:S(2)}, u32[]{:S(2)}) collective-permute-start(f32[8,128]{1,0:T(8,128)S(1)} %get-tuple-element.50), channel_id=1, source_target_pairs={{0,1},{1,0},{2,3},{3,2},{4,5},{5,4},{6,7},{7,6},{8,9},{9,8},{10,11... | collective-permute-start | bytes 12296 | tf_op jit(solution)/shard_map/ppermute | solution.py:471
  63.1 0.0 collective-permute-done.2.mirrored
  63.1 0.0 copy-done.6
  63.1 0.0 copy-done.3
  63.1 0.0 copy-done.11
  63.1 1.1 shard_map.163
  64.2 1.4 %collective-permute-done.3.odd = f32[8,128]{1,0:T(8,128)S(1)} collective-permute-done((f32[8,128]{1,0:T(8,128)S(1)}, f32[8,128]{1,0:T(8,128)S(1)}, u32[]{:S(2)}, u32[]{:S(2)}) %collective-permute-start.3) | collective-permute-done | bytes 4128 | tf_op jit(solution)/shard_map/ppermute | solution.py:470
  65.7 0.1 collective-permute-done.4.even
  65.8 1.9 %shard_map.164 = (f32[512,128]{1,0:T(8,128)S(1)}, f32[1024,128]{1,0:T(8,128)S(1)}) custom-call(f32[528,128]{1,0:T(8,128)S(1)} %get-tuple-element.41.window, f32[528,128]{1,0:T(8,128)S(1)} %get-tuple-element.42.rates, f32[528,128]{1,0:T(8,128)S(1)} %get-tuple-element.43.tend, bf16[384,128]{1,0:T(8,128)(2,1)S(1)} %get-tuple-element.36.right, ...), custom_call_target="tpu_custom_call" | custom-call | tf_op jit(solution)/shard_map/pallas_call | solution.py:24
  67.7 23.3 %all_to_all.10 = f32[64,16,128]{2,1,0:T(8,128)S(1)} all-to-all(f32[64,16,128]{2,1,0:T(8,128)S(1)} %bitcast.23), channel_id=1, replica_groups={{0,1,2,3,4,5,6,7,8,9,10,11,12,13,14,15,16,17,18,19,20,21,22,23,24,25,26..., dimensions={0} | all-to-all | bytes 1048576 | tf_op jit(solution)/shard_map/all_to_all | solution.py:490
  91.0 0.5 shard_map.165
  91.4 5.2 %collective-permute-start.5 = (f32[4,32,128]{2,1,0:T(8,128)S(1)}, f32[4,32,128]{2,1,0:T(8,128)S(1)}, u32[]{:S(2)}, u32[]{:S(2)}) collective-permute-start(f32[4,32,128]{2,1,0:T(8,128)S(1)} %get-tuple-element.59), channel_id=1, source_target_pairs={{0,128},{128,0},{256,384},{384,256},{1,129},{129,1},{257,385},{385... | collective-permute-start | bytes 196616 | tf_op jit(solution)/shard_map/ppermute | solution.py:502
  96.6 0.8 shard_map.166
  97.5 0.0 collective-permute-done.5
  97.5 0.0 copy-start.8
  97.5 16.9 %all_to_all.11.received = f32[4,32,128]{2,1,0:T(8,128)S(1)} all-to-all(f32[4,32,128]{2,1,0:T(8,128)S(1)} %add.3), channel_id=1, replica_groups={{0,64,256,320},{1,65,257,321},{2,66,258,322},{3,67,259,323},{4,68,260,3..., dimensions={0} | all-to-all | bytes 131072 | tf_op jit(solution)/shard_map/all_to_all | solution.py:506
  114.4 0.0 copy-done.8
  114.4 0.8 shard_map.167
  (1 shorter events, 0.0 us)
Async XLA Ops:
  0.6 22.4 %copy-start.4 = (s32[1,4,512]{2,1,0:T(4,128)S(1)}, s32[1,4,512]{2,1,0:T(4,128)}, u32[]{:S(2)}) copy-start(s32[1,4,512]{2,1,0:T(4,128)} %param.20) | copy-start | bytes 24580
  0.6 22.4 %copy-start.5 = (f32[1,4,512]{2,1,0:T(4,128)S(1)}, f32[1,4,512]{2,1,0:T(4,128)}, u32[]{:S(2)}) copy-start(f32[1,4,512]{2,1,0:T(4,128)} %param.21) | copy-start | bytes 24580
  0.7 22.3 %copy-start.9 = (s32[2,1,8,64]{3,2,1,0:T(8,128)S(1)}, s32[2,1,8,64]{3,2,1,0:T(8,128)}, u32[]{:S(2)}) copy-start(s32[2,1,8,64]{3,2,1,0:T(8,128)} %param.24) | copy-start | bytes 12292
  0.7 22.3 %copy-start.10 = (f32[2,1,8,64]{3,2,1,0:T(8,128)S(1)}, f32[2,1,8,64]{3,2,1,0:T(8,128)}, u32[]{:S(2)}) copy-start(f32[2,1,8,64]{3,2,1,0:T(8,128)} %param.25) | copy-start | bytes 12292
  0.7 22.3 %copy-start.12 = (s32[2,1,64]{2,1,0:T(1,128)S(1)}, s32[2,1,64]{2,1,0:T(1,128)}, u32[]{:S(2)}) copy-start(s32[2,1,64]{2,1,0:T(1,128)} %param.26) | copy-start | bytes 1540
  0.7 37.2 %copy-start.7 = (f32[1,128,128]{2,1,0:T(8,128)S(1)}, f32[1,128,128]{2,1,0:T(8,128)}, u32[]{:S(2)}) copy-start(f32[1,128,128]{2,1,0:T(8,128)} %param.18) | copy-start | bytes 196612
  0.7 37.9 %copy-start.2 = (bf16[1,128,512]{2,1,0:T(8,128)(2,1)S(1)}, bf16[1,128,512]{2,1,0:T(8,128)(2,1)}, u32[]{:S(2)}) copy-start(bf16[1,128,512]{2,1,0:T(8,128)(2,1)} %param.17) | copy-start | bytes 393220
  2.0 35.9 %copy-start.13 = (s32[4]{0:T(128)S(1)}, s32[4]{0:T(128)}, u32[]{:S(2)}) copy-start(s32[4]{0:T(128)} %active.1) | copy-start | bytes 52
  2.0 35.9 %copy-start.14 = (f32[1,128]{1,0:T(1,128)S(1)}, f32[1,128]{1,0:T(1,128)}, u32[]{:S(2)}) copy-start(f32[1,128]{1,0:T(1,128)} %coupling.1) | copy-start | bytes 1540
  2.0 36.6 %copy-start = (f32[1,128,512]{2,1,0:T(8,128)S(1)}, f32[1,128,512]{2,1,0:T(8,128)}, u32[]{:S(2)}) copy-start(f32[1,128,512]{2,1,0:T(8,128)} %param.15) | copy-start | bytes 786436
  23.0 15.6 %copy-start.1 = (bf16[1,128,512]{2,1,0:T(8,128)(2,1)S(1)}, bf16[1,128,512]{2,1,0:T(8,128)(2,1)}, u32[]{:S(2)}) copy-start(bf16[1,128,512]{2,1,0:T(8,128)(2,1)} %param.16) | copy-start | bytes 393220
  23.2 15.3 %collective-permute-start = (f32[32,128]{1,0:T(8,128)S(1)}, f32[32,128]{1,0:T(8,128)S(1)}, u32[]{:S(2)}, u32[]{:S(2)}) collective-permute-start(f32[32,128]{1,0:T(8,128)S(1)} %get-tuple-element.39), channel_id=1, source_target_pairs={{1,2},{2,1},{3,4},{4,3},{5,6},{6,5},{7,8},{8,7},{9,10},{10,9},{11,... | collective-permute-start | bytes 49160 | tf_op jit(solution)/shard_map/ppermute | solution.py:441
  34.0 4.5 %collective-permute-start.1 = (f32[32,128]{1,0:T(8,128)S(1)}, f32[32,128]{1,0:T(8,128)S(1)}, u32[]{:S(2)}, u32[]{:S(2)}) collective-permute-start(f32[32,128]{1,0:T(8,128)S(1)} %get-tuple-element.40), channel_id=1, source_target_pairs={{0,1},{1,0},{2,3},{3,2},{4,5},{5,4},{6,7},{7,6},{8,9},{9,8},{10,11... | collective-permute-start | bytes 49160 | tf_op jit(solution)/shard_map/ppermute | solution.py:443
  35.9 27.1 %collective-permute-start.2 = (f32[32,64]{1,0:T(8,128)S(1)}, f32[32,64]{1,0:T(8,128)S(1)}, u32[]{:S(2)}, u32[]{:S(2)}) collective-permute-start(f32[32,64]{1,0:T(8,128)S(1)} %get-tuple-element.44.lists), channel_id=1, source_target_pairs={{0,64},{1,65},{2,66},{3,67},{4,68},{5,69},{6,70},{7,71},{8,72},{9,... | collective-permute-start | bytes 24584 | tf_op jit(solution)/shard_map/ppermute | solution.py:442
  38.6 24.5 %copy-start.6 = (f32[1,128,128]{2,1,0:T(8,128)S(1)}, f32[1,128,128]{2,1,0:T(8,128)}, u32[]{:S(2)}) copy-start(f32[1,128,128]{2,1,0:T(8,128)} %param.27) | copy-start | bytes 196612
  40.4 22.7 %copy-start.3 = (f32[128,256]{1,0:T(8,128)S(1)}, f32[128,256]{1,0:T(8,128)}, u32[]{:S(2)}) copy-start(f32[128,256]{1,0:T(8,128)} %abel.1) | copy-start | bytes 393220
  55.9 9.8 %collective-permute-start.3 = (f32[8,128]{1,0:T(8,128)S(1)}, f32[8,128]{1,0:T(8,128)S(1)}, u32[]{:S(2)}, u32[]{:S(2)}) collective-permute-start(f32[8,128]{1,0:T(8,128)S(1)} %get-tuple-element.49), channel_id=1, source_target_pairs={{1,2},{2,1},{3,4},{4,3},{5,6},{6,5},{7,8},{8,7},{9,10},{10,9},{11,... | collective-permute-start | bytes 12296 | tf_op jit(solution)/shard_map/ppermute | solution.py:470
  61.1 2.0 %copy-start.11 = (s32[2,1,1,128,4]{3,4,2,1,0:T(4,128)S(1)}, s32[2,1,1,128,4]{3,4,2,1,0:T(4,128)}, u32[]{:S(2)}) copy-start(s32[2,1,1,128,4]{3,4,2,1,0:T(4,128)} %param.23) | copy-start | bytes 12292
  61.1 4.6 %collective-permute-start.4 = (f32[8,128]{1,0:T(8,128)S(1)}, f32[8,128]{1,0:T(8,128)S(1)}, u32[]{:S(2)}, u32[]{:S(2)}) collective-permute-start(f32[8,128]{1,0:T(8,128)S(1)} %get-tuple-element.50), channel_id=1, source_target_pairs={{0,1},{1,0},{2,3},{3,2},{4,5},{5,4},{6,7},{7,6},{8,9},{9,8},{10,11... | collective-permute-start | bytes 12296 | tf_op jit(solution)/shard_map/ppermute | solution.py:471
  91.4 6.1 %collective-permute-start.5 = (f32[4,32,128]{2,1,0:T(8,128)S(1)}, f32[4,32,128]{2,1,0:T(8,128)S(1)}, u32[]{:S(2)}, u32[]{:S(2)}) collective-permute-start(f32[4,32,128]{2,1,0:T(8,128)S(1)} %get-tuple-element.59), channel_id=1, source_target_pairs={{0,128},{128,0},{256,384},{384,256},{1,129},{129,1},{257,385},{385... | collective-permute-start | bytes 196616 | tf_op jit(solution)/shard_map/ppermute | solution.py:502
  97.5 16.9 %copy-start.8 = (f32[2,16,256]{2,1,0:T(8,128)S(1)}, f32[2,16,256]{2,1,0:T(8,128)}, u32[]{:S(2)}) copy-start(f32[2,16,256]{2,1,0:T(8,128)} %observed.1) | copy-start | bytes 98308

commit v8 on v7

--- a/solution.py
+++ b/solution.py
@@ -206,9 +206,12 @@
     return [x[:, j * LANES : (j + 1) * LANES].T for j in range(x.shape[1] // LANES)]
 
 
-def advance(field, rates, constant, right, alive):
+def advance(field, rates, constant, right, live_limit):
     count = field.shape[0]
-    live = alive[...] > 0.0
+    row = lax.broadcasted_iota(jnp.int32, field.shape, 0)
+    columns = count - 2 * HALO
+    column = jnp.where(row < columns, row, row - columns)
+    live = jnp.where(row < columns + HALO, column, row - 2 * HALO) < live_limit
     for _ in range(SUBS):
         near = pltpu.roll(field, 1, 0) + pltpu.roll(field, count - 1, 0)
         spread = field + rates * (near - 2.0 * field)
@@ -257,9 +260,11 @@
 
 
 def step_first(
-    state, tendency, diffusion, right, response, alive, boundary, odd, even,
-    window, rates_out, forcing_out, surface,
+    active, state, tendency, diffusion, mixing, coupling, boundary, odd, even,
+    window, rates_out, forcing_out, surface, right, response,
 ):
+    right[...] = right_operand(mixing[...].T)
+    response[...] = jnp.broadcast_to(coupling[...], response.shape)
     rates = jnp.concatenate(turned(diffusion[...]) + [halo_rows(odd, even, 8)], axis=0)
     tend = jnp.concatenate(turned(tendency[...]) + [halo_rows(odd, even, 16)], axis=0)
     field = jnp.concatenate(turned(state[...]) + [halo_rows(odd, even, 0)], axis=0)
@@ -267,7 +272,7 @@
     constant = forcing(response[0:1, :], boundary, edge, tend)
     rates_out[...] = rates
     forcing_out[...] = tend
-    field = advance(field, rates, constant, right[...], alive)
+    field = advance(field, rates, constant, right[...], active[lax.axis_index("sec")])
     window[...] = field
     for j in range(surface.shape[0]):
         block = field[j * LANES : (j + 1) * LANES].T
@@ -275,12 +280,13 @@
 
 
 def step_second(
-    window, rates, tend, right, response, alive, hits, boundary, odd, even, earlier,
+    active, window, rates, tend, right, response, hits, boundary, odd, even, earlier,
     last, parcels,
 ):
     edge = edge_row(*sides(odd, even, 0, 1))
     constant = forcing(response[0:1, :], boundary, edge, tend[...])
-    field = advance(window[...], rates[...], constant, right[...], alive)
+    live_limit = active[lax.axis_index("sec")]
+    field = advance(window[...], rates[...], constant, right[...], live_limit)
     own = field[: last.shape[0]]
     last[...] = own
     parcels[...] = earlier[...]
@@ -291,16 +297,6 @@
     for j in range(final.shape[1] // LANES):
         cut = slice(j * LANES, (j + 1) * LANES)
         final[:, cut] = last[cut, :].T
-
-
-def ready_first(active, mixing, coupling, right, response, alive):
-    right[...] = right_operand(mixing[...].T)
-    response[...] = jnp.broadcast_to(coupling[...], response.shape)
-    row = lax.broadcasted_iota(jnp.int32, alive.shape, 0)
-    columns = alive.shape[0] - 2 * HALO
-    column = jnp.where(row < columns, row, row - columns)
-    column = jnp.where(row < columns + HALO, column, row - 2 * HALO)
-    alive[...] = jnp.where(column < active[lax.axis_index("sec")], 1.0, 0.0)
 
 
 def ready_second(
@@ -441,25 +437,17 @@
     odd = lax.ppermute(odd, AXES, above_odd)
     mirrored = lax.ppermute(lists, "tile", [(t, (t + part) % tiles) for t in range(tiles)])
     even = lax.ppermute(even, AXES, above_even)
-    mixing_row, _ = after((mixing[0], boundary))
-    right, response, alive = call(
-        ready_first,
-        (
-            shape((3 * levels, levels), bf16),
-            shape((8, levels), f32),
-            shape((width, levels), f32),
-        ),
-        active_cols, mixing_row, coupling,
-    )
-    window, rates, tend, surface = call(
+    window, rates, tend, surface, right, response = call(
         step_first,
         (
             shape((width, levels), f32),
             shape((width, levels), f32),
             shape((width, levels), f32),
             shape((columns // LANES, LANES), f32),
+            shape((3 * levels, levels), bf16),
+            shape((8, levels), f32),
         ),
-        state[0], tendency[0], diffusion[0], right, response, alive, boundary, odd, even,
+        active_cols, state[0], tendency[0], diffusion[0], mixing[0], coupling, boundary, odd, even,
     )
     surfaces = lax.all_gather(surface, "sec", axis=0, tiled=False)
     boundary, odd, even = call(
@@ -484,7 +472,7 @@
     last, parcels = call(
         step_second,
         (shape((columns, levels), f32), shape((8 * tiles, levels), f32)),
-        window, rates, tend, right, response, alive, hits, boundary, odd, even, parcels,
+        active_cols, window, rates, tend, right, response, hits, boundary, odd, even, parcels,
     )
     parcels, spread, refract, bend = after((parcels, spread, refract, bend))
     arrived = lax.all_to_all(

time: 116 us -> 117 us (level)
    pallas_call x10 -> x9, Pallas kernels: 9.21 us -> 9.75 us  [call(): pl.pallas_call(body, out_shape=outs if single else tuple(outs), in_specs=...]
where the time goes in v8:
time: 117 us
  blocking collectives  76.5 us (65%)
  starting transfers between devices  26.9 us (23%)
  Pallas kernels  9.75 us (8%)
  waiting for transfers between devices  2.2 us (2%)
    all_to_all x1, blocking collectives, shards(): lax.all_to_all(parcels.reshape(part, 8 * PARTS, levels), 'tile', split_ax...  22.6 us
    all_gather x1, blocking collectives, shards(): shared = lax.all_gather(edges, 'sec', axis=0, tiled=False)  21 us
    all_to_all x1, blocking collectives, shards(): lax.all_to_all(kept + got, AXES, split_axis=0, concat_axis=0, axis_index_...  17.5 us
    ppermute x2, starting transfers between devices, shards(): odd = lax.ppermute(odd, AXES, above_odd)  15.9 us
    all_gather x1, blocking collectives, shards(): surfaces = lax.all_gather(surface, 'sec', axis=0, tiled=False)  15.4 us
    pallas_call x9, Pallas kernels, call(): pl.pallas_call(body, out_shape=outs if single else tuple(outs), in_specs=...  9.75 us
    ppermute x1, starting transfers between devices, shards(): got = lax.ppermute(sent, 'sec', [(s, s ^ 1) for s in range(sections)])  5.2 us
    ppermute x2, starting transfers between devices, shards(): even = lax.ppermute(even, AXES, above_even)  3.84 us
  transfers between devices with their start and end apart: 6, of which 2 were waited for; matrix products, arithmetic and copies ran while one was open for 0% of the time, Pallas kernels for 4%

profile of v8, /device:TPU:1, one launch (start us, length us, event | category | flops | bytes accessed | tf_op | source)
XLA Modules:
  0.0 116.9 jit_solution(12764694816391496670)
XLA Ops:
  0.6 0.0 copy-start.4
  0.6 0.0 copy-start.5
  0.7 0.0 copy-start.9
  0.7 0.0 copy-start.10
  0.7 0.0 copy-start.13
  0.7 0.0 copy-start.1
  0.7 0.0 copy-start.2
  0.7 1.3 %shard_map.158 = f32[64,128]{1,0:T(8,128)S(1)} custom-call(f32[128,512]{1,0:T(8,128)} %bitcast.21, bf16[128,512]{1,0:T(8,128)(2,1)} %bitcast.24, bf16[128,512]{1,0:T(8,128)(2,1)} %bitcast.26, s32[4,512]{1,0:T(4,128)} %bitcast.28, f32[4,512]{1,0:T(4,128)} %bitcast.31), custom_call_target="tpu_custom_call" | custom-call | tf_op jit(solution)/shard_map/pallas_call | solution.py:24
  2.0 0.0 copy-start
  2.0 21.0 %all-gather = f32[256,128]{1,0:T(8,128)S(1)} all-gather(f32[64,128]{1,0:T(8,128)S(1)} %shard_map.158), channel_id=2, replica_groups=mesh['sec'=4,'tile'=128] {'sec'}, dimensions={0}, use_global_device_ids=true | all-gather | bytes 163840 | tf_op jit(solution)/shard_map/all_gather | solution.py:426
  23.0 0.0 copy-done.4
  23.0 0.0 copy-done.5
  23.0 0.0 copy-done.9
  23.0 0.0 copy-done.10
  23.0 0.0 copy-done.13
  23.0 0.0 copy-start.6
  23.0 0.2 shard_map.159
  23.2 10.7 %collective-permute-start = (f32[32,128]{1,0:T(8,128)S(1)}, f32[32,128]{1,0:T(8,128)S(1)}, u32[]{:S(2)}, u32[]{:S(2)}) collective-permute-start(f32[32,128]{1,0:T(8,128)S(1)} %get-tuple-element.33), channel_id=1, source_target_pairs={{1,2},{2,1},{3,4},{4,3},{5,6},{6,5},{7,8},{8,7},{9,10},{10,9},{11,... | collective-permute-start | bytes 49160 | tf_op jit(solution)/shard_map/ppermute | solution.py:437
  34.0 1.9 %collective-permute-start.1 = (f32[32,128]{1,0:T(8,128)S(1)}, f32[32,128]{1,0:T(8,128)S(1)}, u32[]{:S(2)}, u32[]{:S(2)}) collective-permute-start(f32[32,128]{1,0:T(8,128)S(1)} %get-tuple-element.34), channel_id=1, source_target_pairs={{0,1},{1,0},{2,3},{3,2},{4,5},{5,4},{6,7},{7,6},{8,9},{9,8},{10,11... | collective-permute-start | bytes 49160 | tf_op jit(solution)/shard_map/ppermute | solution.py:439
  35.9 1.9 %collective-permute-start.2 = (f32[32,64]{1,0:T(8,128)S(1)}, f32[32,64]{1,0:T(8,128)S(1)}, u32[]{:S(2)}, u32[]{:S(2)}) collective-permute-start(f32[32,64]{1,0:T(8,128)S(1)} %get-tuple-element.40.lists), channel_id=1, source_target_pairs={{0,64},{1,65},{2,66},{3,67},{4,68},{5,69},{6,70},{7,71},{8,72},{9,... | collective-permute-start | bytes 24584 | tf_op jit(solution)/shard_map/ppermute | solution.py:438
  37.8 0.0 collective-permute-done.odd
  37.8 0.6 collective-permute-done.1.even
  38.5 0.0 copy-start.12
  38.5 0.0 copy-start.14
  38.5 0.0 copy-done.1
  38.5 0.0 copy-done.2
  38.5 0.0 copy-done
  38.5 0.0 copy-done.6
  38.5 0.6 copy-done.12
  39.1 0.0 copy-done.14
  39.1 0.0 copy-start.7
  39.1 2.4 %shard_map.160 = (f32[528,128]{1,0:T(8,128)S(1)}, f32[528,128]{1,0:T(8,128)S(1)}, f32[528,128]{1,0:T(8,128)S(1)}, f32[4,128]{1,0:T(4,128)S(1)}, bf16[384,128]{1,0:T(8,128)(2,1)S(1)}, /*index=5*/f32[8,128]{1,0:T(8,128)S(1)}) custom-call(s32[4]{0:T(128)S(1)} %copy-done.12, f32[128,512]{1,0:T(8,128)S(1)} %bitcast.22, bf16[128,512]{1,0:T(8,128)(2,1)S(1)} %bitcast.25, ...), custom_call_target="tpu_custom_call" | custom-call | tf_op jit(solution)/shard_map/pallas_call | solution.py:24
  41.5 0.0 copy-start.3
  41.5 15.4 %all-gather.2.surfaces = f32[4,4,128]{2,1,0:T(4,128)S(1)} all-gather(f32[1,4,128]{2,1,0:T(4,128)S(1)} %bitcast.39), channel_id=3, replica_groups=mesh['sec'=4,'tile'=128] {'sec'}, dimensions={0}, use_global_device_ids=true | all-gather | bytes 10240 | tf_op jit(solution)/shard_map/all_gather | solution.py:452
  56.9 0.2 shard_map.161
  57.1 5.1 %collective-permute-start.3 = (f32[8,128]{1,0:T(8,128)S(1)}, f32[8,128]{1,0:T(8,128)S(1)}, u32[]{:S(2)}, u32[]{:S(2)}) collective-permute-start(f32[8,128]{1,0:T(8,128)S(1)} %get-tuple-element.45), channel_id=1, source_target_pairs={{1,2},{2,1},{3,4},{4,3},{5,6},{6,5},{7,8},{8,7},{9,10},{10,9},{11,... | collective-permute-start | bytes 12296 | tf_op jit(solution)/shard_map/ppermute | solution.py:458
  62.3 0.0 copy-start.11
  62.3 1.9 %collective-permute-start.4 = (f32[8,128]{1,0:T(8,128)S(1)}, f32[8,128]{1,0:T(8,128)S(1)}, u32[]{:S(2)}, u32[]{:S(2)}) collective-permute-start(f32[8,128]{1,0:T(8,128)S(1)} %get-tuple-element.46), channel_id=1, source_target_pairs={{0,1},{1,0},{2,3},{3,2},{4,5},{5,4},{6,7},{7,6},{8,9},{9,8},{10,11... | collective-permute-start | bytes 12296 | tf_op jit(solution)/shard_map/ppermute | solution.py:459
  64.2 0.0 collective-permute-done.2.mirrored
  64.2 0.0 copy-done.7
  64.2 0.0 copy-done.3
  64.3 0.0 copy-done.11
  64.3 1.1 shard_map.162
  65.4 1.5 %collective-permute-done.3.odd = f32[8,128]{1,0:T(8,128)S(1)} collective-permute-done((f32[8,128]{1,0:T(8,128)S(1)}, f32[8,128]{1,0:T(8,128)S(1)}, u32[]{:S(2)}, u32[]{:S(2)}) %collective-permute-start.3) | collective-permute-done | bytes 4128 | tf_op jit(solution)/shard_map/ppermute | solution.py:458
  66.9 0.0 collective-permute-done.4.even
  66.9 2.5 %shard_map.163 = (f32[512,128]{1,0:T(8,128)S(1)}, f32[1024,128]{1,0:T(8,128)S(1)}) custom-call(s32[4]{0:T(128)S(1)} %copy-done.12, f32[528,128]{1,0:T(8,128)S(1)} %get-tuple-element.35.window, f32[528,128]{1,0:T(8,128)S(1)} %get-tuple-element.36.rates, f32[528,128]{1,0:T(8,128)S(1)} %get-tuple-element.37.tend, bf16[384,128]{1,0:T(8,128)(2,1)S(1)} %get-tuple-element.38.right, ...), custom_call_target="tpu_custom_call" | custom-call | tf_op jit(solution)/shard_map/pallas_call | solution.py:24
  69.5 22.6 %all_to_all.10 = f32[64,16,128]{2,1,0:T(8,128)S(1)} all-to-all(f32[64,16,128]{2,1,0:T(8,128)S(1)} %bitcast.23), channel_id=1, replica_groups={{0,1,2,3,4,5,6,7,8,9,10,11,12,13,14,15,16,17,18,19,20,21,22,23,24,25,26..., dimensions={0} | all-to-all | bytes 1048576 | tf_op jit(solution)/shard_map/all_to_all | solution.py:478
  92.1 0.5 shard_map.164
  92.5 5.2 %collective-permute-start.5 = (f32[4,32,128]{2,1,0:T(8,128)S(1)}, f32[4,32,128]{2,1,0:T(8,128)S(1)}, u32[]{:S(2)}, u32[]{:S(2)}) collective-permute-start(f32[4,32,128]{2,1,0:T(8,128)S(1)} %get-tuple-element.55), channel_id=1, source_target_pairs={{0,128},{128,0},{256,384},{384,256},{1,129},{129,1},{257,385},{385... | collective-permute-start | bytes 196616 | tf_op jit(solution)/shard_map/ppermute | solution.py:490
  97.8 0.8 shard_map.165
  98.6 0.0 collective-permute-done.5
  98.7 0.0 copy-start.8
  98.7 17.5 %all_to_all.11.received = f32[4,32,128]{2,1,0:T(8,128)S(1)} all-to-all(f32[4,32,128]{2,1,0:T(8,128)S(1)} %add.3), channel_id=1, replica_groups={{0,64,256,320},{1,65,257,321},{2,66,258,322},{3,67,259,323},{4,68,260,3..., dimensions={0} | all-to-all | bytes 131072 | tf_op jit(solution)/shard_map/all_to_all | solution.py:494
  116.1 0.0 copy-done.8
  116.1 0.8 shard_map.166
  (1 shorter events, 0.0 us)
Async XLA Ops:
  0.6 22.3 %copy-start.4 = (s32[1,4,512]{2,1,0:T(4,128)S(1)}, s32[1,4,512]{2,1,0:T(4,128)}, u32[]{:S(2)}) copy-start(s32[1,4,512]{2,1,0:T(4,128)} %param.20) | copy-start | bytes 24580
  0.6 22.3 %copy-start.5 = (f32[1,4,512]{2,1,0:T(4,128)S(1)}, f32[1,4,512]{2,1,0:T(4,128)}, u32[]{:S(2)}) copy-start(f32[1,4,512]{2,1,0:T(4,128)} %param.21) | copy-start | bytes 24580
  0.7 22.3 %copy-start.9 = (s32[2,1,8,64]{3,2,1,0:T(8,128)S(1)}, s32[2,1,8,64]{3,2,1,0:T(8,128)}, u32[]{:S(2)}) copy-start(s32[2,1,8,64]{3,2,1,0:T(8,128)} %param.24) | copy-start | bytes 12292
  0.7 22.3 %copy-start.10 = (f32[2,1,8,64]{3,2,1,0:T(8,128)S(1)}, f32[2,1,8,64]{3,2,1,0:T(8,128)}, u32[]{:S(2)}) copy-start(f32[2,1,8,64]{3,2,1,0:T(8,128)} %param.25) | copy-start | bytes 12292
  0.7 22.3 %copy-start.13 = (s32[2,1,64]{2,1,0:T(1,128)S(1)}, s32[2,1,64]{2,1,0:T(1,128)}, u32[]{:S(2)}) copy-start(s32[2,1,64]{2,1,0:T(1,128)} %param.26) | copy-start | bytes 1540
  0.7 37.8 %copy-start.1 = (bf16[1,128,512]{2,1,0:T(8,128)(2,1)S(1)}, bf16[1,128,512]{2,1,0:T(8,128)(2,1)}, u32[]{:S(2)}) copy-start(bf16[1,128,512]{2,1,0:T(8,128)(2,1)} %param.16) | copy-start | bytes 393220
  0.7 37.8 %copy-start.2 = (bf16[1,128,512]{2,1,0:T(8,128)(2,1)S(1)}, bf16[1,128,512]{2,1,0:T(8,128)(2,1)}, u32[]{:S(2)}) copy-start(bf16[1,128,512]{2,1,0:T(8,128)(2,1)} %param.17) | copy-start | bytes 393220
  2.0 36.5 %copy-start = (f32[1,128,512]{2,1,0:T(8,128)S(1)}, f32[1,128,512]{2,1,0:T(8,128)}, u32[]{:S(2)}) copy-start(f32[1,128,512]{2,1,0:T(8,128)} %param.15) | copy-start | bytes 786436
  23.0 15.5 %copy-start.6 = (f32[1,128,128]{2,1,0:T(8,128)S(1)}, f32[1,128,128]{2,1,0:T(8,128)}, u32[]{:S(2)}) copy-start(f32[1,128,128]{2,1,0:T(8,128)} %param.18) | copy-start | bytes 196612
  23.2 14.6 %collective-permute-start = (f32[32,128]{1,0:T(8,128)S(1)}, f32[32,128]{1,0:T(8,128)S(1)}, u32[]{:S(2)}, u32[]{:S(2)}) collective-permute-start(f32[32,128]{1,0:T(8,128)S(1)} %get-tuple-element.33), channel_id=1, source_target_pairs={{1,2},{2,1},{3,4},{4,3},{5,6},{6,5},{7,8},{8,7},{9,10},{10,9},{11,... | collective-permute-start | bytes 49160 | tf_op jit(solution)/shard_map/ppermute | solution.py:437
  34.0 4.5 %collective-permute-start.1 = (f32[32,128]{1,0:T(8,128)S(1)}, f32[32,128]{1,0:T(8,128)S(1)}, u32[]{:S(2)}, u32[]{:S(2)}) collective-permute-start(f32[32,128]{1,0:T(8,128)S(1)} %get-tuple-element.34), channel_id=1, source_target_pairs={{0,1},{1,0},{2,3},{3,2},{4,5},{5,4},{6,7},{7,6},{8,9},{9,8},{10,11... | collective-permute-start | bytes 49160 | tf_op jit(solution)/shard_map/ppermute | solution.py:439
  35.9 28.3 %collective-permute-start.2 = (f32[32,64]{1,0:T(8,128)S(1)}, f32[32,64]{1,0:T(8,128)S(1)}, u32[]{:S(2)}, u32[]{:S(2)}) collective-permute-start(f32[32,64]{1,0:T(8,128)S(1)} %get-tuple-element.40.lists), channel_id=1, source_target_pairs={{0,64},{1,65},{2,66},{3,67},{4,68},{5,69},{6,70},{7,71},{8,72},{9,... | collective-permute-start | bytes 24584 | tf_op jit(solution)/shard_map/ppermute | solution.py:438
  38.5 0.7 copy-start.12
  38.5 0.7 copy-start.14
  39.1 25.1 %copy-start.7 = (f32[1,128,128]{2,1,0:T(8,128)S(1)}, f32[1,128,128]{2,1,0:T(8,128)}, u32[]{:S(2)}) copy-start(f32[1,128,128]{2,1,0:T(8,128)} %param.27) | copy-start | bytes 196612
  41.5 22.7 %copy-start.3 = (f32[128,256]{1,0:T(8,128)S(1)}, f32[128,256]{1,0:T(8,128)}, u32[]{:S(2)}) copy-start(f32[128,256]{1,0:T(8,128)} %abel.1) | copy-start | bytes 393220
  57.1 9.8 %collective-permute-start.3 = (f32[8,128]{1,0:T(8,128)S(1)}, f32[8,128]{1,0:T(8,128)S(1)}, u32[]{:S(2)}, u32[]{:S(2)}) collective-permute-start(f32[8,128]{1,0:T(8,128)S(1)} %get-tuple-element.45), channel_id=1, source_target_pairs={{1,2},{2,1},{3,4},{4,3},{5,6},{6,5},{7,8},{8,7},{9,10},{10,9},{11,... | collective-permute-start | bytes 12296 | tf_op jit(solution)/shard_map/ppermute | solution.py:458
  62.3 2.0 %copy-start.11 = (s32[2,1,1,128,4]{3,4,2,1,0:T(4,128)S(1)}, s32[2,1,1,128,4]{3,4,2,1,0:T(4,128)}, u32[]{:S(2)}) copy-start(s32[2,1,1,128,4]{3,4,2,1,0:T(4,128)} %param.23) | copy-start | bytes 12292
  62.3 4.6 %collective-permute-start.4 = (f32[8,128]{1,0:T(8,128)S(1)}, f32[8,128]{1,0:T(8,128)S(1)}, u32[]{:S(2)}, u32[]{:S(2)}) collective-permute-start(f32[8,128]{1,0:T(8,128)S(1)} %get-tuple-element.46), channel_id=1, source_target_pairs={{0,1},{1,0},{2,3},{3,2},{4,5},{5,4},{6,7},{7,6},{8,9},{9,8},{10,11... | collective-permute-start | bytes 12296 | tf_op jit(solution)/shard_map/ppermute | solution.py:459
  92.5 6.1 %collective-permute-start.5 = (f32[4,32,128]{2,1,0:T(8,128)S(1)}, f32[4,32,128]{2,1,0:T(8,128)S(1)}, u32[]{:S(2)}, u32[]{:S(2)}) collective-permute-start(f32[4,32,128]{2,1,0:T(8,128)S(1)} %get-tuple-element.55), channel_id=1, source_target_pairs={{0,128},{128,0},{256,384},{384,256},{1,129},{129,1},{257,385},{385... | collective-permute-start | bytes 196616 | tf_op jit(solution)/shard_map/ppermute | solution.py:490
  98.7 17.5 %copy-start.8 = (f32[2,16,256]{2,1,0:T(8,128)S(1)}, f32[2,16,256]{2,1,0:T(8,128)}, u32[]{:S(2)}) copy-start(f32[2,16,256]{2,1,0:T(8,128)} %observed.1) | copy-start | bytes 98308

commit v9 on v7

--- a/solution.py
+++ b/solution.py
@@ -103,10 +103,12 @@
     return jnp.where(lane < HALO, first, pltpu.roll(last, 2 * HALO, 1))
 
 
-def prepare(state, tendency, diffusion, index, weight, out, *scratch):
+def prepare(
+    state, tendency, diffusion, index, weight, slot, share, count, out, lists, *scratch
+):
     levels, columns = state.shape
     tail = columns - LANES
-    *ends, bottom, indices, weights, sems = scratch
+    *ends, bottom, indices, weights, slots, shares, counts, sems = scratch
     pairs = []
     for ref, head, back in zip((state, diffusion, tendency), ends[::2], ends[1::2]):
         pairs.append((ref.at[:, pl.ds(0, LANES)], head))
@@ -114,6 +116,9 @@
     pairs.append((state.at[pl.ds(levels - 8, 8), :], bottom))
     pairs.append((index, indices))
     pairs.append((weight, weights))
+    pairs.append((slot, slots))
+    pairs.append((share, shares))
+    pairs.append((count, counts))
     copies = [
         pltpu.make_async_copy(source, target, sems.at[i])
         for i, (source, target) in enumerate(pairs)
@@ -122,6 +127,12 @@
         copy.start()
     for copy in copies:
         copy.wait()
+    steps, ranks, occultations = slots.shape
+    for p in range(steps):
+        rank = lax.broadcasted_iota(jnp.int32, (ranks, occultations), 0)
+        lists[p * ranks : (p + 1) * ranks, :] = slots[p].astype(f32)
+        live = jnp.where(rank < counts[p : p + 1, :], shares[p], 0.0)
+        lists[(steps + p) * ranks : (steps + p + 1) * ranks, :] = live
     block = jnp.zeros((levels, LANES), f32)
     lane = lane_ids(block.shape)
     for i in range(3):
@@ -155,15 +166,7 @@
         out[:, cut] = partner - surface(j)
 
 
-def couple_first(
-    shared, index, weight, slots, weights, counts, boundary, odd, lists, even
-):
-    steps, ranks, occultations = slots.shape
-    for p in range(steps):
-        rank = lax.broadcasted_iota(jnp.int32, (ranks, occultations), 0)
-        lists[p * ranks : (p + 1) * ranks, :] = slots[p].astype(f32)
-        live = jnp.where(rank < counts[p : p + 1, :], weights[p], 0.0)
-        lists[(steps + p) * ranks : (steps + p + 1) * ranks, :] = live
+def couple_first(shared, index, weight, boundary, odd, even):
     section = lax.axis_index("sec")
     table = [shared[s, r : r + 1, :] for s in range(shared.shape[0]) for r in range(48, 52)]
     own_boundary(
@@ -410,12 +413,15 @@
     shape = jax.ShapeDtypeStruct
     after = lax.optimization_barrier
 
-    edges = call(
+    edges, lists = call(
         prepare,
-        shape((64, LANES), f32),
+        (shape((64, LANES), f32), shape((2 * STEPS * ranks, owned), f32)),
         *(
             pltpu.with_memory_space_constraint(x, pltpu.HBM)
-            for x in (state[0], tendency[0], diffusion[0], index, weight)
+            for x in (
+                state[0], tendency[0], diffusion[0], index, weight,
+                occ_slot[:, 0], occ_weight[:, 0], occ_count[:, 0],
+            )
         ),
         space=pltpu.HBM,
         scratch=[pltpu.VMEM((levels, LANES), f32)] * 2
@@ -424,22 +430,21 @@
             pltpu.VMEM((8, columns), f32),
             pltpu.VMEM(index.shape, jnp.int32),
             pltpu.VMEM(weight.shape, f32),
-            pltpu.SemaphoreType.DMA((9,)),
+            pltpu.VMEM((STEPS, ranks, owned), jnp.int32),
+            pltpu.VMEM((STEPS, ranks, owned), f32),
+            pltpu.VMEM((STEPS, owned), jnp.int32),
+            pltpu.SemaphoreType.DMA((12,)),
         ],
     )
+    mirrored = lax.ppermute(lists, "tile", [(t, (t + part) % tiles) for t in range(tiles)])
     shared = lax.all_gather(edges, "sec", axis=0, tiled=False)
-    boundary, odd, lists, even = call(
+    shared, mirrored = after((shared, mirrored))
+    boundary, odd, even = call(
         couple_first,
-        (
-            shape((1, columns), f32),
-            shape((32, LANES), f32),
-            shape((2 * STEPS * ranks, owned), f32),
-            shape((32, LANES), f32),
-        ),
-        shared, index, weight, occ_slot[:, 0], occ_weight[:, 0], occ_count[:, 0],
+        (shape((1, columns), f32), shape((32, LANES), f32), shape((32, LANES), f32)),
+        shared, index, weight,
     )
     odd = lax.ppermute(odd, AXES, above_odd)
-    mirrored = lax.ppermute(lists, "tile", [(t, (t + part) % tiles) for t in range(tiles)])
     even = lax.ppermute(even, AXES, above_even)
     mixing_row, _ = after((mixing[0], boundary))
     right, response, alive = call(

time: 116 us -> 120 us (1.034)
  starting transfers between devices: 26.9 us -> 36 us
  blocking collectives: 76.4 us -> 69.5 us
  waiting for transfers between devices: 1.59 us -> 3.46 us
    ppermute x1, starting transfers between devices: 1.92 us -> 9.78 us  [shards(): lax.ppermute(lists, 'tile', [(t, (t + part) % tiles) for t in range(tiles)])]
    all_gather x1, blocking collectives: 21 us -> 14.9 us  [shards(): shared = lax.all_gather(edges, 'sec', axis=0, tiled=False)]
    all_to_all x1, blocking collectives: 23.3 us -> 20.3 us  [shards(): lax.all_to_all(parcels.reshape(part, 8 * PARTS, levels), 'tile', split_ax...]
    all_to_all x1, blocking collectives: 16.9 us -> 18.9 us  [shards(): lax.all_to_all(kept + got, AXES, split_axis=0, concat_axis=0, axis_index_...]
    ppermute x2, waiting for transfers between devices: 0.1 us -> 1.9 us  [shards(): even = lax.ppermute(even, AXES, above_even)]
    ppermute x2, starting transfers between devices: 16 us -> 17.3 us  [shards(): odd = lax.ppermute(odd, AXES, above_odd)]
  transfers between devices with their start and end apart: 6 -> 6, of which waited for: 2 -> 2; matrix products, arithmetic and copies ran while one was open for 0% -> 0% of each run, Pallas kernels for 4% -> 2%
where the time goes in v9:
time: 120 us; the launch traced here: 119 us
  blocking collectives  69.5 us (58%)
  starting transfers between devices  36 us (30%)
  Pallas kernels  9.22 us (8%)
  waiting for transfers between devices  3.46 us (3%)
    all_to_all x1, blocking collectives, shards(): lax.all_to_all(parcels.reshape(part, 8 * PARTS, levels), 'tile', split_ax...  20.3 us
    all_to_all x1, blocking collectives, shards(): lax.all_to_all(kept + got, AXES, split_axis=0, concat_axis=0, axis_index_...  18.9 us
    ppermute x2, starting transfers between devices, shards(): odd = lax.ppermute(odd, AXES, above_odd)  17.3 us
    all_gather x1, blocking collectives, shards(): surfaces = lax.all_gather(surface, 'sec', axis=0, tiled=False)  15.4 us
    all_gather x1, blocking collectives, shards(): shared = lax.all_gather(edges, 'sec', axis=0, tiled=False)  14.9 us
    ppermute x1, starting transfers between devices, shards(): lax.ppermute(lists, 'tile', [(t, (t + part) % tiles) for t in range(tiles)])  9.78 us
    pallas_call x10, Pallas kernels, call(): pl.pallas_call(body, out_shape=outs if single else tuple(outs), in_specs=...  9.22 us
    ppermute x1, starting transfers between devices, shards(): got = lax.ppermute(sent, 'sec', [(s, s ^ 1) for s in range(sections)])  5.07 us
  transfers between devices with their start and end apart: 6, of which 2 were waited for; matrix products, arithmetic and copies ran while one was open for 0% of the time, Pallas kernels for 2%

profile of v9, /device:TPU:1, one launch (start us, length us, event | category | flops | bytes accessed | tf_op | source)
XLA Modules:
  0.0 119.2 jit_solution(11040938145379674969)
XLA Ops:
  0.6 0.0 copy-start.4
  0.6 0.0 copy-start.5
  0.7 0.0 copy-start.7
  0.7 0.0 copy-start.2
  0.7 1.3 %shard_map.158 = (f32[64,128]{1,0:T(8,128)S(1)}, f32[32,64]{1,0:T(8,128)S(1)}) custom-call(f32[128,512]{1,0:T(8,128)} %bitcast.21, bf16[128,512]{1,0:T(8,128)(2,1)} %bitcast.23, bf16[128,512]{1,0:T(8,128)(2,1)} %bitcast.25, s32[4,512]{1,0:T(4,128)} %bitcast.28, f32[4,512]{1,0:T(4,128)} %bitcast.31, s32[2,8,64]{2,1,0:T(8,128)} %bitcast.39, ...), custom_call_target="tpu_custom_call" | custom-call | tf_op jit(solution)/shard_map/pallas_call | solution.py:24
  2.0 0.0 copy-start
  2.0 9.8 %collective-permute-start = (f32[32,64]{1,0:T(8,128)S(1)}, f32[32,64]{1,0:T(8,128)S(1)}, u32[]{:S(2)}, u32[]{:S(2)}) collective-permute-start(f32[32,64]{1,0:T(8,128)S(1)} %get-tuple-element.38.lists), channel_id=1, source_target_pairs={{0,64},{1,65},{2,66},{3,67},{4,68},{5,69},{6,70},{7,71},{8,72},{9,... | collective-permute-start | bytes 24584 | tf_op jit(solution)/shard_map/ppermute | solution.py:439
  11.8 0.0 copy-start.10
  11.8 0.0 copy-start.11
  11.8 14.9 %all-gather = f32[256,128]{1,0:T(8,128)S(1)} all-gather(f32[64,128]{1,0:T(8,128)S(1)} %get-tuple-element.37), channel_id=2, replica_groups=mesh['sec'=4,'tile'=128] {'sec'}, dimensions={0}, use_global_device_ids=true | all-gather | bytes 163840 | tf_op jit(solution)/shard_map/all_gather | solution.py:440
  26.7 0.0 copy-start.1
  26.7 0.0 collective-permute-done.mirrored
  26.7 0.0 copy-done.4
  26.7 0.0 copy-done.5
  26.7 0.2 shard_map.159
  26.9 12.1 %collective-permute-start.1 = (f32[32,128]{1,0:T(8,128)S(1)}, f32[32,128]{1,0:T(8,128)S(1)}, u32[]{:S(2)}, u32[]{:S(2)}) collective-permute-start(f32[32,128]{1,0:T(8,128)S(1)} %get-tuple-element.45), channel_id=1, source_target_pairs={{1,2},{2,1},{3,4},{4,3},{5,6},{6,5},{7,8},{8,7},{9,10},{10,9},{11,... | collective-permute-start | bytes 49160 | tf_op jit(solution)/shard_map/ppermute | solution.py:447
  39.1 1.9 %collective-permute-start.2 = (f32[32,128]{1,0:T(8,128)S(1)}, f32[32,128]{1,0:T(8,128)S(1)}, u32[]{:S(2)}, u32[]{:S(2)}) collective-permute-start(f32[32,128]{1,0:T(8,128)S(1)} %get-tuple-element.46), channel_id=1, source_target_pairs={{0,1},{1,0},{2,3},{3,2},{4,5},{5,4},{6,7},{7,6},{8,9},{9,8},{10,11... | collective-permute-start | bytes 49160 | tf_op jit(solution)/shard_map/ppermute | solution.py:448
  41.0 0.0 copy-done.7
  41.0 0.0 copy-done.10
  41.0 0.0 copy-done.11
  41.0 0.6 shard_map.160
  41.7 0.0 collective-permute-done.1.odd
  41.7 1.9 %collective-permute-done.2.even = f32[32,128]{1,0:T(8,128)S(1)} collective-permute-done((f32[32,128]{1,0:T(8,128)S(1)}, f32[32,128]{1,0:T(8,128)S(1)}, u32[]{:S(2)}, u32[]{:S(2)}) %collective-permute-start.2) | collective-permute-done | bytes 16416 | tf_op jit(solution)/shard_map/ppermute | solution.py:448
  43.6 0.0 copy-done.2
  43.6 0.0 copy-done
  43.6 0.0 copy-done.1
  43.6 0.0 copy-start.6
  43.6 1.8 %shard_map.161 = (f32[528,128]{1,0:T(8,128)S(1)}, f32[528,128]{1,0:T(8,128)S(1)}, f32[528,128]{1,0:T(8,128)S(1)}, f32[4,128]{1,0:T(4,128)S(1)}) custom-call(f32[128,512]{1,0:T(8,128)S(1)} %bitcast.22, bf16[128,512]{1,0:T(8,128)(2,1)S(1)} %bitcast.24, bf16[128,512]{1,0:T(8,128)(2,1)S(1)} %bitcast.26, bf16[384,128]{1,0:T(8,128)(2,1)S(1)} %get-tuple-element.42.right, ...), custom_call_target="tpu_custom_call" | custom-call | tf_op jit(solution)/shard_map/pallas_call | solution.py:24
  45.4 0.0 copy-start.3
  45.4 15.4 %all-gather.2.surfaces = f32[4,4,128]{2,1,0:T(4,128)S(1)} all-gather(f32[1,4,128]{2,1,0:T(4,128)S(1)} %bitcast.37), channel_id=3, replica_groups=mesh['sec'=4,'tile'=128] {'sec'}, dimensions={0}, use_global_device_ids=true | all-gather | bytes 10240 | tf_op jit(solution)/shard_map/all_gather | solution.py:469
  60.8 0.2 shard_map.162
  61.0 5.2 %collective-permute-start.3 = (f32[8,128]{1,0:T(8,128)S(1)}, f32[8,128]{1,0:T(8,128)S(1)}, u32[]{:S(2)}, u32[]{:S(2)}) collective-permute-start(f32[8,128]{1,0:T(8,128)S(1)} %get-tuple-element.55), channel_id=1, source_target_pairs={{1,2},{2,1},{3,4},{4,3},{5,6},{6,5},{7,8},{8,7},{9,10},{10,9},{11,... | collective-permute-start | bytes 12296 | tf_op jit(solution)/shard_map/ppermute | solution.py:475
  66.1 0.0 copy-start.9
  66.2 1.9 %collective-permute-start.4 = (f32[8,128]{1,0:T(8,128)S(1)}, f32[8,128]{1,0:T(8,128)S(1)}, u32[]{:S(2)}, u32[]{:S(2)}) collective-permute-start(f32[8,128]{1,0:T(8,128)S(1)} %get-tuple-element.56), channel_id=1, source_target_pairs={{0,1},{1,0},{2,3},{3,2},{4,5},{5,4},{6,7},{7,6},{8,9},{9,8},{10,11... | collective-permute-start | bytes 12296 | tf_op jit(solution)/shard_map/ppermute | solution.py:476
  68.1 0.0 copy-done.6
  68.1 0.0 copy-done.3
  68.1 0.0 copy-done.9
  68.1 1.1 shard_map.163
  69.3 1.5 %collective-permute-done.3.odd = f32[8,128]{1,0:T(8,128)S(1)} collective-permute-done((f32[8,128]{1,0:T(8,128)S(1)}, f32[8,128]{1,0:T(8,128)S(1)}, u32[]{:S(2)}, u32[]{:S(2)}) %collective-permute-start.3) | collective-permute-done | bytes 4128 | tf_op jit(solution)/shard_map/ppermute | solution.py:475
  70.8 0.0 collective-permute-done.4.even
  70.8 1.9 %shard_map.164 = (f32[512,128]{1,0:T(8,128)S(1)}, f32[1024,128]{1,0:T(8,128)S(1)}) custom-call(f32[528,128]{1,0:T(8,128)S(1)} %get-tuple-element.47.window, f32[528,128]{1,0:T(8,128)S(1)} %get-tuple-element.48.rates, f32[528,128]{1,0:T(8,128)S(1)} %get-tuple-element.49.tend, bf16[384,128]{1,0:T(8,128)(2,1)S(1)} %get-tuple-element.42.right, ...), custom_call_target="tpu_custom_call" | custom-call | tf_op jit(solution)/shard_map/pallas_call | solution.py:24
  72.7 20.3 %all_to_all.10 = f32[64,16,128]{2,1,0:T(8,128)S(1)} all-to-all(f32[64,16,128]{2,1,0:T(8,128)S(1)} %bitcast.27), channel_id=1, replica_groups={{0,1,2,3,4,5,6,7,8,9,10,11,12,13,14,15,16,17,18,19,20,21,22,23,24,25,26..., dimensions={0} | all-to-all | bytes 1048576 | tf_op jit(solution)/shard_map/all_to_all | solution.py:495
  93.1 0.5 shard_map.165
  93.5 5.1 %collective-permute-start.5 = (f32[4,32,128]{2,1,0:T(8,128)S(1)}, f32[4,32,128]{2,1,0:T(8,128)S(1)}, u32[]{:S(2)}, u32[]{:S(2)}) collective-permute-start(f32[4,32,128]{2,1,0:T(8,128)S(1)} %get-tuple-element.65), channel_id=1, source_target_pairs={{0,128},{128,0},{256,384},{384,256},{1,129},{129,1},{257,385},{385... | collective-permute-start | bytes 196616 | tf_op jit(solution)/shard_map/ppermute | solution.py:507
  98.6 0.8 shard_map.166
  99.4 0.0 collective-permute-done.5
  99.5 0.0 copy-start.8
  99.5 18.9 %all_to_all.11.received = f32[4,32,128]{2,1,0:T(8,128)S(1)} all-to-all(f32[4,32,128]{2,1,0:T(8,128)S(1)} %add.3), channel_id=1, replica_groups={{0,64,256,320},{1,65,257,321},{2,66,258,322},{3,67,259,323},{4,68,260,3..., dimensions={0} | all-to-all | bytes 131072 | tf_op jit(solution)/shard_map/all_to_all | solution.py:511
  118.4 0.0 copy-done.8
  118.4 0.8 shard_map.167
  (1 shorter events, 0.0 us)
Async XLA Ops:
  0.6 26.1 %copy-start.4 = (s32[1,4,512]{2,1,0:T(4,128)S(1)}, s32[1,4,512]{2,1,0:T(4,128)}, u32[]{:S(2)}) copy-start(s32[1,4,512]{2,1,0:T(4,128)} %param.20) | copy-start | bytes 24580
  0.6 26.1 %copy-start.5 = (f32[1,4,512]{2,1,0:T(4,128)S(1)}, f32[1,4,512]{2,1,0:T(4,128)}, u32[]{:S(2)}) copy-start(f32[1,4,512]{2,1,0:T(4,128)} %param.21) | copy-start | bytes 24580
  0.7 40.4 %copy-start.7 = (f32[1,128,128]{2,1,0:T(8,128)S(1)}, f32[1,128,128]{2,1,0:T(8,128)}, u32[]{:S(2)}) copy-start(f32[1,128,128]{2,1,0:T(8,128)} %param.18) | copy-start | bytes 196612
  0.7 42.9 %copy-start.2 = (bf16[1,128,512]{2,1,0:T(8,128)(2,1)S(1)}, bf16[1,128,512]{2,1,0:T(8,128)(2,1)}, u32[]{:S(2)}) copy-start(bf16[1,128,512]{2,1,0:T(8,128)(2,1)} %param.17) | copy-start | bytes 393220
  2.0 41.6 %copy-start = (f32[1,128,512]{2,1,0:T(8,128)S(1)}, f32[1,128,512]{2,1,0:T(8,128)}, u32[]{:S(2)}) copy-start(f32[1,128,512]{2,1,0:T(8,128)} %param.15) | copy-start | bytes 786436
  2.0 24.7 %collective-permute-start = (f32[32,64]{1,0:T(8,128)S(1)}, f32[32,64]{1,0:T(8,128)S(1)}, u32[]{:S(2)}, u32[]{:S(2)}) collective-permute-start(f32[32,64]{1,0:T(8,128)S(1)} %get-tuple-element.38.lists), channel_id=1, source_target_pairs={{0,64},{1,65},{2,66},{3,67},{4,68},{5,69},{6,70},{7,71},{8,72},{9,... | collective-permute-start | bytes 24584 | tf_op jit(solution)/shard_map/ppermute | solution.py:439
  11.8 29.3 %copy-start.10 = (s32[4]{0:T(128)S(1)}, s32[4]{0:T(128)}, u32[]{:S(2)}) copy-start(s32[4]{0:T(128)} %active.1) | copy-start | bytes 52
  11.8 29.3 %copy-start.11 = (f32[1,128]{1,0:T(1,128)S(1)}, f32[1,128]{1,0:T(1,128)}, u32[]{:S(2)}) copy-start(f32[1,128]{1,0:T(1,128)} %coupling.1) | copy-start | bytes 1540
  26.7 16.9 %copy-start.1 = (bf16[1,128,512]{2,1,0:T(8,128)(2,1)S(1)}, bf16[1,128,512]{2,1,0:T(8,128)(2,1)}, u32[]{:S(2)}) copy-start(bf16[1,128,512]{2,1,0:T(8,128)(2,1)} %param.16) | copy-start | bytes 393220
  26.9 14.8 %collective-permute-start.1 = (f32[32,128]{1,0:T(8,128)S(1)}, f32[32,128]{1,0:T(8,128)S(1)}, u32[]{:S(2)}, u32[]{:S(2)}) collective-permute-start(f32[32,128]{1,0:T(8,128)S(1)} %get-tuple-element.45), channel_id=1, source_target_pairs={{1,2},{2,1},{3,4},{4,3},{5,6},{6,5},{7,8},{8,7},{9,10},{10,9},{11,... | collective-permute-start | bytes 49160 | tf_op jit(solution)/shard_map/ppermute | solution.py:447
  39.1 4.5 %collective-permute-start.2 = (f32[32,128]{1,0:T(8,128)S(1)}, f32[32,128]{1,0:T(8,128)S(1)}, u32[]{:S(2)}, u32[]{:S(2)}) collective-permute-start(f32[32,128]{1,0:T(8,128)S(1)} %get-tuple-element.46), channel_id=1, source_target_pairs={{0,1},{1,0},{2,3},{3,2},{4,5},{5,4},{6,7},{7,6},{8,9},{9,8},{10,11... | collective-permute-start | bytes 49160 | tf_op jit(solution)/shard_map/ppermute | solution.py:448
  43.6 24.5 %copy-start.6 = (f32[1,128,128]{2,1,0:T(8,128)S(1)}, f32[1,128,128]{2,1,0:T(8,128)}, u32[]{:S(2)}) copy-start(f32[1,128,128]{2,1,0:T(8,128)} %param.27) | copy-start | bytes 196612
  45.4 22.7 %copy-start.3 = (f32[128,256]{1,0:T(8,128)S(1)}, f32[128,256]{1,0:T(8,128)}, u32[]{:S(2)}) copy-start(f32[128,256]{1,0:T(8,128)} %abel.1) | copy-start | bytes 393220
  61.0 9.8 %collective-permute-start.3 = (f32[8,128]{1,0:T(8,128)S(1)}, f32[8,128]{1,0:T(8,128)S(1)}, u32[]{:S(2)}, u32[]{:S(2)}) collective-permute-start(f32[8,128]{1,0:T(8,128)S(1)} %get-tuple-element.55), channel_id=1, source_target_pairs={{1,2},{2,1},{3,4},{4,3},{5,6},{6,5},{7,8},{8,7},{9,10},{10,9},{11,... | collective-permute-start | bytes 12296 | tf_op jit(solution)/shard_map/ppermute | solution.py:475
  66.1 2.0 %copy-start.9 = (s32[2,1,1,128,4]{3,4,2,1,0:T(4,128)S(1)}, s32[2,1,1,128,4]{3,4,2,1,0:T(4,128)}, u32[]{:S(2)}) copy-start(s32[2,1,1,128,4]{3,4,2,1,0:T(4,128)} %param.23) | copy-start | bytes 12292
  66.2 4.6 %collective-permute-start.4 = (f32[8,128]{1,0:T(8,128)S(1)}, f32[8,128]{1,0:T(8,128)S(1)}, u32[]{:S(2)}, u32[]{:S(2)}) collective-permute-start(f32[8,128]{1,0:T(8,128)S(1)} %get-tuple-element.56), channel_id=1, source_target_pairs={{0,1},{1,0},{2,3},{3,2},{4,5},{5,4},{6,7},{7,6},{8,9},{9,8},{10,11... | collective-permute-start | bytes 12296 | tf_op jit(solution)/shard_map/ppermute | solution.py:476
  93.5 6.0 %collective-permute-start.5 = (f32[4,32,128]{2,1,0:T(8,128)S(1)}, f32[4,32,128]{2,1,0:T(8,128)S(1)}, u32[]{:S(2)}, u32[]{:S(2)}) collective-permute-start(f32[4,32,128]{2,1,0:T(8,128)S(1)} %get-tuple-element.65), channel_id=1, source_target_pairs={{0,128},{128,0},{256,384},{384,256},{1,129},{129,1},{257,385},{385... | collective-permute-start | bytes 196616 | tf_op jit(solution)/shard_map/ppermute | solution.py:507
  99.5 18.9 %copy-start.8 = (f32[2,16,256]{2,1,0:T(8,128)S(1)}, f32[2,16,256]{2,1,0:T(8,128)}, u32[]{:S(2)}) copy-start(f32[2,16,256]{2,1,0:T(8,128)} %observed.1) | copy-start | bytes 98308

commit v10 on v7

--- a/solution.py
+++ b/solution.py
@@ -156,8 +156,10 @@
 
 
 def couple_first(
-    shared, index, weight, slots, weights, counts, boundary, odd, lists, even
+    active, shared, index, weight, slots, weights, counts, mixing, coupling,
+    boundary, odd, lists, even, right, response, alive,
 ):
+    ready_first(active, mixing, coupling, right, response, alive)
     steps, ranks, occultations = slots.shape
     for p in range(steps):
         rank = lax.broadcasted_iota(jnp.int32, (ranks, occultations), 0)
@@ -428,29 +430,23 @@
         ],
     )
     shared = lax.all_gather(edges, "sec", axis=0, tiled=False)
-    boundary, odd, lists, even = call(
+    boundary, odd, lists, even, right, response, alive = call(
         couple_first,
         (
             shape((1, columns), f32),
             shape((32, LANES), f32),
             shape((2 * STEPS * ranks, owned), f32),
             shape((32, LANES), f32),
-        ),
-        shared, index, weight, occ_slot[:, 0], occ_weight[:, 0], occ_count[:, 0],
-    )
-    odd = lax.ppermute(odd, AXES, above_odd)
-    mirrored = lax.ppermute(lists, "tile", [(t, (t + part) % tiles) for t in range(tiles)])
-    even = lax.ppermute(even, AXES, above_even)
-    mixing_row, _ = after((mixing[0], boundary))
-    right, response, alive = call(
-        ready_first,
-        (
             shape((3 * levels, levels), bf16),
             shape((8, levels), f32),
             shape((width, levels), f32),
         ),
-        active_cols, mixing_row, coupling,
-    )
+        active_cols, shared, index, weight, occ_slot[:, 0], occ_weight[:, 0], occ_count[:, 0],
+        mixing[0], coupling,
+    )
+    odd = lax.ppermute(odd, AXES, above_odd)
+    mirrored = lax.ppermute(lists, "tile", [(t, (t + part) % tiles) for t in range(tiles)])
+    even = lax.ppermute(even, AXES, above_even)
     window, rates, tend, surface = call(
         step_first,
         (

time: 116 us -> 116 us (level)
    pallas_call x10 -> x9, Pallas kernels: 9.21 us -> 9.18 us  [call(): pl.pallas_call(body, out_shape=outs if single else tuple(outs), in_specs=...]
  transfers between devices with their start and end apart: 6 -> 6, of which waited for: 2 -> 2; matrix products, arithmetic and copies ran while one was open for 0% -> 0% of each run, Pallas kernels for 4% -> 3%
where the time goes in v10:
time: 116 us
  blocking collectives  76.5 us (66%)
  starting transfers between devices  26.9 us (23%)
  Pallas kernels  9.18 us (8%)
  waiting for transfers between devices  2.2 us (2%)
    all_to_all x1, blocking collectives, shards(): lax.all_to_all(parcels.reshape(part, 8 * PARTS, levels), 'tile', split_ax...  22.6 us
    all_gather x1, blocking collectives, shards(): shared = lax.all_gather(edges, 'sec', axis=0, tiled=False)  21 us
    all_to_all x1, blocking collectives, shards(): lax.all_to_all(kept + got, AXES, split_axis=0, concat_axis=0, axis_index_...  17.5 us
    ppermute x2, starting transfers between devices, shards(): odd = lax.ppermute(odd, AXES, above_odd)  15.9 us
    all_gather x1, blocking collectives, shards(): surfaces = lax.all_gather(surface, 'sec', axis=0, tiled=False)  15.4 us
    pallas_call x9, Pallas kernels, call(): pl.pallas_call(body, out_shape=outs if single else tuple(outs), in_specs=...  9.18 us
    ppermute x1, starting transfers between devices, shards(): got = lax.ppermute(sent, 'sec', [(s, s ^ 1) for s in range(sections)])  5.21 us
    ppermute x2, starting transfers between devices, shards(): even = lax.ppermute(even, AXES, above_even)  3.84 us
  transfers between devices with their start and end apart: 6, of which 2 were waited for; matrix products, arithmetic and copies ran while one was open for 0% of the time, Pallas kernels for 3%

profile of v10, /device:TPU:1, one launch (start us, length us, event | category | flops | bytes accessed | tf_op | source)
XLA Modules:
  0.0 115.7 jit_solution(18369565063515761314)
XLA Ops:
  0.6 0.0 copy-start.4
  0.6 0.0 copy-start.5
  0.7 0.0 copy-start.6
  0.7 0.0 copy-start.9
  0.7 0.0 copy-start.10
  0.7 0.0 copy-start.12
  0.7 0.0 copy-start.13
  0.7 0.0 copy-start.14
  0.7 0.0 copy-start.2
  0.7 1.3 %shard_map.158 = f32[64,128]{1,0:T(8,128)S(1)} custom-call(f32[128,512]{1,0:T(8,128)} %bitcast.21, bf16[128,512]{1,0:T(8,128)(2,1)} %bitcast.24, bf16[128,512]{1,0:T(8,128)(2,1)} %bitcast.26, s32[4,512]{1,0:T(4,128)} %bitcast.28, f32[4,512]{1,0:T(4,128)} %bitcast.31), custom_call_target="tpu_custom_call" | custom-call | tf_op jit(solution)/shard_map/pallas_call | solution.py:24
  2.0 0.0 copy-start
  2.0 21.0 %all-gather = f32[256,128]{1,0:T(8,128)S(1)} all-gather(f32[64,128]{1,0:T(8,128)S(1)} %shard_map.158), channel_id=2, replica_groups=mesh['sec'=4,'tile'=128] {'sec'}, dimensions={0}, use_global_device_ids=true | all-gather | bytes 163840 | tf_op jit(solution)/shard_map/all_gather | solution.py:432
  23.0 0.0 copy-start.1
  23.0 0.0 copy-done.4
  23.0 0.0 copy-done.5
  23.0 0.0 copy-done.6
  23.0 0.0 copy-done.9
  23.0 0.0 copy-done.10
  23.0 0.0 copy-done.12
  23.0 0.0 copy-done.13
  23.1 0.0 copy-done.14
  23.1 0.8 shard_map.159
  23.9 10.7 %collective-permute-start = (f32[32,128]{1,0:T(8,128)S(1)}, f32[32,128]{1,0:T(8,128)S(1)}, u32[]{:S(2)}, u32[]{:S(2)}) collective-permute-start(f32[32,128]{1,0:T(8,128)S(1)} %get-tuple-element.37), channel_id=1, source_target_pairs={{1,2},{2,1},{3,4},{4,3},{5,6},{6,5},{7,8},{8,7},{9,10},{10,9},{11,... | collective-permute-start | bytes 49160 | tf_op jit(solution)/shard_map/ppermute | solution.py:447
  34.6 1.9 %collective-permute-start.1 = (f32[32,128]{1,0:T(8,128)S(1)}, f32[32,128]{1,0:T(8,128)S(1)}, u32[]{:S(2)}, u32[]{:S(2)}) collective-permute-start(f32[32,128]{1,0:T(8,128)S(1)} %get-tuple-element.38), channel_id=1, source_target_pairs={{0,1},{1,0},{2,3},{3,2},{4,5},{5,4},{6,7},{7,6},{8,9},{9,8},{10,11... | collective-permute-start | bytes 49160 | tf_op jit(solution)/shard_map/ppermute | solution.py:449
  36.6 1.9 %collective-permute-start.2 = (f32[32,64]{1,0:T(8,128)S(1)}, f32[32,64]{1,0:T(8,128)S(1)}, u32[]{:S(2)}, u32[]{:S(2)}) collective-permute-start(f32[32,64]{1,0:T(8,128)S(1)} %get-tuple-element.42.lists), channel_id=1, source_target_pairs={{0,64},{1,65},{2,66},{3,67},{4,68},{5,69},{6,70},{7,71},{8,72},{9,... | collective-permute-start | bytes 24584 | tf_op jit(solution)/shard_map/ppermute | solution.py:448
  38.5 0.0 collective-permute-done.odd
  38.5 0.6 collective-permute-done.1.even
  39.1 0.0 copy-done.2
  39.1 0.0 copy-done
  39.1 0.0 copy-done.1
  39.1 0.0 copy-start.7
  39.1 1.8 %shard_map.160 = (f32[528,128]{1,0:T(8,128)S(1)}, f32[528,128]{1,0:T(8,128)S(1)}, f32[528,128]{1,0:T(8,128)S(1)}, f32[4,128]{1,0:T(4,128)S(1)}) custom-call(f32[128,512]{1,0:T(8,128)S(1)} %bitcast.22, bf16[128,512]{1,0:T(8,128)(2,1)S(1)} %bitcast.25, bf16[128,512]{1,0:T(8,128)(2,1)S(1)} %bitcast.27, bf16[384,128]{1,0:T(8,128)(2,1)S(1)} %get-tuple-element.33.right, ...), custom_call_target="tpu_custom_call" | custom-call | tf_op jit(solution)/shard_map/pallas_call | solution.py:24
  40.9 0.0 copy-start.3
  40.9 15.4 %all-gather.2.surfaces = f32[4,4,128]{2,1,0:T(4,128)S(1)} all-gather(f32[1,4,128]{2,1,0:T(4,128)S(1)} %bitcast.39), channel_id=3, replica_groups=mesh['sec'=4,'tile'=128] {'sec'}, dimensions={0}, use_global_device_ids=true | all-gather | bytes 10240 | tf_op jit(solution)/shard_map/all_gather | solution.py:460
  56.3 0.2 shard_map.161
  56.5 5.2 %collective-permute-start.3 = (f32[8,128]{1,0:T(8,128)S(1)}, f32[8,128]{1,0:T(8,128)S(1)}, u32[]{:S(2)}, u32[]{:S(2)}) collective-permute-start(f32[8,128]{1,0:T(8,128)S(1)} %get-tuple-element.47), channel_id=1, source_target_pairs={{1,2},{2,1},{3,4},{4,3},{5,6},{6,5},{7,8},{8,7},{9,10},{10,9},{11,... | collective-permute-start | bytes 12296 | tf_op jit(solution)/shard_map/ppermute | solution.py:466
  61.7 0.0 copy-start.11
  61.7 1.9 %collective-permute-start.4 = (f32[8,128]{1,0:T(8,128)S(1)}, f32[8,128]{1,0:T(8,128)S(1)}, u32[]{:S(2)}, u32[]{:S(2)}) collective-permute-start(f32[8,128]{1,0:T(8,128)S(1)} %get-tuple-element.48), channel_id=1, source_target_pairs={{0,1},{1,0},{2,3},{3,2},{4,5},{5,4},{6,7},{7,6},{8,9},{9,8},{10,11... | collective-permute-start | bytes 12296 | tf_op jit(solution)/shard_map/ppermute | solution.py:467
  63.6 0.0 collective-permute-done.2.mirrored
  63.6 0.0 copy-done.7
  63.6 0.0 copy-done.3
  63.7 0.0 copy-done.11
  63.7 1.1 shard_map.162
  64.8 1.5 %collective-permute-done.3.odd = f32[8,128]{1,0:T(8,128)S(1)} collective-permute-done((f32[8,128]{1,0:T(8,128)S(1)}, f32[8,128]{1,0:T(8,128)S(1)}, u32[]{:S(2)}, u32[]{:S(2)}) %collective-permute-start.3) | collective-permute-done | bytes 4128 | tf_op jit(solution)/shard_map/ppermute | solution.py:466
  66.3 0.0 collective-permute-done.4.even
  66.3 1.9 %shard_map.163 = (f32[512,128]{1,0:T(8,128)S(1)}, f32[1024,128]{1,0:T(8,128)S(1)}) custom-call(f32[528,128]{1,0:T(8,128)S(1)} %get-tuple-element.39.window, f32[528,128]{1,0:T(8,128)S(1)} %get-tuple-element.40.rates, f32[528,128]{1,0:T(8,128)S(1)} %get-tuple-element.41.tend, bf16[384,128]{1,0:T(8,128)(2,1)S(1)} %get-tuple-element.33.right, ...), custom_call_target="tpu_custom_call" | custom-call | tf_op jit(solution)/shard_map/pallas_call | solution.py:24
  68.3 22.6 %all_to_all.10 = f32[64,16,128]{2,1,0:T(8,128)S(1)} all-to-all(f32[64,16,128]{2,1,0:T(8,128)S(1)} %bitcast.23), channel_id=1, replica_groups={{0,1,2,3,4,5,6,7,8,9,10,11,12,13,14,15,16,17,18,19,20,21,22,23,24,25,26..., dimensions={0} | all-to-all | bytes 1048576 | tf_op jit(solution)/shard_map/all_to_all | solution.py:486
  90.9 0.5 shard_map.164
  91.4 5.2 %collective-permute-start.5 = (f32[4,32,128]{2,1,0:T(8,128)S(1)}, f32[4,32,128]{2,1,0:T(8,128)S(1)}, u32[]{:S(2)}, u32[]{:S(2)}) collective-permute-start(f32[4,32,128]{2,1,0:T(8,128)S(1)} %get-tuple-element.57), channel_id=1, source_target_pairs={{0,128},{128,0},{256,384},{384,256},{1,129},{129,1},{257,385},{385... | collective-permute-start | bytes 196616 | tf_op jit(solution)/shard_map/ppermute | solution.py:498
  96.6 0.8 shard_map.165
  97.4 0.0 collective-permute-done.5
  97.5 0.0 copy-start.8
  97.5 17.5 %all_to_all.11.received = f32[4,32,128]{2,1,0:T(8,128)S(1)} all-to-all(f32[4,32,128]{2,1,0:T(8,128)S(1)} %add.3), channel_id=1, replica_groups={{0,64,256,320},{1,65,257,321},{2,66,258,322},{3,67,259,323},{4,68,260,3..., dimensions={0} | all-to-all | bytes 131072 | tf_op jit(solution)/shard_map/all_to_all | solution.py:502
  115.0 0.0 copy-done.8
  115.0 0.8 shard_map.166
  (1 shorter events, 0.0 us)
Async XLA Ops:
  0.6 22.4 %copy-start.4 = (s32[1,4,512]{2,1,0:T(4,128)S(1)}, s32[1,4,512]{2,1,0:T(4,128)}, u32[]{:S(2)}) copy-start(s32[1,4,512]{2,1,0:T(4,128)} %param.20) | copy-start | bytes 24580
  0.6 22.4 %copy-start.5 = (f32[1,4,512]{2,1,0:T(4,128)S(1)}, f32[1,4,512]{2,1,0:T(4,128)}, u32[]{:S(2)}) copy-start(f32[1,4,512]{2,1,0:T(4,128)} %param.21) | copy-start | bytes 24580
  0.7 22.4 %copy-start.6 = (f32[1,128,128]{2,1,0:T(8,128)S(1)}, f32[1,128,128]{2,1,0:T(8,128)}, u32[]{:S(2)}) copy-start(f32[1,128,128]{2,1,0:T(8,128)} %param.18) | copy-start | bytes 196612
  0.7 22.4 %copy-start.9 = (s32[2,1,8,64]{3,2,1,0:T(8,128)S(1)}, s32[2,1,8,64]{3,2,1,0:T(8,128)}, u32[]{:S(2)}) copy-start(s32[2,1,8,64]{3,2,1,0:T(8,128)} %param.24) | copy-start | bytes 12292
  0.7 22.4 %copy-start.10 = (f32[2,1,8,64]{3,2,1,0:T(8,128)S(1)}, f32[2,1,8,64]{3,2,1,0:T(8,128)}, u32[]{:S(2)}) copy-start(f32[2,1,8,64]{3,2,1,0:T(8,128)} %param.25) | copy-start | bytes 12292
  0.7 22.4 %copy-start.12 = (s32[2,1,64]{2,1,0:T(1,128)S(1)}, s32[2,1,64]{2,1,0:T(1,128)}, u32[]{:S(2)}) copy-start(s32[2,1,64]{2,1,0:T(1,128)} %param.26) | copy-start | bytes 1540
  0.7 22.4 %copy-start.13 = (s32[4]{0:T(128)S(1)}, s32[4]{0:T(128)}, u32[]{:S(2)}) copy-start(s32[4]{0:T(128)} %active.1) | copy-start | bytes 52
  0.7 22.4 %copy-start.14 = (f32[1,128]{1,0:T(1,128)S(1)}, f32[1,128]{1,0:T(1,128)}, u32[]{:S(2)}) copy-start(f32[1,128]{1,0:T(1,128)} %coupling.1) | copy-start | bytes 1540
  0.7 38.4 %copy-start.2 = (bf16[1,128,512]{2,1,0:T(8,128)(2,1)S(1)}, bf16[1,128,512]{2,1,0:T(8,128)(2,1)}, u32[]{:S(2)}) copy-start(bf16[1,128,512]{2,1,0:T(8,128)(2,1)} %param.17) | copy-start | bytes 393220
  2.0 37.1 %copy-start = (f32[1,128,512]{2,1,0:T(8,128)S(1)}, f32[1,128,512]{2,1,0:T(8,128)}, u32[]{:S(2)}) copy-start(f32[1,128,512]{2,1,0:T(8,128)} %param.15) | copy-start | bytes 786436
  23.0 16.1 %copy-start.1 = (bf16[1,128,512]{2,1,0:T(8,128)(2,1)S(1)}, bf16[1,128,512]{2,1,0:T(8,128)(2,1)}, u32[]{:S(2)}) copy-start(bf16[1,128,512]{2,1,0:T(8,128)(2,1)} %param.16) | copy-start | bytes 393220
  23.9 14.6 %collective-permute-start = (f32[32,128]{1,0:T(8,128)S(1)}, f32[32,128]{1,0:T(8,128)S(1)}, u32[]{:S(2)}, u32[]{:S(2)}) collective-permute-start(f32[32,128]{1,0:T(8,128)S(1)} %get-tuple-element.37), channel_id=1, source_target_pairs={{1,2},{2,1},{3,4},{4,3},{5,6},{6,5},{7,8},{8,7},{9,10},{10,9},{11,... | collective-permute-start | bytes 49160 | tf_op jit(solution)/shard_map/ppermute | solution.py:447
  34.6 4.5 %collective-permute-start.1 = (f32[32,128]{1,0:T(8,128)S(1)}, f32[32,128]{1,0:T(8,128)S(1)}, u32[]{:S(2)}, u32[]{:S(2)}) collective-permute-start(f32[32,128]{1,0:T(8,128)S(1)} %get-tuple-element.38), channel_id=1, source_target_pairs={{0,1},{1,0},{2,3},{3,2},{4,5},{5,4},{6,7},{7,6},{8,9},{9,8},{10,11... | collective-permute-start | bytes 49160 | tf_op jit(solution)/shard_map/ppermute | solution.py:449
  36.6 27.1 %collective-permute-start.2 = (f32[32,64]{1,0:T(8,128)S(1)}, f32[32,64]{1,0:T(8,128)S(1)}, u32[]{:S(2)}, u32[]{:S(2)}) collective-permute-start(f32[32,64]{1,0:T(8,128)S(1)} %get-tuple-element.42.lists), channel_id=1, source_target_pairs={{0,64},{1,65},{2,66},{3,67},{4,68},{5,69},{6,70},{7,71},{8,72},{9,... | collective-permute-start | bytes 24584 | tf_op jit(solution)/shard_map/ppermute | solution.py:448
  39.1 24.5 %copy-start.7 = (f32[1,128,128]{2,1,0:T(8,128)S(1)}, f32[1,128,128]{2,1,0:T(8,128)}, u32[]{:S(2)}) copy-start(f32[1,128,128]{2,1,0:T(8,128)} %param.27) | copy-start | bytes 196612
  40.9 22.7 %copy-start.3 = (f32[128,256]{1,0:T(8,128)S(1)}, f32[128,256]{1,0:T(8,128)}, u32[]{:S(2)}) copy-start(f32[128,256]{1,0:T(8,128)} %abel.1) | copy-start | bytes 393220
  56.5 9.8 %collective-permute-start.3 = (f32[8,128]{1,0:T(8,128)S(1)}, f32[8,128]{1,0:T(8,128)S(1)}, u32[]{:S(2)}, u32[]{:S(2)}) collective-permute-start(f32[8,128]{1,0:T(8,128)S(1)} %get-tuple-element.47), channel_id=1, source_target_pairs={{1,2},{2,1},{3,4},{4,3},{5,6},{6,5},{7,8},{8,7},{9,10},{10,9},{11,... | collective-permute-start | bytes 12296 | tf_op jit(solution)/shard_map/ppermute | solution.py:466
  61.7 2.0 %copy-start.11 = (s32[2,1,1,128,4]{3,4,2,1,0:T(4,128)S(1)}, s32[2,1,1,128,4]{3,4,2,1,0:T(4,128)}, u32[]{:S(2)}) copy-start(s32[2,1,1,128,4]{3,4,2,1,0:T(4,128)} %param.23) | copy-start | bytes 12292
  61.7 4.6 %collective-permute-start.4 = (f32[8,128]{1,0:T(8,128)S(1)}, f32[8,128]{1,0:T(8,128)S(1)}, u32[]{:S(2)}, u32[]{:S(2)}) collective-permute-start(f32[8,128]{1,0:T(8,128)S(1)} %get-tuple-element.48), channel_id=1, source_target_pairs={{0,1},{1,0},{2,3},{3,2},{4,5},{5,4},{6,7},{7,6},{8,9},{9,8},{10,11... | collective-permute-start | bytes 12296 | tf_op jit(solution)/shard_map/ppermute | solution.py:467
  91.4 6.1 %collective-permute-start.5 = (f32[4,32,128]{2,1,0:T(8,128)S(1)}, f32[4,32,128]{2,1,0:T(8,128)S(1)}, u32[]{:S(2)}, u32[]{:S(2)}) collective-permute-start(f32[4,32,128]{2,1,0:T(8,128)S(1)} %get-tuple-element.57), channel_id=1, source_target_pairs={{0,128},{128,0},{256,384},{384,256},{1,129},{129,1},{257,385},{385... | collective-permute-start | bytes 196616 | tf_op jit(solution)/shard_map/ppermute | solution.py:498
  97.5 17.5 %copy-start.8 = (f32[2,16,256]{2,1,0:T(8,128)S(1)}, f32[2,16,256]{2,1,0:T(8,128)}, u32[]{:S(2)}) copy-start(f32[2,16,256]{2,1,0:T(8,128)} %observed.1) | copy-start | bytes 98308
